TPU v7x, 128 devices: a whole 4x4x4 slice. The times are simulated.
128 devices in a mesh: seq: 32 (over y, x, core), head: 4 (over z).
Axes of the slice: x: 4, y: 4, z: 4, core: 2. Of those that a mesh axis runs over, the one named last changes fastest.
Arguments:
- tokens: bfloat16 [2, 32768, 2048], P(None, ('seq', 'head')), may hold values from -6 to 6
- norm_gain: float32 [2048], replicated, may hold values from 0.25 to 1.75
- projection: bfloat16 [2048, 6144], P(None, 'head'), may hold values from -0.125 to 0.125
- level_table: float32 [16, 16, 18], P(None, 'head'), may hold values from 0.05 to 1
- level_index: int32 [2, 32768], P(None, 'seq'), may hold values from 0 to 15
- lengths: int32 [2], replicated, may hold values from 16384 to 32768, as said below
Outputs:
- attended: bfloat16 [2, 32768, 2048], P(None, 'seq', 'head')
Inputs may be any that keep to these rules, and one draw needn't show every extreme that they name: The first sequence is always whole: lengths[0] = 32768.
All inputs are finite; a program needn't handle non-finite values.
Results may differ from a plain program's by a relative error of at most 0.0097.
Values may be sent and summed in bfloat16 or wider, within the bound.
No kernel may reach another device: no remote copies, remote signals or barrier semaphores. Data moves between devices by JAX's collectives and lax.ppermute only.
A program may use at most 128 MiB of HBM per device.

v0:
```python
import jax
import jax.numpy as jnp
from jax import lax
from jax.sharding import PartitionSpec as P

SPAN = 512


def digit_count(values, limit):
    counted = jnp.zeros(values.shape, jnp.int32)
    for shift in range(limit):
        counted = counted + (values >= 1 << shift).astype(jnp.int32)
    return counted


def on_device(tokens, norm_gain, projection, level_table, level_index, lengths):
    batch_seqs, row_count, model_width = tokens.shape
    heads_here = level_table.shape[1]
    head_size = projection.shape[1] // (3 * heads_here)
    widened = tokens.astype(jnp.float32)
    normed = (
        widened * lax.rsqrt(jnp.mean(widened * widened, -1, keepdims=True) + 1e-06) * norm_gain
    ).astype(jnp.bfloat16)
    groups = lax.axis_size("head")
    block_len = row_count * groups
    block_rows = lax.all_gather(normed, "head", axis=1, tiled=True)
    projected_here = jnp.einsum(
        "srd,dc->src", block_rows, projection, preferred_element_type=jnp.float32
    )
    projected_here = projected_here.astype(jnp.bfloat16).reshape(
        batch_seqs, block_len, heads_here, 3, head_size
    )
    span_count = block_len // SPAN
    local_bits = span_count.bit_length() - 1
    lchunk = SPAN.bit_length() - 1
    table_count = level_table.shape[0]
    level_total = level_table.shape[2]
    onehot = (level_index[..., None] == jnp.arange(table_count, dtype=jnp.int32)).astype(
        jnp.float32
    )
    weights = jnp.einsum("stg,ghl->sthl", onehot, level_table, precision=lax.Precision.HIGHEST)
    weights = weights.reshape(batch_seqs, span_count, SPAN, heads_here, level_total)
    shaped = projected_here.reshape(batch_seqs, span_count, SPAN, heads_here, 3, head_size)
    queries = shaped[:, :, :, :, 0]
    keys_here = shaped[:, :, :, :, 1]
    values_here = shaped[:, :, :, :, 2]
    positions = jnp.arange(SPAN, dtype=jnp.int32)
    level_grid = digit_count(jnp.bitwise_xor(positions[:, None], positions[None, :]), lchunk + 1)
    causal = (positions[:, None] >= positions[None, :]).astype(jnp.float32)
    scores = jnp.einsum(
        "scthd,scuhd->schtu", queries, keys_here, preferred_element_type=jnp.float32
    )
    head_weights = weights.transpose(0, 1, 3, 2, 4)
    grid = jnp.zeros(scores.shape, jnp.float32)
    for level_step in range(lchunk + 1):
        grid = grid + head_weights[..., level_step][..., None] * (level_grid == level_step).astype(
            jnp.float32
        )
    weighted = (scores * grid * causal).astype(jnp.bfloat16)
    near_part = jnp.einsum(
        "schtu,scuhe->scthe", weighted, values_here, preferred_element_type=jnp.float32
    )
    states = jnp.einsum(
        "scthd,scthe->schde", keys_here, values_here, preferred_element_type=jnp.float32
    )
    totals = jnp.sum(states, axis=1)
    span_ids = jnp.arange(span_count, dtype=jnp.int32)
    span_dist = digit_count(jnp.bitwise_xor(span_ids[:, None], span_ids[None, :]), local_bits + 1)
    span_earlier = span_ids[None, :] < span_ids[:, None]
    level_step = 0
    span_mask = ((span_dist == level_step + 1) & span_earlier).astype(jnp.float32)
    bucket = jnp.einsum(
        "cb,sbhde->schde", span_mask, states, precision=lax.Precision.HIGHEST
    ).astype(jnp.bfloat16)
    readout = jnp.einsum("scthd,schde->scthe", queries, bucket, preferred_element_type=jnp.float32)
    far_part = weights[..., lchunk + 1 + level_step][..., None] * readout
    own_index = lax.axis_index("seq")
    seq_bits = lax.axis_size("seq").bit_length() - 1
    shards_part = lax.all_gather(totals[None], "seq", axis=0, tiled=True)
    others = jnp.arange(shards_part.shape[0], dtype=jnp.int32)
    distance = digit_count(jnp.bitwise_xor(others, own_index), seq_bits + 1)
    earlier = others < own_index
    levels_row = jnp.arange(1, seq_bits + 1, dtype=jnp.int32)
    selector = ((distance[None, :] == levels_row[:, None]) & earlier[None, :]).astype(jnp.float32)
    far_buckets = jnp.einsum(
        "jq,qshde->jshde", selector, shards_part, precision=lax.Precision.HIGHEST
    )
    for level_step in range(seq_bits):
        bucket = far_buckets[level_step].astype(jnp.bfloat16)
        readout = jnp.einsum(
            "scthd,shde->scthe", queries, bucket, preferred_element_type=jnp.float32
        )
        far_part = (
            far_part + weights[..., lchunk + local_bits + 1 + level_step][..., None] * readout
        )
    output = near_part + far_part
    output = output * lax.rsqrt(jnp.mean(output * output, -1, keepdims=True) + 1e-06)
    output = output.reshape(batch_seqs, block_len, heads_here * head_size)
    global_pos = own_index * block_len + jnp.arange(block_len, dtype=jnp.int32)
    valid = global_pos[None, :] < lengths[:, None]
    return jnp.where(valid[..., None], output, 0.0).astype(jnp.bfloat16)


def solution(mesh):
    in_specs = (
        P(None, ("seq", "head"), None),
        P(),
        P(None, "head"),
        P(None, "head", None),
        P(None, "seq"),
        P(),
    )
    out_specs = P(None, "seq", "head")
    return jax.shard_map(
        on_device, mesh=mesh, in_specs=in_specs, out_specs=out_specs, check_vma=False
    )
```

profile of v0, /device:TPU:1, one launch (start us, length us, event | category | flops | bytes accessed | tf_op | source)
XLA Modules:
  0.0 305.9 jit_solution(16156649064156791461)
XLA Ops:
  6.5 0.0 all-gather.4.cloned.1.call-start
  6.5 2.1 fusion.10
  8.6 3.5 %fusion.12 = bf16[2,256,2048]{2,1,0:T(8,128)(2,1)} fusion(bf16[2,256,2048]{2,1,0:T(8,128)(2,1)} %param.6, f32[2048]{0:T(1024)} %param.7, f32[2,256]{1,0:T(2,128)S(1)} %add_rsqrt_fusion.1), kind=kLoop, calls=%fused_computation.12 | loop fusion | flops 4194304 | bytes 4204544 | tf_op jit(solution)/shard_map/convert_element_type | solution.py:23
  12.1 0.0 all-gather.4.cloned.1.call-update
  12.1 0.0 all-gather.6.cloned.1.call-start
  12.2 86.4 %all-gather.4.cloned.1.call-done = bf16[2,1024,2048]{2,1,0:T(8,128)(2,1)} async-done(((bf16[2,256,2048]{2,1,0:T(8,128)(2,1)}), bf16[2,1024,2048]{2,1,0:T(8,128)(2,1)}) %all-gather.4.cloned.1.call-update) | async-done | bytes 8388624 | tf_op jit(solution)/shard_map/all_gather | solution.py:26
  98.6 18.7 %fusion.7 = bf16[2,1024,1536]{2,1,0:T(8,128)(2,1)} fusion(bf16[2,1024,2048]{2,1,0:T(8,128)(2,1)} %all-gather.4.cloned.1.call-done, bf16[2048,1536]{1,0:T(8,128)(2,1)} %param.8), kind=kOutput, calls=%fused_computation.7 | convolution fusion | flops 12888047616 | bytes 20971520 | tf_op jit(solution)/shard_map/srd,dc->src/dot_general | solution.py:27
  117.2 8.7 %copy.83 = bf16[2,1024,1536]{1,2,0:T(8,128)(2,1)} copy(bf16[2,1024,1536]{2,1,0:T(8,128)(2,1)} %fusion.7) | data formatting | bytes 12582912 | tf_op jit(solution)/shard_map/convert_element_type | solution.py:30
  125.9 11.2 %reshape_reshape.3 = bf16[2,2,512,4,3,128]{2,1,5,4,3,0:T(2,128)(2,1)} reshape(bf16[2,1024,1536]{1,2,0:T(8,128)(2,1)} %copy.83) | data formatting | bytes 12582912 | tf_op jit(solution)/shard_map/reshape;reshape | solution.py:43
  137.1 7.5 %fusion.88 = (bf16[2,2,512,4,1,128]{2,1,5,4,3,0:T(2,128)(2,1)}, bf16[2,2,512,4,1,128]{2,1,5,4,3,0:T(2,128)(2,1)}, bf16[2,2,512,4,1,128]{2,1,5,4,3,0:T(2,128)(2,1)}) fusion(bf16[2,2,512,4,3,128]{2,1,5,4,3,0:T(2,128)(2,1)} %reshape_reshape.3), kind=kLoop, calls=%fused_computation.139 | loop fusion | bytes 12582912 | tf_op jit(solution)/shard_map/slice | solution.py:46
  144.6 4.9 %copy.134 = bf16[2,2,512,4,1,128]{5,2,3,1,0,4:T(8,128)(2,1)S(1)} copy(bf16[2,2,512,4,1,128]{2,1,5,4,3,0:T(2,128)(2,1)} %get-tuple-element.6) | data formatting | bytes 4194304
  149.5 0.0 copy-start.8
  149.5 0.0 copy-start.15
  149.5 0.0 copy-start.16
  149.5 5.0 %fusion.91 = (f32[2,4,128,128]{3,2,1,0:T(8,128)}, f32[2,2,4,128,128]{4,3,2,1,0:T(8,128)}) fusion(bf16[2,2,512,4,1,128]{2,1,5,4,3,0:T(2,128)(2,1)} %get-tuple-element.5, bf16[2,2,512,4,1,128]{5,2,3,1,0,4:T(8,128)(2,1)S(1)} %copy.134), kind=kOutput, calls=%fused_computation.142 | convolution fusion | flops 268566528 | bytes 5767168 | tf_op jit(solution)/shard_map/scthd,scthe->schde/dot_general | solution.py:63
  154.6 0.0 all-gather.6.cloned.1.call-update
  154.6 0.0 copy-done.15
  154.6 0.0 copy-done.16
  154.6 0.5 fusion.60
  155.1 0.5 reshape.258
  155.6 0.0 copy-done.8
  155.6 0.3 copy.157
  156.0 0.6 copy.109
  156.6 0.6 copy.107
  157.3 0.6 copy.104
  157.9 0.6 copy.113
  158.8 0.3 compare_convert_fusion.9
  159.0 1.8 compare_convert_fusion.7
  160.8 1.7 compare_convert_fusion.5
  162.6 1.8 compare_convert_fusion.3
  164.3 1.8 compare_convert_fusion.1
  166.1 1.7 fusion.52
  167.8 0.0 copy-done.17
  167.8 0.1 broadcast_compare_fusion
  167.9 5.1 %copy.133 = bf16[2,2,512,4,1,128]{5,2,3,1,0,4:T(8,128)(2,1)S(1)} copy(bf16[2,2,512,4,1,128]{2,1,5,4,3,0:T(2,128)(2,1)} %get-tuple-element.7) | data formatting | bytes 4194304
  173.0 0.0 copy-start
  173.0 0.0 copy-start.1
  173.0 0.0 copy-start.2
  173.0 0.0 copy-start.3
  173.1 4.0 %fusion.40 = bf16[2,2,4,128,128]{4,1,3,2,0:T(2,128)(2,1)S(1)} fusion(f32[2,2,4,128,128]{4,3,2,1,0:T(8,128)} %get-tuple-element.32), kind=kOutput, calls=%fused_computation.47 | convolution fusion | flops 6553636 | bytes 1572864 | tf_op jit(solution)/shard_map/cb,sbhde->schde/dot_general | solution.py:72
  177.0 2.7 fusion.33
  179.8 0.0 copy-done
  179.8 0.0 copy-done.2
  179.8 23.3 %multiply_convert_fusion.3.clone.4 = bf16[2,2,4,512,512]{4,3,2,1,0:T(8,128)(2,1)} fusion(f32[512,512]{1,0:T(8,128)} %get-tuple-element.35, f32[512,512]{1,0:T(8,128)} %get-tuple-element.36, f32[2,2,4,512]{3,2,1,0:T(4,128)S(1)} %copy.98, f32[512,512]{1,0:T(8,128)S(1)} %copy-done.6, f32[2,2,4,512]{3,2,1,0:T(4,128)S(1)} %copy.97, ...), kind=kOutput, calls=%fused_computation.2.clone.clone.clone.clone.clone.clone.1 | convolution fusion | flops 1166016512 | bytes 24444928 | tf_op jit(solution)/shard_map/scthd,scuhd->schtu/dot_general | solution.py:50
  203.1 25.4 %all-gather.6.cloned.1.call-done = f32[64,4,128,128]{3,2,1,0:T(8,128)} async-done(((f32[2,4,128,128]{3,2,1,0:T(8,128)}), f32[64,4,128,128]{3,2,1,0:T(8,128)}) %all-gather.6.cloned.1.call-update) | async-done | bytes 16777232 | tf_op jit(solution)/shard_map/all_gather | solution.py:79
  228.5 20.0 %fusion.37 = bf16[5,2,4,128,128]{4,0,3,2,1:T(8,128)(2,1)S(1)} fusion(f32[32,2,4,128,128]{4,3,2,1,0:T(8,128)} %bitcast.175, s32[32]{0:T(128)S(1)} %fusion.83, s32[5]{0:T(128)S(1)} %iota_add_fusion.1, pred[32]{0:T(512)(128)(4,1)S(1)} %iota_compare_fusion.2), kind=kOutput, calls=%fused_computation.45 | convolution fusion | flops 252313920 | bytes 18088116 | tf_op jit(solution)/shard_map/jq,qshde->jshde/dot_general | solution.py:85
  248.6 3.4 %fusion.89 = (bf16[1,2,4,128,128]{4,0,3,2,1:T(2,128)(2,1)}, bf16[1,2,4,128,128]{4,0,3,2,1:T(2,128)(2,1)}, bf16[1,2,4,128,128]{4,0,3,2,1:T(2,128)(2,1)}, bf16[1,2...) fusion(bf16[5,2,4,128,128]{4,0,3,2,1:T(8,128)(2,1)S(1)} %fusion.37), kind=kLoop, calls=%fused_computation.140 | loop fusion | bytes 2621440 | tf_op jit(solution)/shard_map/slice | solution.py:89
  252.0 1.9 copy.127
  253.9 1.3 copy.131
  255.2 1.9 copy.130
  257.1 1.0 copy.129
  258.0 0.6 copy.128
  258.6 3.7 %fusion.31 = f32[2,4,128,2,512]{4,2,1,3,0:T(8,128)} fusion(bf16[2,2,512,4,1,128]{5,2,3,1,0,4:T(8,128)(2,1)S(1)} %copy.133, bf16[1,2,4,128,128]{3,4,2,1,0:T(8,128)(2,1)} %copy.127), kind=kOutput, calls=%fused_computation.39 | convolution fusion | flops 268435456 | bytes 6553600 | tf_op jit(solution)/shard_map/scthd,shde->scthe/dot_general | solution.py:90
  262.3 2.7 fusion.29
  265.0 2.6 fusion.27
  267.7 2.7 fusion.25
  270.4 2.7 fusion.23
  273.0 0.0 copy-done.11
  273.0 0.0 copy-done.13
  273.0 16.2 %multiply_reduce_fusion = (f32[2,2,512,4]{2,3,1,0:T(4,128)S(1)}, f32[2,2,512,4,128]{2,4,3,1,0:T(8,128)}) fusion(f32[2,4,128,2,512]{4,2,1,3,0:T(8,128)} %fusion.23, f32[2,2,512,4]{2,3,1,0:T(4,128)S(1)} %copy-done.14, f32[2,4,128,2,512]{4,2,1,3,0:T(8,128)} %fusion.25, f32[2,2,512,4]{2,3,1,0:T(4,128)S(1)} %copy.111, f32[2,4,128,2,512]{4,2,1,3,0:T(8,128)} %fusion.27, ...), kind=kOutput, calls=%fused_computation.26 | convolution fusion | flops 1088413696 | bytes 40075264 | tf_op jit(solution)/shard_map/schtu,scuhe->scthe/dot_general | solution.py:60
  289.3 2.8 broadcast_multiply_fusion
  292.1 2.5 copy.115
  294.6 2.7 reshape.246
  297.4 1.7 select_convert_fusion
  (41 shorter events, 0.3 us)
Async XLA Ops:
  6.5 92.0 %all-gather.4.cloned.1.call-start = ((), (), s32[]{:S(2)}) async-start(), calls=%async_computation | async-start | bytes 10485760 | tf_op jit(solution)/shard_map/all_gather | solution.py:26
  12.1 216.4 %all-gather.6.cloned.1.call-start = ((), (), s32[]{:S(2)}) async-start(), calls=%async_computation.1 | async-start | bytes 17301504 | tf_op jit(solution)/shard_map/all_gather | solution.py:79
  149.5 6.1 %copy-start.8 = (bf16[2,2,512,4,1,128]{5,2,3,1,0,4:T(8,128)(2,1)}, bf16[2,2,512,4,1,128]{5,2,3,1,0,4:T(8,128)(2,1)S(1)}, u32[]{:S(2)}) copy-start(bf16[2,2,512,4,1,128]{5,2,3,1,0,4:T(8,128)(2,1)S(1)} %copy.134) | copy-start | bytes 6291460
  149.5 5.1 %copy-start.15 = (f32[16,4,18]{2,1,0:T(4,128)S(1)}, f32[16,4,18]{2,1,0:T(4,128)}, u32[]{:S(2)}) copy-start(f32[16,4,18]{2,1,0:T(4,128)} %param.9) | copy-start | bytes 13828
  149.5 5.1 %copy-start.16 = (s32[2,1024]{1,0:T(2,128)S(1)}, s32[2,1024]{1,0:T(2,128)}, u32[]{:S(2)}) copy-start(s32[2,1024]{1,0:T(2,128)} %param.10) | copy-start | bytes 24580
  160.8 7.0 %copy-start.17 = (s32[2]{0:T(128)S(1)}, s32[2]{0:T(128)}, u32[]{:S(2)}) copy-start(s32[2]{0:T(128)} %param.11) | copy-start | bytes 28
  173.0 6.8 %copy-start = (f32[512,512]{1,0:T(8,128)S(1)}, f32[512,512]{1,0:T(8,128)}, u32[]{:S(2)}) copy-start(f32[512,512]{1,0:T(8,128)} %get-tuple-element.43) | copy-start | bytes 3145732
  173.0 6.8 %copy-start.1 = (f32[512,512]{1,0:T(8,128)S(1)}, f32[512,512]{1,0:T(8,128)}, u32[]{:S(2)}) copy-start(f32[512,512]{1,0:T(8,128)} %get-tuple-element.44) | copy-start | bytes 3145732
  173.0 6.8 %copy-start.2 = (f32[512,512]{1,0:T(8,128)S(1)}, f32[512,512]{1,0:T(8,128)}, u32[]{:S(2)}) copy-start(f32[512,512]{1,0:T(8,128)} %get-tuple-element.41) | copy-start | bytes 3145732
  173.0 6.8 %copy-start.3 = (f32[512,512]{1,0:T(8,128)S(1)}, f32[512,512]{1,0:T(8,128)}, u32[]{:S(2)}) copy-start(f32[512,512]{1,0:T(8,128)} %get-tuple-element.42) | copy-start | bytes 3145732
  173.0 6.8 %copy-start.4 = (f32[512,512]{1,0:T(8,128)S(1)}, f32[512,512]{1,0:T(8,128)}, u32[]{:S(2)}) copy-start(f32[512,512]{1,0:T(8,128)} %get-tuple-element.39) | copy-start | bytes 3145732
  173.0 6.8 %copy-start.5 = (f32[512,512]{1,0:T(8,128)S(1)}, f32[512,512]{1,0:T(8,128)}, u32[]{:S(2)}) copy-start(f32[512,512]{1,0:T(8,128)} %get-tuple-element.40) | copy-start | bytes 3145732
  173.0 6.8 %copy-start.6 = (f32[512,512]{1,0:T(8,128)S(1)}, f32[512,512]{1,0:T(8,128)}, u32[]{:S(2)}) copy-start(f32[512,512]{1,0:T(8,128)} %get-tuple-element.37) | copy-start | bytes 3145732
  173.0 6.8 %copy-start.7 = (f32[512,512]{1,0:T(8,128)S(1)}, f32[512,512]{1,0:T(8,128)}, u32[]{:S(2)}) copy-start(f32[512,512]{1,0:T(8,128)} %get-tuple-element.38) | copy-start | bytes 3145732
  262.3 2.7 copy-start.10
  265.0 2.6 copy-start.9
  270.3 2.7 copy-start.11
  270.4 2.7 copy-start.12
  270.4 2.7 copy-start.13
  270.4 2.7 copy-start.14
Sparse Core Ops, SparseCore 0:
  12.2 86.3 all-gather.3
  154.7 73.7 all-gather.5
where the time goes:
time: 307 us; the launch traced here: 306 us
  waiting for transfers between devices  112 us (36%)
  matrix products  105 us (34%)
  local copies, waits for them, and re-layouts  56.2 us (18%)
  other arithmetic  19.2 us (6%)
  between operations  13.8 us (4%)
    all_gather x1, waiting for transfers between devices, on_device(): block_rows = lax.all_gather(normed, 'head', axis=1, tiled=True)  86.4 us
    all_gather x1, waiting for transfers between devices, on_device(): shards_part = lax.all_gather(totals[None], 'seq', axis=0, tiled=True)  25.4 us
    dot_general x1, matrix products, on_device(): jnp.einsum('scthd,scuhd->schtu', queries, keys_here, preferred_element_ty...  23.3 us
    dot_general x1, matrix products, on_device(): jnp.einsum('jq,qshde->jshde', selector, shards_part, precision=lax.Precis...  20 us
    dot_general x1, matrix products, on_device(): jnp.einsum('srd,dc->src', block_rows, projection, preferred_element_type=...  18.7 us
    dot_general x1, matrix products, on_device(): jnp.einsum('schtu,scuhe->scthe', weighted, values_here, preferred_element...  16.2 us
    dot_general x5, matrix products, on_device(): jnp.einsum('scthd,shde->scthe', queries, bucket, preferred_element_type=j...  14.4 us
    another operation x1, local copies, waits for them, and re-layouts, on_device(): projected_here.reshape(batch_seqs, span_count, SPAN, heads_here, 3, head_...  11.2 us
  transfers between devices with their start and end apart: 2, of which 2 were waited for; matrix products, arithmetic and copies ran while one was open for 16% of the time, Pallas kernels for 0%

commit v1 on v0

v1 whole, which is shorter than its diff:
```python
import jax
import jax.numpy as jnp
from jax import lax
from jax.experimental import pallas as pl
from jax.experimental.pallas import tpu as pltpu
from jax.sharding import PartitionSpec as P


TILE = 128
ROWS = 2 * TILE
F32 = jnp.float32
BF16 = jnp.bfloat16
NT = (((1,), (1,)), ((), ()))


def in_vmem(value):
    return pltpu.with_memory_space_constraint(value, pltpu.VMEM)


def fold_kernel(gain_ref, w_ref, out_ref):
    for at in range(0, w_ref.shape[0], TILE):
        column = jnp.broadcast_to(gain_ref[:, at : at + TILE], (TILE, TILE)).T
        for lane in range(0, w_ref.shape[1], TILE):
            part = w_ref[at : at + TILE, lane : lane + TILE].astype(F32) * column
            out_ref[at : at + TILE, lane : lane + TILE] = part.astype(BF16)


def fold_gain(gain, projection):
    width, cols = projection.shape
    return pl.pallas_call(
        fold_kernel,
        grid=(width // ROWS,),
        in_specs=[
            pl.BlockSpec((1, ROWS), lambda i: (0, i)),
            pl.BlockSpec((ROWS, cols), lambda i: (i, 0)),
        ],
        out_specs=pl.BlockSpec((ROWS, cols), lambda i: (i, 0)),
        out_shape=pltpu.VMEM((width, cols), BF16),
        compiler_params=pltpu.CompilerParams(vmem_limit_bytes=8 << 20),
        name="fold_gain",
    )(gain.reshape(1, width), pltpu.with_memory_space_constraint(projection, pltpu.HBM))


def place_of(relative):
    return (lax.axis_index("head") + (0, 3, 1, 2)[relative]) % 4


def project_kernel(pieces, relatives, heads_step, level_rows):
    cols = heads_step * 384
    chunks = len(relatives)

    def body(*refs):
        xs = refs[: len(pieces)]
        w_ref, wt_ref = refs[len(pieces) : len(pieces) + 2]
        q_ref, near_ref, state_ref, wt_out, held, scales = refs[len(pieces) + 2 :]
        step = pl.program_id(0)

        @pl.when(step == 0)
        def _():
            at = 0
            sums = []
            for x_ref, (count, rows) in zip(xs, pieces):
                for i in range(count):
                    x = x_ref[i]
                    held[pl.ds(at, rows), :] = x
                    at += rows
                    total = jnp.zeros((rows, TILE), F32)
                    for lane in range(0, x.shape[1], TILE):
                        part = x[:, lane : lane + TILE].astype(F32)
                        total = total + part * part
                    sums.append(total)
            sums = jnp.concatenate(sums, axis=0)
            ones = jnp.full((8, TILE), 1.0, F32)
            for c in range(chunks):
                mean = lax.dot_general(
                    ones,
                    sums[c * ROWS : (c + 1) * ROWS],
                    NT,
                    precision=lax.Precision.HIGHEST,
                    preferred_element_type=F32,
                ) * (1.0 / held.shape[1])
                scales[c] = lax.rsqrt(mean + 1e-06)

        source = lax.broadcasted_iota(jnp.int32, (TILE, TILE), 0)
        target = lax.broadcasted_iota(jnp.int32, (TILE, TILE), 1)
        differ = jnp.bitwise_xor(source, target)
        causal = source <= target
        zeros = jnp.zeros((TILE, TILE), BF16)
        every = [(c, hh) for c in range(chunks) for hh in range(heads_step)]
        qkv = jnp.dot(held[...], w_ref[:, pl.ds(pl.multiple_of(step * cols, cols), cols)], preferred_element_type=F32)
        q, k, v, scores = {}, {}, {}, {}
        for c in range(chunks):
            scale = scales[c, 0:1, :]
            wt_out[c] = wt_ref[0, place_of(relatives[c])] * scale
            rows = slice(c * ROWS, (c + 1) * ROWS)
            for hh in range(heads_step):
                at = hh * 384
                q[c, hh] = qkv[rows, at : at + 128].T.astype(BF16)
                k[c, hh] = qkv[rows, at + 128 : at + 256].astype(BF16)
                v[c, hh] = (qkv[rows, at + 256 : at + 384].T * (scale * scale)).astype(BF16)
                q_ref[c, hh * 128 : (hh + 1) * 128, :] = q[c, hh]
        for i in every:
            scores[i] = jnp.dot(k[i], q[i], preferred_element_type=F32)
            state_ref[i[0], i[1]] = jnp.dot(v[i], k[i], preferred_element_type=F32)
        for c, hh in every:
            base = hh * level_rows
            blocks = []
            for t in range(2):
                lanes = slice(t * TILE, (t + 1) * TILE)
                grid = wt_out[c, base : base + 1, lanes]
                for level in range(1, 8):
                    row = wt_out[c, base + level : base + level + 1, lanes]
                    grid = jnp.where(differ >= 1 << (level - 1), row, grid)
                grid = jnp.where(causal, grid, 0.0)
                blocks.append((scores[c, hh][lanes, lanes] * grid).astype(BF16))
            row = wt_out[c, base + 8 : base + 9, TILE:]
            cross = (scores[c, hh][:TILE, TILE:] * row).astype(BF16)
            weighted = jnp.concatenate(
                [
                    jnp.concatenate([blocks[0], cross], axis=1),
                    jnp.concatenate([zeros, blocks[1]], axis=1),
                ],
                axis=0,
            )
            near = jnp.dot(v[c, hh], weighted, preferred_element_type=F32)
            near_ref[c, hh * 128 : (hh + 1) * 128, :] = near

    return body


def project(xs, seq, relatives, weight, wt, pick=0):
    pieces = [(1, x.shape[1]) for x in xs]
    chunks = len(relatives)
    width, cols = weight.shape
    heads = cols // 384
    heads_step = 2 if heads % 2 == 0 else 1
    level_rows = wt.shape[2] // heads
    rows = chunks * ROWS
    return pl.pallas_call(
        project_kernel(pieces, relatives, heads_step, level_rows),
        grid=(heads // heads_step,),
        in_specs=[pl.BlockSpec((1,) + x.shape[1:], lambda j: (pick, 0, 0)) for x in xs]
        + [pl.BlockSpec(memory_space=pltpu.VMEM)]
        + [pl.BlockSpec((1, 4, heads_step * level_rows, ROWS), lambda j: (seq, 0, j, 0))],
        out_specs=[
            pl.BlockSpec((chunks, heads_step * 128, ROWS), lambda j: (0, j, 0)),
            pl.BlockSpec((chunks, heads_step * 128, ROWS), lambda j: (0, j, 0)),
            pl.BlockSpec((chunks, heads_step, 128, 128), lambda j: (0, j, 0, 0)),
            pl.BlockSpec((chunks, heads_step * level_rows, ROWS), lambda j: (0, j, 0)),
        ],
        scratch_shapes=[pltpu.VMEM((rows, width), BF16), pltpu.VMEM((chunks, 8, ROWS), F32)],
        out_shape=[
            pltpu.VMEM((chunks, heads * 128, ROWS), BF16),
            pltpu.VMEM((chunks, heads * 128, ROWS), F32),
            pltpu.VMEM((chunks, heads, 128, 128), F32),
            pltpu.VMEM((chunks, heads * level_rows, ROWS), F32),
        ],
        cost_estimate=pl.CostEstimate(
            flops=2 * rows * width * cols, transcendentals=rows, bytes_accessed=width * cols * 2
        ),
        compiler_params=pltpu.CompilerParams(vmem_limit_bytes=16 << 20),
        name="project_near",
    )(*xs, in_vmem(weight), wt)


def far_kernel(seq, half_heads):
    before = [1, 3, 0, 2]

    def body(lengths_ref, *refs):
        qs, nears, states, wts = refs[0:4], refs[4:8], refs[8:12], refs[12:16]
        core_ref, mine_ref, other_ref = refs[16:19]
        out_ref = refs[-1]
        core = lax.axis_index("seq") % 2
        places = [place_of(r) for r in range(4)]
        limit = lengths_ref[seq] - lax.axis_index("seq") * (4 * ROWS)
        st = [states[r][0, 0] for r in range(4)]
        is_mine = pl.program_id(0) // half_heads == core
        level11 = (core_ref[0].astype(F32) * core.astype(F32)).astype(BF16)
        levels = mine_ref.shape[0]
        picked = [jnp.where(is_mine, mine_ref[j, 0], other_ref[j, 0]) for j in range(levels)]
        far_buckets = jnp.concatenate([level11] + picked, axis=1)
        at = lax.broadcasted_iota(jnp.int32, (1, ROWS), 1)
        for r in range(4):
            place = places[r]
            q = qs[r][0]
            level9 = st[before[r]] * (place % 2).astype(F32)
            upper = (place // 2).astype(F32)
            level10 = sum(
                [st[o] * (upper * (1 - places[o] // 2).astype(F32)) for o in range(4) if o != r]
            )
            mats = jnp.concatenate(
                [level9.astype(BF16), level10.astype(BF16), far_buckets], axis=1
            )
            q16 = q.reshape(8, 16, ROWS)
            scaled = []
            for j in range(3 + levels):
                row = jnp.broadcast_to(wts[r][0, 9 + j : 10 + j, :], (16, ROWS)).astype(BF16)
                scaled.append((q16 * row[None]).reshape(128, ROWS))
            scaled = jnp.concatenate(scaled, axis=0)
            acc = nears[r][0] + jnp.dot(mats, scaled, preferred_element_type=F32)
            scale = lax.rsqrt(jnp.mean(acc * acc, 0, keepdims=True) + 1e-06)
            valid = place * ROWS + at < limit
            acc = jnp.where(valid, acc * scale, 0.0)
            out_ref[0, place] = acc.T.astype(BF16)

    return body


def far(lengths, chunks, core_bucket, mine, other, seq, out_prev, seqs):
    heads = core_bucket.shape[0]
    levels, half_heads = mine.shape[:2]
    level_rows = chunks[0][0][3].shape[1] // heads
    picks = [c for _, c in chunks]
    in_specs = (
        [pl.BlockSpec(memory_space=pltpu.SMEM)]
        + [pl.BlockSpec((1, 128, ROWS), lambda h, c=c: (c, h, 0)) for c in picks]
        + [pl.BlockSpec((1, 128, ROWS), lambda h, c=c: (c, h, 0)) for c in picks]
        + [pl.BlockSpec((1, 1, 128, 128), lambda h, c=c: (c, h, 0, 0)) for c in picks]
        + [pl.BlockSpec((1, level_rows, ROWS), lambda h, c=c: (c, h, 0)) for c in picks]
        + [pl.BlockSpec((1, 128, 128), lambda h: (h, 0, 0))]
        + [pl.BlockSpec((levels, 1, 128, 128), lambda h: (0, h % half_heads, 0, 0))] * 2
    )
    args = [lengths] + [in_vmem(call[i]) for i in range(4) for call, _ in chunks]
    args += [core_bucket, mine, other]
    aliases = {}
    if out_prev is not None:
        in_specs.append(pl.BlockSpec(memory_space=pl.ANY))
        args.append(out_prev)
        aliases = {len(args) - 1: 0}
    return pl.pallas_call(
        far_kernel(seq, half_heads),
        grid=(heads,),
        in_specs=in_specs,
        out_specs=pl.BlockSpec((1, 4, ROWS, 128), lambda h: (seq, 0, 0, h)),
        out_shape=jax.ShapeDtypeStruct((seqs, 4, ROWS, heads * 128), BF16),
        input_output_aliases=aliases,
        cost_estimate=pl.CostEstimate(
            flops=2 * 1024 * 128 * 128 * heads * 7, transcendentals=0, bytes_accessed=5 << 20
        ),
        compiler_params=pltpu.CompilerParams(vmem_limit_bytes=8 << 20),
        name="far_part",
    )(*args)


def small_call(body, outs, *args):
    return pl.pallas_call(
        body,
        in_specs=[pl.BlockSpec(memory_space=pltpu.VMEM)] * len(args),
        out_specs=[pl.BlockSpec(memory_space=pltpu.VMEM)] * len(outs),
        out_shape=[jax.ShapeDtypeStruct(shape, dtype) for shape, dtype in outs],
        compiler_params=pltpu.CompilerParams(vmem_limit_bytes=4 << 20),
    )(*args)


def seq_bit(j):
    return (lax.axis_index("seq") // (1 << j)) % 2


def total_kernel(own_ref, ab_ref, cd_ref, total_ref, sent_ref):
    total = own_ref[0] + ab_ref[0] + ab_ref[1] + cd_ref[0]
    total_ref[...] = total
    sent_ref[...] = total.astype(BF16)


def core_kernel(total_ref, received_ref, part_ref, sent_ref):
    half = part_ref.shape[0]
    heads = pl.ds(seq_bit(0) * half, half)
    part = total_ref[heads] + received_ref[heads].astype(F32)
    part_ref[...] = part
    sent_ref[...] = part.astype(BF16)


def stage_kernel(low, last):
    def body(part_ref, one_ref, two_ref, three_ref, *refs):
        one, two, three = [r[...].astype(F32) for r in (one_ref, two_ref, three_ref)]
        near_level = (one * seq_bit(low).astype(F32)).astype(BF16)
        far_level = ((two + three) * seq_bit(low + 1).astype(F32)).astype(BF16)
        if last:
            before_ref, mine_ref = refs
            count = before_ref.shape[0]
            mine_ref[0:count] = before_ref[...]
            mine_ref[count] = near_level
            mine_ref[count + 1] = far_level
        else:
            mine_ref, next_ref, sent_ref = refs
            mine_ref[0] = near_level
            mine_ref[1] = far_level
            part = part_ref[...] + (one + (two + three))
            next_ref[...] = part
            sent_ref[...] = part.astype(BF16)

    return body


def exchange(own, ab, cd):
    size = lax.axis_size("seq")
    heads = own.shape[1]
    whole, half = (heads, 128, 128), (heads // 2, 128, 128)

    def swap(value, mask):
        return lax.ppermute(value, "seq", [(i, i ^ mask) for i in range(size)])

    total, sent = small_call(
        total_kernel, [(whole, F32), (whole, BF16)], *map(in_vmem, (own, ab, cd))
    )
    core_bucket = swap(sent, 1)
    part, sent = small_call(core_kernel, [(half, F32), (half, BF16)], total, core_bucket)
    heard = [swap(sent, mask << 1) for mask in (1, 2, 3)]
    levels, part, sent = small_call(
        stage_kernel(1, False), [((2,) + half, BF16), (half, F32), (half, BF16)], part, *heard
    )
    heard = [swap(sent, mask << 3) for mask in (1, 2, 3)]
    (mine,) = small_call(stage_kernel(3, True), [((4,) + half, BF16)], part, *heard, levels)
    return core_bucket, mine, swap(mine, 1)


def on_device(tokens, norm_gain, projection, level_table, level_index, lengths):
    seqs, row_count, _ = tokens.shape
    tables, heads, level_total = level_table.shape
    groups = lax.axis_size("head")
    half = row_count // 2
    up = [(i, (i + 1) % groups) for i in range(groups)]
    down = [(i, (i - 1) % groups) for i in range(groups)]

    got = []
    held = tokens
    for s in range(seqs):
        low, high = held[s : s + 1, :half], held[s : s + 1, half:]
        a_low = lax.ppermute(low, "head", up)
        b_high = lax.ppermute(high, "head", down)
        a_high = lax.ppermute(high, "head", up)
        b_low = lax.ppermute(low, "head", down)
        if s + 1 < seqs:
            held, a_low, b_high = lax.optimization_barrier((tokens, a_low, b_high))
        c = lax.ppermute(a_low, "head", up)
        d = lax.ppermute(b_high, "head", down)
        got.append(([a_low, a_high, b_low, b_high], [c, d]))

    level_rows = -(-level_total // 8) * 8
    onehot = (level_index[..., None] == jnp.arange(tables, dtype=jnp.int32)).astype(F32)
    table = jnp.pad(level_table, ((0, 0), (0, 0), (0, level_rows - level_total)))
    wt = jnp.einsum(
        "gm,szrg->szmr",
        table.reshape(tables, heads * level_rows),
        onehot.reshape(seqs, groups, row_count, tables),
        precision=lax.Precision.HIGHEST,
    )

    weight = fold_gain(norm_gain, projection)

    own = []
    for s in range(seqs):
        own.append(project([tokens], s, [0], weight, wt, s))
    parts = []
    for s in range(seqs):
        ab = project(got[s][0], s, [1, 2], weight, wt)
        cd = project(got[s][1], s, [3], weight, wt)
        parts.append((ab, cd))

    out = None
    for s in range(seqs):
        ab, cd = parts[s]
        core_bucket, mine, other = exchange(own[s][2], ab[2], cd[2])
        chunks = [(own[s], 0), (ab, 0), (ab, 1), (cd, 0)]
        out = far(lengths, chunks, core_bucket, mine, other, s, out, seqs)
    return out.reshape(seqs, row_count * groups, heads * 128)


def solution(mesh):
    in_specs = (
        P(None, ("seq", "head"), None),
        P(),
        P(None, "head"),
        P(None, "head", None),
        P(None, "seq"),
        P(),
    )
    out_specs = P(None, "seq", "head")

    return jax.shard_map(on_device, mesh=mesh, in_specs=in_specs, out_specs=out_specs, check_vma=False)
```

time: 307 us -> 118 us (0.38)
  matrix products: 105 us -> 0.51 us
  waiting for transfers between devices: 112 us -> 34.2 us
  local copies, waits for them, and re-layouts: 56.2 us -> 1.54 us
  starting transfers between devices: 0.04 us -> 41.5 us
  Pallas kernels: 0 us -> 39.9 us
  other arithmetic: 19.2 us -> 0 us
  between operations: 13.8 us -> 0.22 us
    all_gather x2 -> x0, waiting for transfers between devices: 112 us -> none  [the longest x1 86.4 us: on_device(): block_rows = lax.all_gather(normed, 'head', axis=1, tiled=True)]
    dot_general x13 -> x1, matrix products: 105 us -> 0.51 us  [on_device(): jnp.einsum('gm,szrg->szmr', table.reshape(tables, heads * level_rows), on...]
    ppermute x0 -> x28, starting transfers between devices: none -> 41.5 us  [the longest x16 25.5 us: swap(): return lax.ppermute(value, 'seq', [(i, i ^ mask) for i in range(size)])]
    pallas_call x0 -> x17, Pallas kernels: none -> 39.9 us  [the longest x6 25.8 us: project(): pl.pallas_call(project_kernel(pieces, relatives, heads_step, level_rows),...]
    ppermute x0 -> x28, waiting for transfers between devices: none -> 34.2 us  [the longest x16 9.88 us: swap(): return lax.ppermute(value, 'seq', [(i, i ^ mask) for i in range(size)])]
    convert_element_type x6 -> x0, local copies, waits for them, and re-layouts: 15.3 us -> none  [the longest x1 8.65 us: on_device(): projected_here.astype(jnp.bfloat16)]
    convert_element_type x8 -> x0, other arithmetic: 14.2 us -> none  [the longest x5 7.33 us: on_device(): (level_grid == level_step).astype(jnp.float32)]
    another operation x1 -> x0, local copies, waits for them, and re-layouts: 11.2 us -> none  [on_device(): projected_here.reshape(batch_seqs, span_count, SPAN, heads_here, 3, head_...]
  transfers between devices with their start and end apart: 2 -> 28, of which waited for: 2 -> 10; matrix products, arithmetic and copies ran while one was open for 16% -> 1% of each run, Pallas kernels for 0% -> 28%
where the time goes in v1:
time: 118 us
  starting transfers between devices  41.5 us (35%)
  Pallas kernels  39.9 us (34%)
  waiting for transfers between devices  34.2 us (29%)
  local copies, waits for them, and re-layouts  1.54 us (1%)
    pallas_call x6, Pallas kernels, project(): pl.pallas_call(project_kernel(pieces, relatives, heads_step, level_rows),...  25.8 us
    ppermute x16, starting transfers between devices, swap(): return lax.ppermute(value, 'seq', [(i, i ^ mask) for i in range(size)])  25.5 us
    ppermute x16, waiting for transfers between devices, swap(): return lax.ppermute(value, 'seq', [(i, i ^ mask) for i in range(size)])  9.88 us
    ppermute x2, waiting for transfers between devices, on_device(): a_low = lax.ppermute(low, 'head', up)  9.4 us
    pallas_call x2, Pallas kernels, far(): pl.pallas_call(far_kernel(seq, half_heads), grid=(heads,), in_specs=in_sp...  7.8 us
    ppermute x2, waiting for transfers between devices, on_device(): c = lax.ppermute(a_low, 'head', up)  7.51 us
    ppermute x2, waiting for transfers between devices, on_device(): a_high = lax.ppermute(high, 'head', up)  7.45 us
    pallas_call x1, Pallas kernels, fold_gain(): pl.pallas_call(fold_kernel, grid=(width // ROWS,), in_specs=[pl.BlockSpec...  6.03 us
  transfers between devices with their start and end apart: 28, of which 10 were waited for; matrix products, arithmetic and copies ran while one was open for 1% of the time, Pallas kernels for 28%

profile of v1, /device:TPU:1, one launch (start us, length us, event | category | flops | bytes accessed | tf_op | source)
XLA Modules:
  0.0 117.9 jit_solution(8028925883862370345)
XLA Ops:
  0.0 1.3 %fusion.3 = (bf16[1,128,2048]{2,1,0:T(8,128)(2,1)S(1)}, bf16[1,128,2048]{2,1,0:T(8,128)(2,1)S(1)}) fusion(bf16[2,256,2048]{2,1,0:T(8,128)(2,1)} %refs_0_.3), kind=kLoop, calls=%fused_computation.5 | loop fusion | bytes 2097152 | tf_op jit(solution)/shard_map/slice | solution.py:328
  1.3 2.5 %collective-permute-start = (bf16[1,128,2048]{2,1,0:T(8,128)(2,1)S(1)}, bf16[1,128,2048]{2,1,0:T(8,128)(2,1)S(1)}, u32[]{:S(2)}, u32[]{:S(2)}) collective-permute-start(bf16[1,128,2048]{2,1,0:T(8,128)(2,1)S(1)} %get-tuple-element.90), channel_id=1, source_target_pairs={{0,1},{1,2},{2,3},{3,0},{4,5},{5,6},{6,7},{7,4},{8,9},{9,10},{10,1... | collective-permute-start | bytes 1572872 | tf_op jit(solution)/shard_map/ppermute | solution.py:329
  3.8 2.2 %collective-permute-start.1 = (bf16[1,128,2048]{2,1,0:T(8,128)(2,1)S(1)}, bf16[1,128,2048]{2,1,0:T(8,128)(2,1)S(1)}, u32[]{:S(2)}, u32[]{:S(2)}) collective-permute-start(bf16[1,128,2048]{2,1,0:T(8,128)(2,1)S(1)} %get-tuple-element.89), channel_id=1, source_target_pairs={{0,3},{1,0},{2,1},{3,2},{4,7},{5,4},{6,5},{7,6},{8,11},{9,8},{10,9... | collective-permute-start | bytes 1572872 | tf_op jit(solution)/shard_map/ppermute | solution.py:330
  6.0 0.0 collective-permute-start.16
  6.0 2.7 %collective-permute-start.17 = (bf16[1,128,2048]{2,1,0:T(8,128)(2,1)S(1)}, bf16[1,128,2048]{2,1,0:T(8,128)(2,1)S(1)}, u32[]{:S(2)}, u32[]{:S(2)}) collective-permute-start(bf16[1,128,2048]{2,1,0:T(8,128)(2,1)S(1)} %get-tuple-element.90), channel_id=1, source_target_pairs={{0,3},{1,0},{2,1},{3,2},{4,7},{5,4},{6,5},{7,6},{8,11},{9,8},{10,9... | collective-permute-start | bytes 1572872 | tf_op jit(solution)/shard_map/ppermute | solution.py:332
  8.7 0.1 reshape.16
  8.8 0.0 copy-start
  8.9 6.0 %fold_gain.1.refs_1_.refs_4_.refs_2_ = bf16[2048,1536]{1,0:T(8,128)(2,1)S(1)} custom-call(f32[1,2048]{1,0:T(1,128)S(1)} %bitcast.7, bf16[2048,1536]{1,0:T(8,128)(2,1)} %w_ref.1), custom_call_target="tpu_custom_call" | custom-call | tf_op jit(solution)/shard_map/fold_gain/pallas_call | solution.py:30
  14.9 2.7 %collective-permute-done.refs_0_ = bf16[1,128,2048]{2,1,0:T(8,128)(2,1)S(1)} collective-permute-done((bf16[1,128,2048]{2,1,0:T(8,128)(2,1)S(1)}, bf16[1,128,2048]{2,1,0:T(8,128)(2,1)S(1)}, u32[]{:S(2)}, u32[]{:S(2)}) %collective-permute-start) | collective-permute-done | bytes 524320 | tf_op jit(solution)/shard_map/ppermute | solution.py:329
  17.6 0.0 collective-permute-done.1.refs_3_
  17.6 0.4 collective-permute-start.18
  18.0 0.1 fusion.2
  18.1 1.4 %collective-permute-start.2 = (bf16[1,128,2048]{2,1,0:T(8,128)(2,1)S(1)}, bf16[1,128,2048]{2,1,0:T(8,128)(2,1)S(1)}, u32[]{:S(2)}, u32[]{:S(2)}) collective-permute-start(bf16[1,128,2048]{2,1,0:T(8,128)(2,1)S(1)} %get-tuple-element.88), channel_id=1, source_target_pairs={{0,1},{1,2},{2,3},{3,0},{4,5},{5,6},{6,7},{7,4},{8,9},{9,10},{10,1... | collective-permute-start | bytes 1572872 | tf_op jit(solution)/shard_map/ppermute | solution.py:329
  19.5 1.3 %collective-permute-start.5 = (bf16[1,128,2048]{2,1,0:T(8,128)(2,1)S(1)}, bf16[1,128,2048]{2,1,0:T(8,128)(2,1)S(1)}, u32[]{:S(2)}, u32[]{:S(2)}) collective-permute-start(bf16[1,128,2048]{2,1,0:T(8,128)(2,1)S(1)} %get-tuple-element.87), channel_id=1, source_target_pairs={{0,3},{1,0},{2,1},{3,2},{4,7},{5,4},{6,5},{7,6},{8,11},{9,8},{10,9... | collective-permute-start | bytes 1572872 | tf_op jit(solution)/shard_map/ppermute | solution.py:330
  20.9 0.5 convolution_bitcast_fusion.refs_2_.refs_5_.refs_3_
  21.4 7.4 %collective-permute-done.16.refs_1_ = bf16[1,128,2048]{2,1,0:T(8,128)(2,1)S(1)} collective-permute-done((bf16[1,128,2048]{2,1,0:T(8,128)(2,1)S(1)}, bf16[1,128,2048]{2,1,0:T(8,128)(2,1)S(1)}, u32[]{:S(2)}, u32[]{:S(2)}) %collective-permute-start.16) | collective-permute-done | bytes 524320 | tf_op jit(solution)/shard_map/ppermute | solution.py:331
  28.8 1.2 %collective-permute-start.19 = (bf16[1,128,2048]{2,1,0:T(8,128)(2,1)S(1)}, bf16[1,128,2048]{2,1,0:T(8,128)(2,1)S(1)}, u32[]{:S(2)}, u32[]{:S(2)}) collective-permute-start(bf16[1,128,2048]{2,1,0:T(8,128)(2,1)S(1)} %collective-permute-done.1.refs_3_), channel_id=1, source_target_pairs={{0,3},{1,0},{2,1},{3,2},{4,7},{5,4},{6,5},{7,6},{8,11},{9,8},{10,9... | collective-permute-start | bytes 1572872 | tf_op jit(solution)/shard_map/ppermute | solution.py:336
  30.0 3.3 %project_near.9 = (bf16[1,512,256]{2,1,0:T(8,128)(2,1)S(1)}, f32[1,512,256]{2,1,0:T(8,128)S(1)}, f32[1,4,128,128]{3,2,1,0:T(8,128)S(1)}, f32[1,96,256]{2,1,0:T(8,128)S(1)}) custom-call(bf16[2,256,2048]{2,1,0:T(8,128)(2,1)S(1)} %copy-done, bf16[2048,1536]{1,0:T(8,128)(2,1)S(1)} %fold_gain.1.refs_1_.refs_4_.refs_2_, ...), custom_call_target="tpu_custom_call" | custom-call | flops 1610612736 | bytes 6291456 | tf_op jit(solution)/shard_map/project_near/pallas_call | solution.py:139
  33.4 0.0 collective-permute-done.17.refs_2_
  33.4 0.4 collective-permute-start.3
  33.7 6.3 %collective-permute-done.18.refs_0_ = bf16[1,128,2048]{2,1,0:T(8,128)(2,1)S(1)} collective-permute-done((bf16[1,128,2048]{2,1,0:T(8,128)(2,1)S(1)}, bf16[1,128,2048]{2,1,0:T(8,128)(2,1)S(1)}, u32[]{:S(2)}, u32[]{:S(2)}) %collective-permute-start.18) | collective-permute-done | bytes 524320 | tf_op jit(solution)/shard_map/ppermute | solution.py:335
  40.1 1.2 %collective-permute-start.4 = (bf16[1,128,2048]{2,1,0:T(8,128)(2,1)S(1)}, bf16[1,128,2048]{2,1,0:T(8,128)(2,1)S(1)}, u32[]{:S(2)}, u32[]{:S(2)}) collective-permute-start(bf16[1,128,2048]{2,1,0:T(8,128)(2,1)S(1)} %get-tuple-element.88), channel_id=1, source_target_pairs={{0,3},{1,0},{2,1},{3,2},{4,7},{5,4},{6,5},{7,6},{8,11},{9,8},{10,9... | collective-permute-start | bytes 1572872 | tf_op jit(solution)/shard_map/ppermute | solution.py:332
  41.2 3.3 %project_near.6 = (bf16[1,512,256]{2,1,0:T(8,128)(2,1)S(1)}, f32[1,512,256]{2,1,0:T(8,128)S(1)}, f32[1,4,128,128]{3,2,1,0:T(8,128)S(1)}, f32[1,96,256]{2,1,0:T(8,128)S(1)}) custom-call(bf16[2,256,2048]{2,1,0:T(8,128)(2,1)S(1)} %copy-done, bf16[2048,1536]{1,0:T(8,128)(2,1)S(1)} %fold_gain.1.refs_1_.refs_4_.refs_2_, ...), custom_call_target="tpu_custom_call" | custom-call | flops 1610612736 | bytes 6291456 | tf_op jit(solution)/shard_map/project_near/pallas_call | solution.py:139
  44.6 6.7 %collective-permute-done.2.refs_0_ = bf16[1,128,2048]{2,1,0:T(8,128)(2,1)S(1)} collective-permute-done((bf16[1,128,2048]{2,1,0:T(8,128)(2,1)S(1)}, bf16[1,128,2048]{2,1,0:T(8,128)(2,1)S(1)}, u32[]{:S(2)}, u32[]{:S(2)}) %collective-permute-start.2) | collective-permute-done | bytes 524320 | tf_op jit(solution)/shard_map/ppermute | solution.py:329
  51.3 0.0 collective-permute-start.6
  51.3 0.0 collective-permute-done.5.refs_3_
  51.3 2.7 %collective-permute-start.7 = (bf16[1,128,2048]{2,1,0:T(8,128)(2,1)S(1)}, bf16[1,128,2048]{2,1,0:T(8,128)(2,1)S(1)}, u32[]{:S(2)}, u32[]{:S(2)}) collective-permute-start(bf16[1,128,2048]{2,1,0:T(8,128)(2,1)S(1)} %collective-permute-done.5.refs_3_), channel_id=1, source_target_pairs={{0,3},{1,0},{2,1},{3,2},{4,7},{5,4},{6,5},{7,6},{8,11},{9,8},{10,9... | collective-permute-start | bytes 1572872 | tf_op jit(solution)/shard_map/ppermute | solution.py:336
  54.0 6.2 %project_near.10 = (bf16[2,512,256]{2,1,0:T(8,128)(2,1)S(1)}, f32[2,512,256]{2,1,0:T(8,128)S(1)}, f32[2,4,128,128]{3,2,1,0:T(8,128)S(1)}, f32[2,96,256]{2,1,0:T(8,128)S(1)}) custom-call(bf16[1,128,2048]{2,1,0:T(8,128)(2,1)S(1)} %collective-permute-done.refs_0_, bf16[1,128,2048]{2,1,0:T(8,128)(2,1)S(1)} %collective-permute-done.16.refs_1_, ...), custom_call_target="tpu_custom_call" | custom-call | flops 3221225472 | bytes 6291456 | tf_op jit(solution)/shard_map/project_near/pallas_call | solution.py:139
  60.2 0.0 collective-permute-done.19.refs_1_
  60.2 3.4 %project_near.11 = (bf16[1,512,256]{2,1,0:T(8,128)(2,1)S(1)}, f32[1,512,256]{2,1,0:T(8,128)S(1)}, f32[1,4,128,128]{3,2,1,0:T(8,128)S(1)}, f32[1,96,256]{2,1,0:T(8,128)S(1)}) custom-call(bf16[1,128,2048]{2,1,0:T(8,128)(2,1)S(1)} %collective-permute-done.18.refs_0_, bf16[1,128,2048]{2,1,0:T(8,128)(2,1)S(1)} %collective-permute-done.19.refs_1_, ...), custom_call_target="tpu_custom_call" | custom-call | flops 1610612736 | bytes 6291456 | tf_op jit(solution)/shard_map/project_near/pallas_call | solution.py:139
  63.6 0.1 shard_map.68
  63.6 2.7 %collective-permute-start.20 = (bf16[4,128,128]{2,1,0:T(8,128)(2,1)S(1)}, bf16[4,128,128]{2,1,0:T(8,128)(2,1)S(1)}, u32[]{:S(2)}, u32[]{:S(2)}) collective-permute-start(bf16[4,128,128]{2,1,0:T(8,128)(2,1)S(1)} %get-tuple-element.80), channel_id=1, source_target_pairs={{0,4},{4,0},{8,12},{12,8},{16,20},{20,16},{24,28},{28,24},{32,36},... | collective-permute-start | bytes 393224 | tf_op jit(solution)/shard_map/ppermute | solution.py:301
  66.4 6.2 %project_near.7 = (bf16[2,512,256]{2,1,0:T(8,128)(2,1)S(1)}, f32[2,512,256]{2,1,0:T(8,128)S(1)}, f32[2,4,128,128]{3,2,1,0:T(8,128)S(1)}, f32[2,96,256]{2,1,0:T(8,128)S(1)}) custom-call(bf16[1,128,2048]{2,1,0:T(8,128)(2,1)S(1)} %collective-permute-done.2.refs_0_, bf16[1,128,2048]{2,1,0:T(8,128)(2,1)S(1)} %collective-permute-done.3.refs_1_, ...), custom_call_target="tpu_custom_call" | custom-call | flops 3221225472 | bytes 6291456 | tf_op jit(solution)/shard_map/project_near/pallas_call | solution.py:139
  72.5 0.0 collective-permute-done.20.received_ref.refs_16_
  72.6 1.2 %collective-permute-done.6.refs_0_ = bf16[1,128,2048]{2,1,0:T(8,128)(2,1)S(1)} collective-permute-done((bf16[1,128,2048]{2,1,0:T(8,128)(2,1)S(1)}, bf16[1,128,2048]{2,1,0:T(8,128)(2,1)S(1)}, u32[]{:S(2)}, u32[]{:S(2)}) %collective-permute-start.6) | collective-permute-done | bytes 524320 | tf_op jit(solution)/shard_map/ppermute | solution.py:335
  73.8 0.0 collective-permute-done.7.refs_1_
  73.8 3.3 %project_near.8 = (bf16[1,512,256]{2,1,0:T(8,128)(2,1)S(1)}, f32[1,512,256]{2,1,0:T(8,128)S(1)}, f32[1,4,128,128]{3,2,1,0:T(8,128)S(1)}, f32[1,96,256]{2,1,0:T(8,128)S(1)}) custom-call(bf16[1,128,2048]{2,1,0:T(8,128)(2,1)S(1)} %collective-permute-done.6.refs_0_, bf16[1,128,2048]{2,1,0:T(8,128)(2,1)S(1)} %collective-permute-done.7.refs_1_, ...), custom_call_target="tpu_custom_call" | custom-call | flops 1610612736 | bytes 6291456 | tf_op jit(solution)/shard_map/project_near/pallas_call | solution.py:139
  77.1 0.0 copy-start.2
  77.1 0.1 shard_map.64
  77.2 1.3 %collective-permute-start.8 = (bf16[4,128,128]{2,1,0:T(8,128)(2,1)S(1)}, bf16[4,128,128]{2,1,0:T(8,128)(2,1)S(1)}, u32[]{:S(2)}, u32[]{:S(2)}) collective-permute-start(bf16[4,128,128]{2,1,0:T(8,128)(2,1)S(1)} %get-tuple-element.59), channel_id=1, source_target_pairs={{0,4},{4,0},{8,12},{12,8},{16,20},{20,16},{24,28},{28,24},{32,36},... | collective-permute-start | bytes 393224 | tf_op jit(solution)/shard_map/ppermute | solution.py:301
  78.5 1.2 %collective-permute-start.21 = (bf16[2,128,128]{2,1,0:T(8,128)(2,1)S(1)}, bf16[2,128,128]{2,1,0:T(8,128)(2,1)S(1)}, u32[]{:S(2)}, u32[]{:S(2)}) collective-permute-start(bf16[2,128,128]{2,1,0:T(8,128)(2,1)S(1)} %get-tuple-element.83), channel_id=1, source_target_pairs={{0,8},{4,12},{8,0},{12,4},{16,24},{20,28},{24,16},{28,20},{32,40},... | collective-permute-start | bytes 196616 | tf_op jit(solution)/shard_map/ppermute | solution.py:301
  79.7 2.4 %collective-permute-start.22 = (bf16[2,128,128]{2,1,0:T(8,128)(2,1)S(1)}, bf16[2,128,128]{2,1,0:T(8,128)(2,1)S(1)}, u32[]{:S(2)}, u32[]{:S(2)}) collective-permute-start(bf16[2,128,128]{2,1,0:T(8,128)(2,1)S(1)} %get-tuple-element.83), channel_id=1, source_target_pairs={{0,16},{4,20},{8,24},{12,28},{16,0},{20,4},{24,8},{28,12},{32,48},... | collective-permute-start | bytes 196616 | tf_op jit(solution)/shard_map/ppermute | solution.py:301
  82.2 0.2 collective-permute-start.23
  82.4 0.0 collective-permute-done.21.one_ref
  82.4 3.3 %collective-permute-done.22.two_ref = bf16[2,128,128]{2,1,0:T(8,128)(2,1)S(1)} collective-permute-done((bf16[2,128,128]{2,1,0:T(8,128)(2,1)S(1)}, bf16[2,128,128]{2,1,0:T(8,128)(2,1)S(1)}, u32[]{:S(2)}, u32[]{:S(2)}) %collective-permute-start.22) | collective-permute-done | bytes 65568 | tf_op jit(solution)/shard_map/ppermute | solution.py:301
  85.7 1.0 collective-permute-done.23.three_ref
  86.6 0.1 shard_map.70
  86.7 1.4 %collective-permute-start.24 = (bf16[2,128,128]{2,1,0:T(8,128)(2,1)S(1)}, bf16[2,128,128]{2,1,0:T(8,128)(2,1)S(1)}, u32[]{:S(2)}, u32[]{:S(2)}) collective-permute-start(bf16[2,128,128]{2,1,0:T(8,128)(2,1)S(1)} %get-tuple-element.85), channel_id=1, source_target_pairs={{0,32},{4,36},{8,40},{12,44},{16,48},{20,52},{24,56},{28,60},{32,0... | collective-permute-start | bytes 196616 | tf_op jit(solution)/shard_map/ppermute | solution.py:301
  88.1 2.6 %collective-permute-start.25 = (bf16[2,128,128]{2,1,0:T(8,128)(2,1)S(1)}, bf16[2,128,128]{2,1,0:T(8,128)(2,1)S(1)}, u32[]{:S(2)}, u32[]{:S(2)}) collective-permute-start(bf16[2,128,128]{2,1,0:T(8,128)(2,1)S(1)} %get-tuple-element.85), channel_id=1, source_target_pairs={{0,64},{4,68},{8,72},{12,76},{16,80},{20,84},{24,88},{28,92},{32,9... | collective-permute-start | bytes 196616 | tf_op jit(solution)/shard_map/ppermute | solution.py:301
  90.7 0.0 collective-permute-start.26
  90.7 0.0 collective-permute-done.8.received_ref.refs_16_
  90.7 0.3 collective-permute-start.10
  91.0 2.5 %collective-permute-start.11 = (bf16[2,128,128]{2,1,0:T(8,128)(2,1)S(1)}, bf16[2,128,128]{2,1,0:T(8,128)(2,1)S(1)}, u32[]{:S(2)}, u32[]{:S(2)}) collective-permute-start(bf16[2,128,128]{2,1,0:T(8,128)(2,1)S(1)} %get-tuple-element.62), channel_id=1, source_target_pairs={{0,24},{4,28},{8,16},{12,20},{16,8},{20,12},{24,0},{28,4},{32,56},... | collective-permute-start | bytes 196616 | tf_op jit(solution)/shard_map/ppermute | solution.py:301
  93.6 2.2 %collective-permute-done.26.three_ref = bf16[2,128,128]{2,1,0:T(8,128)(2,1)S(1)} collective-permute-done((bf16[2,128,128]{2,1,0:T(8,128)(2,1)S(1)}, bf16[2,128,128]{2,1,0:T(8,128)(2,1)S(1)}, u32[]{:S(2)}, u32[]{:S(2)}) %collective-permute-start.26) | collective-permute-done | bytes 65568 | tf_op jit(solution)/shard_map/ppermute | solution.py:301
  95.8 2.8 %collective-permute-start.27 = (bf16[4,2,128,128]{3,2,1,0:T(8,128)(2,1)S(1)}, bf16[4,2,128,128]{3,2,1,0:T(8,128)(2,1)S(1)}, u32[]{:S(2)}, u32[]{:S(2)}) collective-permute-start(bf16[4,2,128,128]{3,2,1,0:T(8,128)(2,1)S(1)} %shard_map.71.refs_17_), channel_id=1, source_target_pairs={{0,4},{4,0},{8,12},{12,8},{16,20},{20,16},{24,28},{28,24},{32,36},... | collective-permute-start | bytes 786440 | tf_op jit(solution)/shard_map/ppermute | solution.py:301
  98.6 0.1 shard_map.66
  98.6 0.1 collective-permute-start.12
  98.7 2.9 %collective-permute-start.13 = (bf16[2,128,128]{2,1,0:T(8,128)(2,1)S(1)}, bf16[2,128,128]{2,1,0:T(8,128)(2,1)S(1)}, u32[]{:S(2)}, u32[]{:S(2)}) collective-permute-start(bf16[2,128,128]{2,1,0:T(8,128)(2,1)S(1)} %get-tuple-element.64), channel_id=1, source_target_pairs={{0,64},{4,68},{8,72},{12,76},{16,80},{20,84},{24,88},{28,92},{32,9... | collective-permute-start | bytes 196616 | tf_op jit(solution)/shard_map/ppermute | solution.py:301
  101.7 0.9 collective-permute-start.14
  102.6 1.4 %collective-permute-done.13.two_ref = bf16[2,128,128]{2,1,0:T(8,128)(2,1)S(1)} collective-permute-done((bf16[2,128,128]{2,1,0:T(8,128)(2,1)S(1)}, bf16[2,128,128]{2,1,0:T(8,128)(2,1)S(1)}, u32[]{:S(2)}, u32[]{:S(2)}) %collective-permute-start.13) | collective-permute-done | bytes 65568 | tf_op jit(solution)/shard_map/ppermute | solution.py:301
  104.0 2.0 %collective-permute-done.14.three_ref = bf16[2,128,128]{2,1,0:T(8,128)(2,1)S(1)} collective-permute-done((bf16[2,128,128]{2,1,0:T(8,128)(2,1)S(1)}, bf16[2,128,128]{2,1,0:T(8,128)(2,1)S(1)}, u32[]{:S(2)}, u32[]{:S(2)}) %collective-permute-start.14) | collective-permute-done | bytes 65568 | tf_op jit(solution)/shard_map/ppermute | solution.py:301
  106.0 4.1 %collective-permute-start.15 = (bf16[4,2,128,128]{3,2,1,0:T(8,128)(2,1)S(1)}, bf16[4,2,128,128]{3,2,1,0:T(8,128)(2,1)S(1)}, u32[]{:S(2)}, u32[]{:S(2)}) collective-permute-start(bf16[4,2,128,128]{3,2,1,0:T(8,128)(2,1)S(1)} %shard_map.67.refs_17_), channel_id=1, source_target_pairs={{0,4},{4,0},{8,12},{12,8},{16,20},{20,16},{24,28},{28,24},{32,36},... | collective-permute-start | bytes 786440 | tf_op jit(solution)/shard_map/ppermute | solution.py:301
  110.1 3.9 %far_part.2.refs_19_ = bf16[2,4,256,512]{3,2,1,0:T(8,128)(2,1)} custom-call(s32[2]{0:T(128)S(1)} %copy-done.2, bf16[1,512,256]{2,1,0:T(8,128)(2,1)S(1)} %get-tuple-element.66.refs_0_, bf16[2,512,256]{2,1,0:T(8,128)(2,1)S(1)} %get-tuple-element.69.refs_1_.refs_2_, bf16[2,512,256]{2,1,0:T(8,128)(2,1)S(1)} %get-tuple-element.69.refs_1_.refs_2_, ...), custom_call_target="tpu_custom_call" | custom-call | flops 939524096 | bytes 5242880 | tf_op jit(solution)/shard_map/far_part/pallas_call | solution.py:230
  114.0 3.9 %far_part.3 = bf16[2,4,256,512]{3,2,1,0:T(8,128)(2,1)} custom-call(s32[2]{0:T(128)S(1)} %copy-done.2, bf16[1,512,256]{2,1,0:T(8,128)(2,1)S(1)} %get-tuple-element.46.refs_0_, bf16[2,512,256]{2,1,0:T(8,128)(2,1)S(1)} %get-tuple-element.48.refs_1_.refs_2_, bf16[2,512,256]{2,1,0:T(8,128)(2,1)S(1)} %get-tuple-element.48.refs_1_.refs_2_, ...), custom_call_target="tpu_custom_call", output_to_operand_aliasing={{}: (20, {})} | custom-call | flops 939524096 | bytes 5242880 | tf_op jit(solution)/shard_map/far_part/pallas_call | solution.py:230
  (25 shorter events, 0.2 us)
Async XLA Ops:
  0.0 8.7 %copy-start.3 = (f32[16,4,18]{2,1,0:T(4,128)S(1)}, f32[16,4,18]{2,1,0:T(4,128)}, u32[]{:S(2)}) copy-start(f32[16,4,18]{2,1,0:T(4,128)} %param.9) | copy-start | bytes 13828
  0.0 8.8 %copy-start.4 = (s32[2,1024]{1,0:T(2,128)S(1)}, s32[2,1024]{1,0:T(2,128)}, u32[]{:S(2)}) copy-start(s32[2,1024]{1,0:T(2,128)} %param.10) | copy-start | bytes 24580
  0.0 8.8 %copy-start.1 = (f32[2048]{0:T(1024)S(1)}, f32[2048]{0:T(1024)}, u32[]{:S(2)}) copy-start(f32[2048]{0:T(1024)} %param.7) | copy-start | bytes 24580
  1.3 16.3 %collective-permute-start = (bf16[1,128,2048]{2,1,0:T(8,128)(2,1)S(1)}, bf16[1,128,2048]{2,1,0:T(8,128)(2,1)S(1)}, u32[]{:S(2)}, u32[]{:S(2)}) collective-permute-start(bf16[1,128,2048]{2,1,0:T(8,128)(2,1)S(1)} %get-tuple-element.90), channel_id=1, source_target_pairs={{0,1},{1,2},{2,3},{3,0},{4,5},{5,6},{6,7},{7,4},{8,9},{9,10},{10,1... | collective-permute-start | bytes 1572872 | tf_op jit(solution)/shard_map/ppermute | solution.py:329
  3.8 13.8 %collective-permute-start.1 = (bf16[1,128,2048]{2,1,0:T(8,128)(2,1)S(1)}, bf16[1,128,2048]{2,1,0:T(8,128)(2,1)S(1)}, u32[]{:S(2)}, u32[]{:S(2)}) collective-permute-start(bf16[1,128,2048]{2,1,0:T(8,128)(2,1)S(1)} %get-tuple-element.89), channel_id=1, source_target_pairs={{0,3},{1,0},{2,1},{3,2},{4,7},{5,4},{6,5},{7,6},{8,11},{9,8},{10,9... | collective-permute-start | bytes 1572872 | tf_op jit(solution)/shard_map/ppermute | solution.py:330
  6.0 22.8 %collective-permute-start.16 = (bf16[1,128,2048]{2,1,0:T(8,128)(2,1)S(1)}, bf16[1,128,2048]{2,1,0:T(8,128)(2,1)S(1)}, u32[]{:S(2)}, u32[]{:S(2)}) collective-permute-start(bf16[1,128,2048]{2,1,0:T(8,128)(2,1)S(1)} %get-tuple-element.89), channel_id=1, source_target_pairs={{0,1},{1,2},{2,3},{3,0},{4,5},{5,6},{6,7},{7,4},{8,9},{9,10},{10,1... | collective-permute-start | bytes 1572872 | tf_op jit(solution)/shard_map/ppermute | solution.py:331
  6.0 27.3 %collective-permute-start.17 = (bf16[1,128,2048]{2,1,0:T(8,128)(2,1)S(1)}, bf16[1,128,2048]{2,1,0:T(8,128)(2,1)S(1)}, u32[]{:S(2)}, u32[]{:S(2)}) collective-permute-start(bf16[1,128,2048]{2,1,0:T(8,128)(2,1)S(1)} %get-tuple-element.90), channel_id=1, source_target_pairs={{0,3},{1,0},{2,1},{3,2},{4,7},{5,4},{6,5},{7,6},{8,11},{9,8},{10,9... | collective-permute-start | bytes 1572872 | tf_op jit(solution)/shard_map/ppermute | solution.py:332
  8.8 9.2 %copy-start = (bf16[2,256,2048]{2,1,0:T(8,128)(2,1)S(1)}, bf16[2,256,2048]{2,1,0:T(8,128)(2,1)}, u32[]{:S(2)}) copy-start(bf16[2,256,2048]{2,1,0:T(8,128)(2,1)} %refs_0_.3) | copy-start | bytes 6291460
  17.6 22.5 %collective-permute-start.18 = (bf16[1,128,2048]{2,1,0:T(8,128)(2,1)S(1)}, bf16[1,128,2048]{2,1,0:T(8,128)(2,1)S(1)}, u32[]{:S(2)}, u32[]{:S(2)}) collective-permute-start(bf16[1,128,2048]{2,1,0:T(8,128)(2,1)S(1)} %collective-permute-done.refs_0_), channel_id=1, source_target_pairs={{0,1},{1,2},{2,3},{3,0},{4,5},{5,6},{6,7},{7,4},{8,9},{9,10},{10,1... | collective-permute-start | bytes 1572872 | tf_op jit(solution)/shard_map/ppermute | solution.py:335
  18.1 33.2 %collective-permute-start.2 = (bf16[1,128,2048]{2,1,0:T(8,128)(2,1)S(1)}, bf16[1,128,2048]{2,1,0:T(8,128)(2,1)S(1)}, u32[]{:S(2)}, u32[]{:S(2)}) collective-permute-start(bf16[1,128,2048]{2,1,0:T(8,128)(2,1)S(1)} %get-tuple-element.88), channel_id=1, source_target_pairs={{0,1},{1,2},{2,3},{3,0},{4,5},{5,6},{6,7},{7,4},{8,9},{9,10},{10,1... | collective-permute-start | bytes 1572872 | tf_op jit(solution)/shard_map/ppermute | solution.py:329
  19.5 31.8 %collective-permute-start.5 = (bf16[1,128,2048]{2,1,0:T(8,128)(2,1)S(1)}, bf16[1,128,2048]{2,1,0:T(8,128)(2,1)S(1)}, u32[]{:S(2)}, u32[]{:S(2)}) collective-permute-start(bf16[1,128,2048]{2,1,0:T(8,128)(2,1)S(1)} %get-tuple-element.87), channel_id=1, source_target_pairs={{0,3},{1,0},{2,1},{3,2},{4,7},{5,4},{6,5},{7,6},{8,11},{9,8},{10,9... | collective-permute-start | bytes 1572872 | tf_op jit(solution)/shard_map/ppermute | solution.py:330
  28.8 31.3 %collective-permute-start.19 = (bf16[1,128,2048]{2,1,0:T(8,128)(2,1)S(1)}, bf16[1,128,2048]{2,1,0:T(8,128)(2,1)S(1)}, u32[]{:S(2)}, u32[]{:S(2)}) collective-permute-start(bf16[1,128,2048]{2,1,0:T(8,128)(2,1)S(1)} %collective-permute-done.1.refs_3_), channel_id=1, source_target_pairs={{0,3},{1,0},{2,1},{3,2},{4,7},{5,4},{6,5},{7,6},{8,11},{9,8},{10,9... | collective-permute-start | bytes 1572872 | tf_op jit(solution)/shard_map/ppermute | solution.py:336
  33.4 33.0 %collective-permute-start.3 = (bf16[1,128,2048]{2,1,0:T(8,128)(2,1)S(1)}, bf16[1,128,2048]{2,1,0:T(8,128)(2,1)S(1)}, u32[]{:S(2)}, u32[]{:S(2)}) collective-permute-start(bf16[1,128,2048]{2,1,0:T(8,128)(2,1)S(1)} %get-tuple-element.87), channel_id=1, source_target_pairs={{0,1},{1,2},{2,3},{3,0},{4,5},{5,6},{6,7},{7,4},{8,9},{9,10},{10,1... | collective-permute-start | bytes 1572872 | tf_op jit(solution)/shard_map/ppermute | solution.py:331
  40.1 26.3 %collective-permute-start.4 = (bf16[1,128,2048]{2,1,0:T(8,128)(2,1)S(1)}, bf16[1,128,2048]{2,1,0:T(8,128)(2,1)S(1)}, u32[]{:S(2)}, u32[]{:S(2)}) collective-permute-start(bf16[1,128,2048]{2,1,0:T(8,128)(2,1)S(1)} %get-tuple-element.88), channel_id=1, source_target_pairs={{0,3},{1,0},{2,1},{3,2},{4,7},{5,4},{6,5},{7,6},{8,11},{9,8},{10,9... | collective-permute-start | bytes 1572872 | tf_op jit(solution)/shard_map/ppermute | solution.py:332
  51.3 22.5 %collective-permute-start.6 = (bf16[1,128,2048]{2,1,0:T(8,128)(2,1)S(1)}, bf16[1,128,2048]{2,1,0:T(8,128)(2,1)S(1)}, u32[]{:S(2)}, u32[]{:S(2)}) collective-permute-start(bf16[1,128,2048]{2,1,0:T(8,128)(2,1)S(1)} %collective-permute-done.2.refs_0_), channel_id=1, source_target_pairs={{0,1},{1,2},{2,3},{3,0},{4,5},{5,6},{6,7},{7,4},{8,9},{9,10},{10,1... | collective-permute-start | bytes 1572872 | tf_op jit(solution)/shard_map/ppermute | solution.py:335
  51.3 22.5 %collective-permute-start.7 = (bf16[1,128,2048]{2,1,0:T(8,128)(2,1)S(1)}, bf16[1,128,2048]{2,1,0:T(8,128)(2,1)S(1)}, u32[]{:S(2)}, u32[]{:S(2)}) collective-permute-start(bf16[1,128,2048]{2,1,0:T(8,128)(2,1)S(1)} %collective-permute-done.5.refs_3_), channel_id=1, source_target_pairs={{0,3},{1,0},{2,1},{3,2},{4,7},{5,4},{6,5},{7,6},{8,11},{9,8},{10,9... | collective-permute-start | bytes 1572872 | tf_op jit(solution)/shard_map/ppermute | solution.py:336
  63.6 8.9 %collective-permute-start.20 = (bf16[4,128,128]{2,1,0:T(8,128)(2,1)S(1)}, bf16[4,128,128]{2,1,0:T(8,128)(2,1)S(1)}, u32[]{:S(2)}, u32[]{:S(2)}) collective-permute-start(bf16[4,128,128]{2,1,0:T(8,128)(2,1)S(1)} %get-tuple-element.80), channel_id=1, source_target_pairs={{0,4},{4,0},{8,12},{12,8},{16,20},{20,16},{24,28},{28,24},{32,36},... | collective-permute-start | bytes 393224 | tf_op jit(solution)/shard_map/ppermute | solution.py:301
  77.1 33.0 %copy-start.2 = (s32[2]{0:T(128)S(1)}, s32[2]{0:T(128)}, u32[]{:S(2)}) copy-start(s32[2]{0:T(128)} %lengths_ref.3) | copy-start | bytes 28
  77.2 13.5 %collective-permute-start.8 = (bf16[4,128,128]{2,1,0:T(8,128)(2,1)S(1)}, bf16[4,128,128]{2,1,0:T(8,128)(2,1)S(1)}, u32[]{:S(2)}, u32[]{:S(2)}) collective-permute-start(bf16[4,128,128]{2,1,0:T(8,128)(2,1)S(1)} %get-tuple-element.59), channel_id=1, source_target_pairs={{0,4},{4,0},{8,12},{12,8},{16,20},{20,16},{24,28},{28,24},{32,36},... | collective-permute-start | bytes 393224 | tf_op jit(solution)/shard_map/ppermute | solution.py:301
  78.5 3.9 %collective-permute-start.21 = (bf16[2,128,128]{2,1,0:T(8,128)(2,1)S(1)}, bf16[2,128,128]{2,1,0:T(8,128)(2,1)S(1)}, u32[]{:S(2)}, u32[]{:S(2)}) collective-permute-start(bf16[2,128,128]{2,1,0:T(8,128)(2,1)S(1)} %get-tuple-element.83), channel_id=1, source_target_pairs={{0,8},{4,12},{8,0},{12,4},{16,24},{20,28},{24,16},{28,20},{32,40},... | collective-permute-start | bytes 196616 | tf_op jit(solution)/shard_map/ppermute | solution.py:301
  79.7 5.9 %collective-permute-start.22 = (bf16[2,128,128]{2,1,0:T(8,128)(2,1)S(1)}, bf16[2,128,128]{2,1,0:T(8,128)(2,1)S(1)}, u32[]{:S(2)}, u32[]{:S(2)}) collective-permute-start(bf16[2,128,128]{2,1,0:T(8,128)(2,1)S(1)} %get-tuple-element.83), channel_id=1, source_target_pairs={{0,16},{4,20},{8,24},{12,28},{16,0},{20,4},{24,8},{28,12},{32,48},... | collective-permute-start | bytes 196616 | tf_op jit(solution)/shard_map/ppermute | solution.py:301
  82.2 4.5 %collective-permute-start.23 = (bf16[2,128,128]{2,1,0:T(8,128)(2,1)S(1)}, bf16[2,128,128]{2,1,0:T(8,128)(2,1)S(1)}, u32[]{:S(2)}, u32[]{:S(2)}) collective-permute-start(bf16[2,128,128]{2,1,0:T(8,128)(2,1)S(1)} %get-tuple-element.83), channel_id=1, source_target_pairs={{0,24},{4,28},{8,16},{12,20},{16,8},{20,12},{24,0},{28,4},{32,56},... | collective-permute-start | bytes 196616 | tf_op jit(solution)/shard_map/ppermute | solution.py:301
  86.7 6.9 %collective-permute-start.24 = (bf16[2,128,128]{2,1,0:T(8,128)(2,1)S(1)}, bf16[2,128,128]{2,1,0:T(8,128)(2,1)S(1)}, u32[]{:S(2)}, u32[]{:S(2)}) collective-permute-start(bf16[2,128,128]{2,1,0:T(8,128)(2,1)S(1)} %get-tuple-element.85), channel_id=1, source_target_pairs={{0,32},{4,36},{8,40},{12,44},{16,48},{20,52},{24,56},{28,60},{32,0... | collective-permute-start | bytes 196616 | tf_op jit(solution)/shard_map/ppermute | solution.py:301
  88.1 5.5 %collective-permute-start.25 = (bf16[2,128,128]{2,1,0:T(8,128)(2,1)S(1)}, bf16[2,128,128]{2,1,0:T(8,128)(2,1)S(1)}, u32[]{:S(2)}, u32[]{:S(2)}) collective-permute-start(bf16[2,128,128]{2,1,0:T(8,128)(2,1)S(1)} %get-tuple-element.85), channel_id=1, source_target_pairs={{0,64},{4,68},{8,72},{12,76},{16,80},{20,84},{24,88},{28,92},{32,9... | collective-permute-start | bytes 196616 | tf_op jit(solution)/shard_map/ppermute | solution.py:301
  90.7 5.0 %collective-permute-start.26 = (bf16[2,128,128]{2,1,0:T(8,128)(2,1)S(1)}, bf16[2,128,128]{2,1,0:T(8,128)(2,1)S(1)}, u32[]{:S(2)}, u32[]{:S(2)}) collective-permute-start(bf16[2,128,128]{2,1,0:T(8,128)(2,1)S(1)} %get-tuple-element.85), channel_id=1, source_target_pairs={{0,96},{4,100},{8,104},{12,108},{16,112},{20,116},{24,120},{28,124... | collective-permute-start | bytes 196616 | tf_op jit(solution)/shard_map/ppermute | solution.py:301
  90.7 7.8 %collective-permute-start.10 = (bf16[2,128,128]{2,1,0:T(8,128)(2,1)S(1)}, bf16[2,128,128]{2,1,0:T(8,128)(2,1)S(1)}, u32[]{:S(2)}, u32[]{:S(2)}) collective-permute-start(bf16[2,128,128]{2,1,0:T(8,128)(2,1)S(1)} %get-tuple-element.62), channel_id=1, source_target_pairs={{0,16},{4,20},{8,24},{12,28},{16,0},{20,4},{24,8},{28,12},{32,48},... | collective-permute-start | bytes 196616 | tf_op jit(solution)/shard_map/ppermute | solution.py:301
  91.0 7.5 %collective-permute-start.11 = (bf16[2,128,128]{2,1,0:T(8,128)(2,1)S(1)}, bf16[2,128,128]{2,1,0:T(8,128)(2,1)S(1)}, u32[]{:S(2)}, u32[]{:S(2)}) collective-permute-start(bf16[2,128,128]{2,1,0:T(8,128)(2,1)S(1)} %get-tuple-element.62), channel_id=1, source_target_pairs={{0,24},{4,28},{8,16},{12,20},{16,8},{20,12},{24,0},{28,4},{32,56},... | collective-permute-start | bytes 196616 | tf_op jit(solution)/shard_map/ppermute | solution.py:301
  93.6 5.0 %collective-permute-start.9 = (bf16[2,128,128]{2,1,0:T(8,128)(2,1)S(1)}, bf16[2,128,128]{2,1,0:T(8,128)(2,1)S(1)}, u32[]{:S(2)}, u32[]{:S(2)}) collective-permute-start(bf16[2,128,128]{2,1,0:T(8,128)(2,1)S(1)} %get-tuple-element.62), channel_id=1, source_target_pairs={{0,8},{4,12},{8,0},{12,4},{16,24},{20,28},{24,16},{28,20},{32,40},... | collective-permute-start | bytes 196616 | tf_op jit(solution)/shard_map/ppermute | solution.py:301
  95.8 14.3 %collective-permute-start.27 = (bf16[4,2,128,128]{3,2,1,0:T(8,128)(2,1)S(1)}, bf16[4,2,128,128]{3,2,1,0:T(8,128)(2,1)S(1)}, u32[]{:S(2)}, u32[]{:S(2)}) collective-permute-start(bf16[4,2,128,128]{3,2,1,0:T(8,128)(2,1)S(1)} %shard_map.71.refs_17_), channel_id=1, source_target_pairs={{0,4},{4,0},{8,12},{12,8},{16,20},{20,16},{24,28},{28,24},{32,36},... | collective-permute-start | bytes 786440 | tf_op jit(solution)/shard_map/ppermute | solution.py:301
  98.6 3.9 %collective-permute-start.12 = (bf16[2,128,128]{2,1,0:T(8,128)(2,1)S(1)}, bf16[2,128,128]{2,1,0:T(8,128)(2,1)S(1)}, u32[]{:S(2)}, u32[]{:S(2)}) collective-permute-start(bf16[2,128,128]{2,1,0:T(8,128)(2,1)S(1)} %get-tuple-element.64), channel_id=1, source_target_pairs={{0,32},{4,36},{8,40},{12,44},{16,48},{20,52},{24,56},{28,60},{32,0... | collective-permute-start | bytes 196616 | tf_op jit(solution)/shard_map/ppermute | solution.py:301
  98.7 5.3 %collective-permute-start.13 = (bf16[2,128,128]{2,1,0:T(8,128)(2,1)S(1)}, bf16[2,128,128]{2,1,0:T(8,128)(2,1)S(1)}, u32[]{:S(2)}, u32[]{:S(2)}) collective-permute-start(bf16[2,128,128]{2,1,0:T(8,128)(2,1)S(1)} %get-tuple-element.64), channel_id=1, source_target_pairs={{0,64},{4,68},{8,72},{12,76},{16,80},{20,84},{24,88},{28,92},{32,9... | collective-permute-start | bytes 196616 | tf_op jit(solution)/shard_map/ppermute | solution.py:301
  101.7 4.3 %collective-permute-start.14 = (bf16[2,128,128]{2,1,0:T(8,128)(2,1)S(1)}, bf16[2,128,128]{2,1,0:T(8,128)(2,1)S(1)}, u32[]{:S(2)}, u32[]{:S(2)}) collective-permute-start(bf16[2,128,128]{2,1,0:T(8,128)(2,1)S(1)} %get-tuple-element.64), channel_id=1, source_target_pairs={{0,96},{4,100},{8,104},{12,108},{16,112},{20,116},{24,120},{28,124... | collective-permute-start | bytes 196616 | tf_op jit(solution)/shard_map/ppermute | solution.py:301
  106.0 8.0 %collective-permute-start.15 = (bf16[4,2,128,128]{3,2,1,0:T(8,128)(2,1)S(1)}, bf16[4,2,128,128]{3,2,1,0:T(8,128)(2,1)S(1)}, u32[]{:S(2)}, u32[]{:S(2)}) collective-permute-start(bf16[4,2,128,128]{3,2,1,0:T(8,128)(2,1)S(1)} %shard_map.67.refs_17_), channel_id=1, source_target_pairs={{0,4},{4,0},{8,12},{12,8},{16,20},{20,16},{24,28},{28,24},{32,36},... | collective-permute-start | bytes 786440 | tf_op jit(solution)/shard_map/ppermute | solution.py:301

commit v2 on v1

v2 whole, which is shorter than its diff:
```python
import jax
import jax.numpy as jnp
from jax import lax
from jax.experimental import pallas as pl
from jax.experimental.pallas import tpu as pltpu
from jax.sharding import PartitionSpec as P


TILE = 128
ROWS = 2 * TILE
F32 = jnp.float32
BF16 = jnp.bfloat16
NT = (((1,), (1,)), ((), ()))


def in_vmem(value):
    return pltpu.with_memory_space_constraint(value, pltpu.VMEM)


def fold_kernel(gain_ref, w_ref, out_ref):
    heads = w_ref.shape[1] // (3 * TILE)
    for at in range(0, w_ref.shape[0], TILE):
        column = jnp.broadcast_to(gain_ref[:, at : at + TILE], (TILE, TILE)).T
        for lane in range(0, w_ref.shape[1], TILE):
            part = w_ref[at : at + TILE, lane : lane + TILE].astype(F32) * column
            head, which = divmod(lane // TILE, 3)
            to = head * TILE if which == 0 else heads * TILE + head * 2 * TILE + (which - 1) * TILE
            out_ref[at : at + TILE, to : to + TILE] = part.astype(BF16)


def fold_gain(gain, projection):
    width, cols = projection.shape
    return pl.pallas_call(
        fold_kernel,
        grid=(width // ROWS,),
        in_specs=[
            pl.BlockSpec((1, ROWS), lambda i: (0, i)),
            pl.BlockSpec((ROWS, cols), lambda i: (i, 0)),
        ],
        out_specs=pl.BlockSpec((ROWS, cols), lambda i: (i, 0)),
        out_shape=pltpu.VMEM((width, cols), BF16),
        compiler_params=pltpu.CompilerParams(vmem_limit_bytes=8 << 20),
        name="fold_gain",
    )(gain.reshape(1, width), pltpu.with_memory_space_constraint(projection, pltpu.HBM))


def place_of(relative):
    return (lax.axis_index("head") + (0, 3, 1, 2)[relative]) % 4


def row_scales(xs, pick, scales):
    sums = []
    for x_ref in xs:
        total = jnp.zeros((x_ref.shape[1], TILE), F32)
        for lane in range(0, x_ref.shape[2], TILE):
            part = x_ref[pick, :, lane : lane + TILE].astype(F32)
            total = total + part * part
        sums.append(total)
    sums = jnp.concatenate(sums, axis=0)
    ones = jnp.full((8, TILE), 1.0, F32)
    for c in range(scales.shape[0]):
        mean = lax.dot_general(
            ones,
            sums[c * ROWS : (c + 1) * ROWS],
            NT,
            precision=lax.Precision.HIGHEST,
            preferred_element_type=F32,
        ) * (1.0 / xs[0].shape[2])
        scales[c] = lax.rsqrt(mean + 1e-06)


def columns(w_ref, start, count):
    return w_ref[:, pl.ds(pl.multiple_of(start, TILE), count)]


def split_keys(kv, scale, rows, hh):
    at = hh * 256
    k = kv[rows, at : at + 128].astype(BF16)
    v = (kv[rows, at + 128 : at + 256].T * (scale * scale)).astype(BF16)
    return k, v


def near_parts(q, k, v, wt_out, near_ref, step, heads_step):
    source = lax.broadcasted_iota(jnp.int32, (TILE, TILE), 0)
    target = lax.broadcasted_iota(jnp.int32, (TILE, TILE), 1)
    differ = jnp.bitwise_xor(source, target)
    causal = source <= target
    zeros = jnp.zeros((TILE, TILE), BF16)
    scores = {i: jnp.dot(k[i], q[i], preferred_element_type=F32) for i in q}
    for c, hh in q:
        head = step * heads_step + hh
        blocks = []
        for t in range(2):
            lanes = slice(t * TILE, (t + 1) * TILE)
            grid = wt_out[c, head, 0:1, lanes]
            for level in range(1, 8):
                row = wt_out[c, head, level : level + 1, lanes]
                grid = jnp.where(differ >= 1 << (level - 1), row, grid)
            grid = jnp.where(causal, grid, 0.0)
            blocks.append((scores[c, hh][lanes, lanes] * grid).astype(BF16))
        row = wt_out[c, head, 8:9, TILE:]
        cross = (scores[c, hh][:TILE, TILE:] * row).astype(BF16)
        weighted = jnp.concatenate(
            [
                jnp.concatenate([blocks[0], cross], axis=1),
                jnp.concatenate([zeros, blocks[1]], axis=1),
            ],
            axis=0,
        )
        near = jnp.dot(v[c, hh], weighted, preferred_element_type=F32)
        near_ref[c, pl.ds(head * 128, 128), :] = near


def project_kernel(count, relatives, seq, pick, heads_step, heads):
    chunks = len(relatives)

    def body(*refs):
        xs = refs[:count]
        w_ref, wt_ref = refs[count : count + 2]
        q_ref, near_ref, state_ref, wt_out, held, scales = refs[count + 2 :]
        step = pl.program_id(0)

        @pl.when(step == 0)
        def _():
            at = 0
            for x_ref in xs:
                held[pl.ds(at, x_ref.shape[1]), :] = x_ref[pick]
                at += x_ref.shape[1]
            row_scales(xs, pick, scales)

        x = held[...]
        queries = jnp.dot(
            x, columns(w_ref, step * (heads_step * 128), heads_step * 128), preferred_element_type=F32
        )
        kv = jnp.dot(
            x,
            columns(w_ref, heads * 128 + step * (heads_step * 256), heads_step * 256),
            preferred_element_type=F32,
        )
        q, k, v = {}, {}, {}
        for c in range(chunks):
            scale = scales[c, 0:1, :]
            heads_now = pl.ds(step * heads_step, heads_step)
            wt_out[c, heads_now] = wt_ref[seq, place_of(relatives[c]), heads_now] * scale
            rows = slice(c * ROWS, (c + 1) * ROWS)
            for hh in range(heads_step):
                head = step * heads_step + hh
                q[c, hh] = queries[rows, hh * 128 : (hh + 1) * 128].T.astype(BF16)
                k[c, hh], v[c, hh] = split_keys(kv, scale, rows, hh)
                q_ref[c, pl.ds(head * 128, 128), :] = q[c, hh]
        for c, hh in q:
            state_ref[c, step * heads_step + hh] = jnp.dot(
                v[c, hh], k[c, hh], preferred_element_type=F32
            )
        near_parts(q, k, v, wt_out, near_ref, step, heads_step)

    return body


def keys_kernel(count, relative, seq, heads):
    def body(*refs):
        xs = refs[:count]
        w_ref, wt_ref = refs[count : count + 2]
        state_ref, k_ref, v_ref, wt_out, held, scales = refs[count + 2 :]
        at = 0
        for x_ref in xs:
            held[pl.ds(at, x_ref.shape[1]), :] = x_ref[0]
            at += x_ref.shape[1]
        kv = jnp.dot(
            held[...], w_ref[:, heads * 128 : heads * 384], preferred_element_type=F32
        )
        row_scales(xs, 0, scales)
        scale = scales[0, 0:1, :]
        wt_out[0] = wt_ref[seq, place_of(relative)] * scale
        for head in range(heads):
            k, v = split_keys(kv, scale, slice(0, ROWS), head)
            k_ref[head] = k
            v_ref[head] = v
            state_ref[0, head] = jnp.dot(v, k, preferred_element_type=F32)

    return body


def queries_kernel(heads_step):
    def body(held, w_ref, k_ref, v_ref, wt_out, q_ref, near_ref):
        step = pl.program_id(0)
        queries = jnp.dot(
            held[...],
            columns(w_ref, step * (heads_step * 128), heads_step * 128),
            preferred_element_type=F32,
        )
        q, k, v = {}, {}, {}
        for hh in range(heads_step):
            head = step * heads_step + hh
            q[0, hh] = queries[:, hh * 128 : (hh + 1) * 128].T.astype(BF16)
            q_ref[0, pl.ds(head * 128, 128), :] = q[0, hh]
            k[0, hh], v[0, hh] = k_ref[head], v_ref[head]
        near_parts(q, k, v, wt_out, near_ref, step, heads_step)

    return body


def vmem_call(body, steps, args, outs, scratch=(), limit=16):
    return pl.pallas_call(
        body,
        grid=(steps,),
        in_specs=[pl.BlockSpec(memory_space=pltpu.VMEM)] * len(args),
        out_specs=[pl.BlockSpec(memory_space=pltpu.VMEM)] * len(outs),
        out_shape=[pltpu.VMEM(shape, dtype) for shape, dtype in outs],
        scratch_shapes=list(scratch),
        compiler_params=pltpu.CompilerParams(vmem_limit_bytes=limit << 20),
    )(*args)


def project(xs, seq, relatives, weight, wt, pick=0, states_first=False):
    chunks = len(relatives)
    width, cols = weight.shape
    heads = cols // 384
    heads_step = 2 if heads % 2 == 0 else 1
    steps = heads // heads_step
    weight = in_vmem(weight)
    levels = (chunks, heads, wt.shape[3], ROWS)
    queries, states = (chunks, heads * 128, ROWS), (chunks, heads, 128, 128)
    held, scales = ((chunks * ROWS, width), BF16), pltpu.VMEM((chunks, 8, ROWS), F32)
    if states_first:
        state, k, v, scaled, held = vmem_call(
            keys_kernel(len(xs), relatives[0], seq, heads),
            1,
            [*xs, weight, wt],
            [
                (states, F32),
                ((heads, ROWS, 128), BF16),
                ((heads, 128, ROWS), BF16),
                (levels, F32),
                held,
            ],
            [scales],
        )
        q, near = vmem_call(
            queries_kernel(heads_step),
            steps,
            [in_vmem(held), weight, in_vmem(k), in_vmem(v), in_vmem(scaled)],
            [(queries, BF16), (queries, F32)],
        )
        return q, near, state, scaled
    return vmem_call(
        project_kernel(len(xs), relatives, seq, pick, heads_step, heads),
        steps,
        [*xs, weight, wt],
        [(queries, BF16), (queries, F32), (states, F32), (levels, F32)],
        [pltpu.VMEM(*held), scales],
    )


BEFORE = (1, 3, 0, 2)


def scaled_levels(q, wt_ref, c, head, levels):
    q16 = q.reshape(8, 16, ROWS)
    scaled = []
    for level in levels:
        row = jnp.broadcast_to(wt_ref[c, head, level : level + 1, :], (16, ROWS)).astype(BF16)
        scaled.append((q16 * row[None]).reshape(128, ROWS))
    return jnp.concatenate(scaled, axis=0)


def part_kernel(picks, half_heads):
    def body(*refs):
        qs, nears, states, wts = refs[0:4], refs[4:8], refs[8:12], refs[12:16]
        core_ref, mine_ref, other_ref = refs[16:19]
        out_ref = refs[-1]
        head = pl.program_id(0)
        rows = pl.ds(head * 128, 128)
        core = lax.axis_index("seq") % 2
        places = [place_of(r) for r in range(4)]
        st = [states[r][picks[r], head] for r in range(4)]
        buckets = [(core_ref[head].astype(F32) * core.astype(F32)).astype(BF16)]
        for j in range(mine_ref.shape[0]):
            at = head % half_heads
            buckets.append(jnp.where(head // half_heads == core, mine_ref[j, at], other_ref[j, at]))
        for r in range(4):
            place = places[r]
            level9 = st[BEFORE[r]] * (place % 2).astype(F32)
            upper = (place // 2).astype(F32)
            level10 = sum(
                [st[o] * (upper * (1 - places[o] // 2).astype(F32)) for o in range(4) if o != r]
            )
            mats = jnp.concatenate([level9.astype(BF16), level10.astype(BF16)] + buckets, axis=1)
            scaled = scaled_levels(
                qs[r][picks[r], rows, :], wts[r], picks[r], head, range(9, 11 + len(buckets))
            )
            out_ref[r, rows, :] = nears[r][picks[r], rows, :] + jnp.dot(
                mats, scaled, preferred_element_type=F32
            )

    return body


def last_kernel(picks, half_heads, seq, first_level, mine):
    def body(lengths_ref, *refs):
        qs, wts = refs[0:4], refs[4:8]
        part_ref, level_ref = refs[8:10]
        out_ref, buf, sem = refs[-3:]
        core = lax.axis_index("seq") % 2
        half = core if mine else 1 - core
        limit = lengths_ref[seq] - lax.axis_index("seq") * (4 * ROWS)
        levels = range(first_level, first_level + level_ref.shape[0])
        lane = lax.broadcasted_iota(jnp.int32, (1, ROWS), 1)
        copies = []
        for j in range(half_heads):
            head = half * half_heads + j
            rows = pl.ds(pl.multiple_of(head * 128, 128), 128)
            mats = jnp.concatenate([level_ref[i, j] for i in range(len(levels))], axis=1)
            for r in range(4):
                place = place_of(r)
                scaled = scaled_levels(
                    qs[r][picks[r], rows, :], wts[r], picks[r], head, levels
                )
                acc = part_ref[r, rows, :] + jnp.dot(mats, scaled, preferred_element_type=F32)
                scale = lax.rsqrt(jnp.mean(acc * acc, 0, keepdims=True) + 1e-06)
                valid = place * ROWS + lane < limit
                acc = acc * jnp.where(valid, scale, 0.0)
                buf[j, place] = acc.astype(BF16).T
            copies.append(
                pltpu.make_async_copy(buf.at[j], out_ref.at[seq, :, :, rows], sem.at[j])
            )
            copies[-1].start()
        for copy in copies:
            copy.wait()

    return body


def far(lengths, chunks, found, seq, out_prev, seqs):
    core_bucket, x_levels, x_other, y_levels, y_other = found
    heads = core_bucket.shape[0]
    half_heads = heads // 2
    picks = [c for _, c in chunks]
    vmem = pl.BlockSpec(memory_space=pltpu.VMEM)
    columns = [[in_vmem(call[i]) for call, _ in chunks] for i in range(4)]
    args = columns[0] + columns[1] + columns[2] + columns[3] + [core_bucket, x_levels, x_other]
    part = pl.pallas_call(
        part_kernel(picks, half_heads),
        grid=(heads,),
        in_specs=[vmem] * len(args),
        out_specs=vmem,
        out_shape=pltpu.VMEM((4, heads * 128, ROWS), F32),
        compiler_params=pltpu.CompilerParams(vmem_limit_bytes=4 << 20),
        name="far_part",
    )(*args)
    out = out_prev
    for mine, levels in ((True, y_levels), (False, y_other)):
        args = [lengths] + columns[0] + columns[3] + [in_vmem(part), in_vmem(levels)]
        in_specs = [pl.BlockSpec(memory_space=pltpu.SMEM)] + [vmem] * (len(args) - 1)
        aliases = {}
        if out is not None:
            in_specs.append(pl.BlockSpec(memory_space=pl.ANY))
            args.append(out)
            aliases = {len(args) - 1: 0}
        out = pl.pallas_call(
            last_kernel(picks, half_heads, seq, 12 + x_levels.shape[0], mine),
            in_specs=in_specs,
            out_specs=pl.BlockSpec(memory_space=pl.ANY),
            out_shape=jax.ShapeDtypeStruct((seqs, 4, ROWS, heads * 128), BF16),
            scratch_shapes=[
                pltpu.VMEM((half_heads, 4, ROWS, 128), BF16),
                pltpu.SemaphoreType.DMA((half_heads,)),
            ],
            input_output_aliases=aliases,
            compiler_params=pltpu.CompilerParams(vmem_limit_bytes=6 << 20),
            name="far_last",
        )(*args)
    return out


def small_call(body, outs, *args):
    return vmem_call(body, 1, [in_vmem(x) for x in args], outs, limit=4)


def seq_bit(j):
    return (lax.axis_index("seq") // (1 << j)) % 2


def total_kernel(own_ref, ab_ref, cd_ref, total_ref, sent_ref):
    total = own_ref[0] + ab_ref[0] + ab_ref[1] + cd_ref[0]
    total_ref[...] = total
    sent_ref[...] = total.astype(BF16)


def core_kernel(total_ref, received_ref, part_ref, sent_ref):
    half = part_ref.shape[0]
    heads = pl.ds(seq_bit(0) * half, half)
    part = total_ref[heads] + received_ref[heads].astype(F32)
    part_ref[...] = part
    sent_ref[...] = part.astype(BF16)


def stage_kernel(low, last):
    def body(part_ref, one_ref, two_ref, three_ref, mine_ref, *outs):
        one, two, three = [r[...].astype(F32) for r in (one_ref, two_ref, three_ref)]
        mine_ref[0] = (one * seq_bit(low).astype(F32)).astype(BF16)
        mine_ref[1] = ((two + three) * seq_bit(low + 1).astype(F32)).astype(BF16)
        if not last:
            next_ref, sent_ref = outs
            part = part_ref[...] + (one + (two + three))
            next_ref[...] = part
            sent_ref[...] = part.astype(BF16)

    return body


def exchange(own, ab, cd):
    size = lax.axis_size("seq")
    heads = own.shape[1]
    whole, half = (heads, 128, 128), (heads // 2, 128, 128)

    def swap(value, mask):
        return lax.ppermute(value, "seq", [(i, i ^ mask) for i in range(size)])

    total, sent = small_call(total_kernel, [(whole, F32), (whole, BF16)], own, ab, cd)
    core_bucket = swap(sent, 1)
    part, sent = small_call(core_kernel, [(half, F32), (half, BF16)], total, core_bucket)
    found = [core_bucket]
    for low in (1, 3):
        heard = [swap(sent, mask << low) for mask in (1, 2, 3)]
        outs = [((2,) + half, BF16), (half, F32), (half, BF16)]
        made = small_call(stage_kernel(low, low == 3), outs[: 1 if low == 3 else 3], part, *heard)
        found += [made[0], swap(made[0], 1)]
        if low == 1:
            part, sent = made[1:]
    return found


def on_device(tokens, norm_gain, projection, level_table, level_index, lengths):
    seqs, row_count, _ = tokens.shape
    tables, heads, level_total = level_table.shape
    groups = lax.axis_size("head")
    half = row_count // 2
    up = [(i, (i + 1) % groups) for i in range(groups)]
    down = [(i, (i - 1) % groups) for i in range(groups)]

    got = []
    held = tokens
    for s in range(seqs):
        low, high = held[s : s + 1, :half], held[s : s + 1, half:]
        a_low = lax.ppermute(low, "head", up)
        b_high = lax.ppermute(high, "head", down)
        a_high = lax.ppermute(high, "head", up)
        b_low = lax.ppermute(low, "head", down)
        if s + 1 < seqs:
            held, a_low, b_high = lax.optimization_barrier((tokens, a_low, b_high))
        c = lax.ppermute(a_low, "head", up)
        d = lax.ppermute(b_high, "head", down)
        got.append(([a_low, a_high, b_low, b_high], [c, d]))

    level_rows = -(-level_total // 8) * 8
    onehot = (level_index[..., None] == jnp.arange(tables, dtype=jnp.int32)).astype(F32)
    table = jnp.pad(level_table, ((0, 0), (0, 0), (0, level_rows - level_total)))
    wt = jnp.einsum(
        "ghl,szrg->szhlr",
        table,
        onehot.reshape(seqs, groups, row_count, tables),
        precision=lax.Precision.HIGHEST,
    )

    weight = fold_gain(norm_gain, projection)

    own = []
    for s in range(seqs):
        own.append(project([tokens], s, [0], weight, wt, s))
    parts = []
    for s in range(seqs):
        ab = project(got[s][0], s, [1, 2], weight, wt)
        cd = project(got[s][1], s, [3], weight, wt, states_first=s + 1 == seqs)
        parts.append((ab, cd))

    out = None
    for s in range(seqs):
        ab, cd = parts[s]
        found = exchange(own[s][2], ab[2], cd[2])
        chunks = [(own[s], 0), (ab, 0), (ab, 1), (cd, 0)]
        out = far(lengths, chunks, found, s, out, seqs)
    return out.reshape(seqs, row_count * groups, heads * 128)


def solution(mesh):
    in_specs = (
        P(None, ("seq", "head"), None),
        P(),
        P(None, "head"),
        P(None, "head", None),
        P(None, "seq"),
        P(),
    )
    out_specs = P(None, "seq", "head")

    return jax.shard_map(on_device, mesh=mesh, in_specs=in_specs, out_specs=out_specs, check_vma=False)
```

time: 118 us -> 134 us (1.14)
  Pallas kernels: 39.9 us -> 49.1 us
  local copies, waits for them, and re-layouts: 1.54 us -> 4.92 us
  starting transfers between devices: 41.5 us -> 43.2 us
    pallas_call x16 -> x21, Pallas kernels: 33.9 us -> 43.2 us  [the longest x15 32.7 us: vmem_call(): pl.pallas_call(body, grid=(steps,), in_specs=[pl.BlockSpec(memory_space=p...]
    ppermute x2, waiting for transfers between devices: 9.4 us -> 18.1 us  [on_device(): a_low = lax.ppermute(low, 'head', up)]
    ppermute x16 -> x18, waiting for transfers between devices: 9.88 us -> 2.17 us  [swap(): return lax.ppermute(value, 'seq', [(i, i ^ mask) for i in range(size)])]
    unnamed x10 -> x27, local copies, waits for them, and re-layouts: 0.02 us -> 2.44 us
    ppermute x16 -> x18, starting transfers between devices: 25.5 us -> 27.3 us  [swap(): return lax.ppermute(value, 'seq', [(i, i ^ mask) for i in range(size)])]
  transfers between devices with their start and end apart: 28 -> 30, of which waited for: 10 -> 5; matrix products, arithmetic and copies ran while one was open for 1% -> 1% of each run, Pallas kernels for 28% -> 35%
where the time goes in v2:
time: 134 us
  Pallas kernels  49.1 us (37%)
  starting transfers between devices  43.2 us (32%)
  waiting for transfers between devices  35.5 us (26%)
  local copies, waits for them, and re-layouts  4.92 us (4%)
    pallas_call x15, Pallas kernels, vmem_call(): pl.pallas_call(body, grid=(steps,), in_specs=[pl.BlockSpec(memory_space=p...  32.7 us
    ppermute x18, starting transfers between devices, swap(): return lax.ppermute(value, 'seq', [(i, i ^ mask) for i in range(size)])  27.3 us
    ppermute x2, waiting for transfers between devices, on_device(): a_low = lax.ppermute(low, 'head', up)  18.1 us
    ppermute x2, waiting for transfers between devices, on_device(): c = lax.ppermute(a_low, 'head', up)  8.17 us
    pallas_call x4, Pallas kernels, far(): pl.pallas_call(last_kernel(picks, half_heads, seq, 12 + x_levels.shape[0]...  7.1 us
    ppermute x2, waiting for transfers between devices, on_device(): a_high = lax.ppermute(high, 'head', up)  6.99 us
    pallas_call x1, Pallas kernels, fold_gain(): pl.pallas_call(fold_kernel, grid=(width // ROWS,), in_specs=[pl.BlockSpec...  5.89 us
    ppermute x2, starting transfers between devices, on_device(): a_low = lax.ppermute(low, 'head', up)  3.86 us
  transfers between devices with their start and end apart: 30, of which 5 were waited for; matrix products, arithmetic and copies ran while one was open for 1% of the time, Pallas kernels for 35%

profile of v2, /device:TPU:1, one launch (start us, length us, event | category | flops | bytes accessed | tf_op | source)
XLA Modules:
  0.0 133.8 jit_solution(14095660655050549478)
XLA Ops:
  0.0 1.4 %fusion.7 = (bf16[1,128,2048]{2,1,0:T(8,128)(2,1)S(1)}, bf16[1,128,2048]{2,1,0:T(8,128)(2,1)S(1)}) fusion(bf16[2,256,2048]{2,1,0:T(8,128)(2,1)} %refs_0_.3), kind=kLoop, calls=%fused_computation.8 | loop fusion | bytes 2097152 | tf_op jit(solution)/shard_map/slice | solution.py:445
  1.4 2.5 %collective-permute-start = (bf16[1,128,2048]{2,1,0:T(8,128)(2,1)S(1)}, bf16[1,128,2048]{2,1,0:T(8,128)(2,1)S(1)}, u32[]{:S(2)}, u32[]{:S(2)}) collective-permute-start(bf16[1,128,2048]{2,1,0:T(8,128)(2,1)S(1)} %get-tuple-element.96), channel_id=1, source_target_pairs={{0,1},{1,2},{2,3},{3,0},{4,5},{5,6},{6,7},{7,4},{8,9},{9,10},{10,1... | collective-permute-start | bytes 1572872 | tf_op jit(solution)/shard_map/ppermute | solution.py:446
  4.0 2.2 %collective-permute-start.1 = (bf16[1,128,2048]{2,1,0:T(8,128)(2,1)S(1)}, bf16[1,128,2048]{2,1,0:T(8,128)(2,1)}, u32[]{:S(2)}, u32[]{:S(2)}) collective-permute-start(bf16[1,128,2048]{2,1,0:T(8,128)(2,1)S(1)} %get-tuple-element.95), channel_id=1, source_target_pairs={{0,3},{1,0},{2,1},{3,2},{4,7},{5,4},{6,5},{7,6},{8,11},{9,8},{10,9... | collective-permute-start | bytes 1572872 | tf_op jit(solution)/shard_map/ppermute | solution.py:447
  6.2 0.0 collective-permute-start.17
  6.2 2.7 %collective-permute-start.18 = (bf16[1,128,2048]{2,1,0:T(8,128)(2,1)S(1)}, bf16[1,128,2048]{2,1,0:T(8,128)(2,1)S(1)}, u32[]{:S(2)}, u32[]{:S(2)}) collective-permute-start(bf16[1,128,2048]{2,1,0:T(8,128)(2,1)S(1)} %get-tuple-element.96), channel_id=1, source_target_pairs={{0,3},{1,0},{2,1},{3,2},{4,7},{5,4},{6,5},{7,6},{8,11},{9,8},{10,9... | collective-permute-start | bytes 1572872 | tf_op jit(solution)/shard_map/ppermute | solution.py:449
  8.8 8.9 %collective-permute-done.refs_0_ = bf16[1,128,2048]{2,1,0:T(8,128)(2,1)S(1)} collective-permute-done((bf16[1,128,2048]{2,1,0:T(8,128)(2,1)S(1)}, bf16[1,128,2048]{2,1,0:T(8,128)(2,1)S(1)}, u32[]{:S(2)}, u32[]{:S(2)}) %collective-permute-start) | collective-permute-done | bytes 524320 | tf_op jit(solution)/shard_map/ppermute | solution.py:446
  17.7 0.0 collective-permute-done.1.refs_3_
  17.7 0.5 collective-permute-start.19
  18.2 1.0 fusion.6
  19.3 1.3 %collective-permute-start.2 = (bf16[1,128,2048]{2,1,0:T(8,128)(2,1)}, bf16[1,128,2048]{2,1,0:T(8,128)(2,1)S(1)}, u32[]{:S(2)}, u32[]{:S(2)}) collective-permute-start(bf16[1,128,2048]{2,1,0:T(8,128)(2,1)} %get-tuple-element.94), channel_id=1, source_target_pairs={{0,1},{1,2},{2,3},{3,0},{4,5},{5,6},{6,7},{7,4},{8,9},{9,10},{10,1... | collective-permute-start | bytes 1572872 | tf_op jit(solution)/shard_map/ppermute | solution.py:446
  20.6 1.3 collective-permute-start.5
  22.0 7.0 %collective-permute-done.17.refs_1_ = bf16[1,128,2048]{2,1,0:T(8,128)(2,1)S(1)} collective-permute-done((bf16[1,128,2048]{2,1,0:T(8,128)(2,1)S(1)}, bf16[1,128,2048]{2,1,0:T(8,128)(2,1)S(1)}, u32[]{:S(2)}, u32[]{:S(2)}) %collective-permute-start.17) | collective-permute-done | bytes 524320 | tf_op jit(solution)/shard_map/ppermute | solution.py:448
  28.9 0.8 copy-done.3
  29.7 1.2 collective-permute-start.20
  30.9 0.0 collective-permute-done.18.refs_2_
  30.9 0.8 copy-done.5
  31.7 0.3 collective-permute-start.3
  32.0 8.2 %collective-permute-done.19.refs_0_ = bf16[1,128,2048]{2,1,0:T(8,128)(2,1)S(1)} collective-permute-done((bf16[1,128,2048]{2,1,0:T(8,128)(2,1)S(1)}, bf16[1,128,2048]{2,1,0:T(8,128)(2,1)S(1)}, u32[]{:S(2)}, u32[]{:S(2)}) %collective-permute-start.19) | collective-permute-done | bytes 524320 | tf_op jit(solution)/shard_map/ppermute | solution.py:452
  40.2 0.8 copy-done.7
  41.0 1.2 collective-permute-start.4
  42.2 9.2 %collective-permute-done.2.refs_0_ = bf16[1,128,2048]{2,1,0:T(8,128)(2,1)S(1)} collective-permute-done((bf16[1,128,2048]{2,1,0:T(8,128)(2,1)}, bf16[1,128,2048]{2,1,0:T(8,128)(2,1)S(1)}, u32[]{:S(2)}, u32[]{:S(2)}) %collective-permute-start.2) | collective-permute-done | bytes 524320 | tf_op jit(solution)/shard_map/ppermute | solution.py:446
  51.4 0.0 collective-permute-start.6
  51.4 0.0 collective-permute-done.5.refs_3_
  51.4 2.7 %collective-permute-start.7 = (bf16[1,128,2048]{2,1,0:T(8,128)(2,1)S(1)}, bf16[1,128,2048]{2,1,0:T(8,128)(2,1)}, u32[]{:S(2)}, u32[]{:S(2)}) collective-permute-start(bf16[1,128,2048]{2,1,0:T(8,128)(2,1)S(1)} %collective-permute-done.5.refs_3_), channel_id=1, source_target_pairs={{0,3},{1,0},{2,1},{3,2},{4,7},{5,4},{6,5},{7,6},{8,11},{9,8},{10,9... | collective-permute-start | bytes 1572872 | tf_op jit(solution)/shard_map/ppermute | solution.py:453
  54.1 5.9 %fold_gain.1.refs_1_.refs_4_.refs_2_.w_ref = bf16[2048,1536]{1,0:T(8,128)(2,1)S(1)} custom-call(f32[1,2048]{1,0:T(1,128)S(1)} %bitcast.14, bf16[2048,1536]{1,0:T(8,128)(2,1)} %w_ref.1), custom_call_target="tpu_custom_call" | custom-call | tf_op jit(solution)/shard_map/fold_gain/pallas_call | solution.py:33
  60.0 0.5 convolution_bitcast_fusion.refs_2_.refs_5_.refs_3_
  60.6 3.8 %shard_map.72 = (bf16[1,512,256]{2,1,0:T(8,128)(2,1)S(1)}, f32[1,512,256]{2,1,0:T(8,128)S(1)}, f32[1,4,128,128]{3,2,1,0:T(8,128)S(1)}, f32[1,4,24,256]{3,2,1,0:T(8,128)S(1)}) custom-call(bf16[2,256,2048]{2,1,0:T(8,128)(2,1)S(1)} %copy-done, bf16[2048,1536]{1,0:T(8,128)(2,1)S(1)} %fold_gain.1.refs_1_.refs_4_.refs_2_.w_ref, ...), custom_call_target="tpu_custom_call" | custom-call | tf_op jit(solution)/shard_map/pallas_call | solution.py:204
  64.4 7.4 %shard_map.73 = (bf16[2,512,256]{2,1,0:T(8,128)(2,1)S(1)}, f32[2,512,256]{2,1,0:T(8,128)S(1)}, f32[2,4,128,128]{3,2,1,0:T(8,128)S(1)}, f32[2,4,24,256]{3,2,1,0:T(8,128)S(1)}) custom-call(bf16[1,128,2048]{2,1,0:T(8,128)(2,1)S(1)} %copy-done.2, bf16[1,128,2048]{2,1,0:T(8,128)(2,1)S(1)} %copy-done.4, bf16[1,128,2048]{2,1,0:T(8,128)(2,1)S(1)} %copy-done.6, ...), custom_call_target="tpu_custom_call" | custom-call | tf_op jit(solution)/shard_map/pallas_call | solution.py:204
  71.9 0.0 collective-permute-done.20.refs_1_
  71.9 4.8 %shard_map.74 = (bf16[1,512,256]{2,1,0:T(8,128)(2,1)S(1)}, f32[1,512,256]{2,1,0:T(8,128)S(1)}, f32[1,4,128,128]{3,2,1,0:T(8,128)S(1)}, f32[1,4,24,256]{3,2,1,0:T(8,128)S(1)}) custom-call(bf16[1,128,2048]{2,1,0:T(8,128)(2,1)S(1)} %copy-done.8, bf16[1,128,2048]{2,1,0:T(8,128)(2,1)} %collective-permute-done.20.refs_1_, ...), custom_call_target="tpu_custom_call" | custom-call | tf_op jit(solution)/shard_map/pallas_call | solution.py:204
  76.7 0.1 shard_map.75
  76.8 2.9 %collective-permute-start.21 = (bf16[4,128,128]{2,1,0:T(8,128)(2,1)S(1)}, bf16[4,128,128]{2,1,0:T(8,128)(2,1)S(1)}, u32[]{:S(2)}, u32[]{:S(2)}) collective-permute-start(bf16[4,128,128]{2,1,0:T(8,128)(2,1)S(1)} %get-tuple-element.86), channel_id=1, source_target_pairs={{0,4},{4,0},{8,12},{12,8},{16,20},{20,16},{24,28},{28,24},{32,36},... | collective-permute-start | bytes 393224 | tf_op jit(solution)/shard_map/ppermute | solution.py:418
  79.7 3.8 %shard_map.64 = (bf16[1,512,256]{2,1,0:T(8,128)(2,1)S(1)}, f32[1,512,256]{2,1,0:T(8,128)S(1)}, f32[1,4,128,128]{3,2,1,0:T(8,128)S(1)}, f32[1,4,24,256]{3,2,1,0:T(8,128)S(1)}) custom-call(bf16[2,256,2048]{2,1,0:T(8,128)(2,1)S(1)} %copy-done, bf16[2048,1536]{1,0:T(8,128)(2,1)S(1)} %fold_gain.1.refs_1_.refs_4_.refs_2_.w_ref, ...), custom_call_target="tpu_custom_call" | custom-call | tf_op jit(solution)/shard_map/pallas_call | solution.py:204
  83.5 0.0 collective-permute-done.3.refs_1_
  83.5 7.5 %shard_map.65 = (bf16[2,512,256]{2,1,0:T(8,128)(2,1)S(1)}, f32[2,512,256]{2,1,0:T(8,128)S(1)}, f32[2,4,128,128]{3,2,1,0:T(8,128)S(1)}, f32[2,4,24,256]{3,2,1,0:T(8,128)S(1)}) custom-call(bf16[1,128,2048]{2,1,0:T(8,128)(2,1)S(1)} %collective-permute-done.2.refs_0_, bf16[1,128,2048]{2,1,0:T(8,128)(2,1)} %collective-permute-done.3.refs_1_, ...), custom_call_target="tpu_custom_call" | custom-call | tf_op jit(solution)/shard_map/pallas_call | solution.py:204
  91.1 3.0 %shard_map.66 = (f32[1,4,128,128]{3,2,1,0:T(8,128)S(1)}, bf16[4,256,128]{2,1,0:T(8,128)(2,1)S(1)}, bf16[4,128,256]{2,1,0:T(8,128)(2,1)S(1)}, f32[1,4,24,256]{3,2,1,0:T(8,128)S(1)}, bf16[256,2048]{1,0:T(8,128)(2,1)S(1)}) custom-call(bf16[1,128,2048]{2,1,0:T(8,128)(2,1)} %collective-permute-done.6.refs_0_, ...), custom_call_target="tpu_custom_call" | custom-call | tf_op jit(solution)/shard_map/pallas_call | solution.py:204
  94.0 0.1 shard_map.68
  94.1 0.1 collective-permute-start.8
  94.2 0.0 collective-permute-done.21.received_ref.refs_16_
  94.2 1.3 collective-permute-start.22
  95.5 2.5 %collective-permute-start.23 = (bf16[2,128,128]{2,1,0:T(8,128)(2,1)S(1)}, bf16[2,128,128]{2,1,0:T(8,128)(2,1)S(1)}, u32[]{:S(2)}, u32[]{:S(2)}) collective-permute-start(bf16[2,128,128]{2,1,0:T(8,128)(2,1)S(1)} %get-tuple-element.89), channel_id=1, source_target_pairs={{0,16},{4,20},{8,24},{12,28},{16,0},{20,4},{24,8},{28,12},{32,48},... | collective-permute-start | bytes 196616 | tf_op jit(solution)/shard_map/ppermute | solution.py:418
  98.0 0.2 collective-permute-start.24
  98.2 1.6 %collective-permute-start.10 = (bf16[2,128,128]{2,1,0:T(8,128)(2,1)S(1)}, bf16[2,128,128]{2,1,0:T(8,128)(2,1)S(1)}, u32[]{:S(2)}, u32[]{:S(2)}) collective-permute-start(bf16[2,128,128]{2,1,0:T(8,128)(2,1)S(1)} %get-tuple-element.68), channel_id=1, source_target_pairs={{0,16},{4,20},{8,24},{12,28},{16,0},{20,4},{24,8},{28,12},{32,48},... | collective-permute-start | bytes 196616 | tf_op jit(solution)/shard_map/ppermute | solution.py:418
  99.8 1.0 collective-permute-start.11
  100.9 0.5 collective-permute-start.9
  101.4 2.1 %collective-permute-done.24.three_ref = bf16[2,128,128]{2,1,0:T(8,128)(2,1)S(1)} collective-permute-done((bf16[2,128,128]{2,1,0:T(8,128)(2,1)S(1)}, bf16[2,128,128]{2,1,0:T(8,128)(2,1)S(1)}, u32[]{:S(2)}, u32[]{:S(2)}) %collective-permute-start.24) | collective-permute-done | bytes 65568 | tf_op jit(solution)/shard_map/ppermute | solution.py:418
  103.5 0.1 shard_map.77
  103.6 1.4 %collective-permute-start.26 = (bf16[2,128,128]{2,1,0:T(8,128)(2,1)S(1)}, bf16[2,128,128]{2,1,0:T(8,128)(2,1)S(1)}, u32[]{:S(2)}, u32[]{:S(2)}) collective-permute-start(bf16[2,128,128]{2,1,0:T(8,128)(2,1)S(1)} %get-tuple-element.92), channel_id=1, source_target_pairs={{0,32},{4,36},{8,40},{12,44},{16,48},{20,52},{24,56},{28,60},{32,0... | collective-permute-start | bytes 196616 | tf_op jit(solution)/shard_map/ppermute | solution.py:418
  104.9 2.6 %collective-permute-start.27 = (bf16[2,128,128]{2,1,0:T(8,128)(2,1)S(1)}, bf16[2,128,128]{2,1,0:T(8,128)(2,1)S(1)}, u32[]{:S(2)}, u32[]{:S(2)}) collective-permute-start(bf16[2,128,128]{2,1,0:T(8,128)(2,1)S(1)} %get-tuple-element.92), channel_id=1, source_target_pairs={{0,64},{4,68},{8,72},{12,76},{16,80},{20,84},{24,88},{28,92},{32,9... | collective-permute-start | bytes 196616 | tf_op jit(solution)/shard_map/ppermute | solution.py:418
  107.6 0.1 shard_map.70
  107.6 0.1 collective-permute-start.13
  107.7 3.8 %collective-permute-start.14 = (bf16[2,128,128]{2,1,0:T(8,128)(2,1)S(1)}, bf16[2,128,128]{2,1,0:T(8,128)(2,1)S(1)}, u32[]{:S(2)}, u32[]{:S(2)}) collective-permute-start(bf16[2,128,128]{2,1,0:T(8,128)(2,1)S(1)} %get-tuple-element.71), channel_id=1, source_target_pairs={{0,64},{4,68},{8,72},{12,76},{16,80},{20,84},{24,88},{28,92},{32,9... | collective-permute-start | bytes 196616 | tf_op jit(solution)/shard_map/ppermute | solution.py:418
  111.6 0.0 collective-permute-start.15
  111.6 3.8 %collective-permute-start.25 = (bf16[2,2,128,128]{3,2,1,0:T(8,128)(2,1)S(1)}, bf16[2,2,128,128]{3,2,1,0:T(8,128)(2,1)S(1)}, u32[]{:S(2)}, u32[]{:S(2)}) collective-permute-start(bf16[2,2,128,128]{3,2,1,0:T(8,128)(2,1)S(1)} %get-tuple-element.90.refs_17_), channel_id=1, source_target_pairs={{0,4},{4,0},{8,12},{12,8},{16,20},{20,16},{24,28},{28,24},{32,36},... | collective-permute-start | bytes 393224 | tf_op jit(solution)/shard_map/ppermute | solution.py:418
  115.4 0.5 collective-permute-start.29
  115.9 0.1 collective-permute-start.12
  116.0 4.9 %collective-permute-start.16 = (bf16[2,2,128,128]{3,2,1,0:T(8,128)(2,1)S(1)}, bf16[2,2,128,128]{3,2,1,0:T(8,128)(2,1)S(1)}, u32[]{:S(2)}, u32[]{:S(2)}) collective-permute-start(bf16[2,2,128,128]{3,2,1,0:T(8,128)(2,1)S(1)} %shard_map.71.refs_9_), channel_id=1, source_target_pairs={{0,4},{4,0},{8,12},{12,8},{16,20},{20,16},{24,28},{28,24},{32,36},... | collective-permute-start | bytes 393224 | tf_op jit(solution)/shard_map/ppermute | solution.py:418
  120.9 1.7 %far_part.3.refs_8_ = f32[4,512,256]{2,1,0:T(8,128)S(1)} custom-call(bf16[1,512,256]{2,1,0:T(8,128)(2,1)S(1)} %get-tuple-element.72.refs_0_, bf16[2,512,256]{2,1,0:T(8,128)(2,1)S(1)} %get-tuple-element.75.refs_1_.refs_2_, bf16[2,512,256]{2,1,0:T(8,128)(2,1)S(1)} %get-tuple-element.75.refs_1_.refs_2_, bf16[1,512,256]{2,1,0:T(8,128)(2,1)S(1)} %get-tuple-element.76.refs_3_, ...), custom_call_target="tpu_custom_call" | custom-call | tf_op jit(solution)/shard_map/far_part/pallas_call | solution.py:342
  122.7 1.8 %far_last.4.refs_10_ = bf16[2,4,256,512]{3,2,1,0:T(8,128)(2,1)} custom-call(s32[2]{0:T(128)S(1)} %copy-done.9, bf16[1,512,256]{2,1,0:T(8,128)(2,1)S(1)} %get-tuple-element.72.refs_0_, bf16[2,512,256]{2,1,0:T(8,128)(2,1)S(1)} %get-tuple-element.75.refs_1_.refs_2_, bf16[2,512,256]{2,1,0:T(8,128)(2,1)S(1)} %get-tuple-element.75.refs_1_.refs_2_, ...), custom_call_target="tpu_custom_call" | custom-call | tf_op jit(solution)/shard_map/far_last/pallas_call | solution.py:360
  124.4 1.8 %far_last.5.refs_10_ = bf16[2,4,256,512]{3,2,1,0:T(8,128)(2,1)} custom-call(s32[2]{0:T(128)S(1)} %copy-done.9, bf16[1,512,256]{2,1,0:T(8,128)(2,1)S(1)} %get-tuple-element.72.refs_0_, bf16[2,512,256]{2,1,0:T(8,128)(2,1)S(1)} %get-tuple-element.75.refs_1_.refs_2_, ...), custom_call_target="tpu_custom_call", output_to_operand_aliasing={{}: (11, {})} | custom-call | tf_op jit(solution)/shard_map/far_last/pallas_call | solution.py:360
  126.2 2.1 %shard_map.67 = (bf16[1,512,256]{2,1,0:T(8,128)(2,1)S(1)}, f32[1,512,256]{2,1,0:T(8,128)S(1)}) custom-call(bf16[256,2048]{1,0:T(8,128)(2,1)S(1)} %get-tuple-element.52.held, bf16[2048,1536]{1,0:T(8,128)(2,1)S(1)} %fold_gain.1.refs_1_.refs_4_.refs_2_.w_ref, bf16[4,256,128]{2,1,0:T(8,128)(2,1)S(1)} %get-tuple-element.53.k_ref, ...), custom_call_target="tpu_custom_call" | custom-call | tf_op jit(solution)/shard_map/pallas_call | solution.py:204
  128.3 1.7 %far_part.2.refs_8_ = f32[4,512,256]{2,1,0:T(8,128)S(1)} custom-call(bf16[1,512,256]{2,1,0:T(8,128)(2,1)S(1)} %get-tuple-element.49.refs_0_, bf16[2,512,256]{2,1,0:T(8,128)(2,1)S(1)} %get-tuple-element.51.refs_1_.refs_2_, bf16[2,512,256]{2,1,0:T(8,128)(2,1)S(1)} %get-tuple-element.51.refs_1_.refs_2_, bf16[1,512,256]{2,1,0:T(8,128)(2,1)S(1)} %get-tuple-element.56.refs_3_, ...), custom_call_target="tpu_custom_call" | custom-call | tf_op jit(solution)/shard_map/far_part/pallas_call | solution.py:342
  130.1 1.8 %far_last.6.refs_10_ = bf16[2,4,256,512]{3,2,1,0:T(8,128)(2,1)} custom-call(s32[2]{0:T(128)S(1)} %copy-done.9, bf16[1,512,256]{2,1,0:T(8,128)(2,1)S(1)} %get-tuple-element.49.refs_0_, bf16[2,512,256]{2,1,0:T(8,128)(2,1)S(1)} %get-tuple-element.51.refs_1_.refs_2_, ...), custom_call_target="tpu_custom_call", output_to_operand_aliasing={{}: (11, {})} | custom-call | tf_op jit(solution)/shard_map/far_last/pallas_call | solution.py:360
  131.8 1.8 %far_last.7 = bf16[2,4,256,512]{3,2,1,0:T(8,128)(2,1)} custom-call(s32[2]{0:T(128)S(1)} %copy-done.9, bf16[1,512,256]{2,1,0:T(8,128)(2,1)S(1)} %get-tuple-element.49.refs_0_, bf16[2,512,256]{2,1,0:T(8,128)(2,1)S(1)} %get-tuple-element.51.refs_1_.refs_2_, bf16[2,512,256]{2,1,0:T(8,128)(2,1)S(1)} %get-tuple-element.51.refs_1_.refs_2_, ...), custom_call_target="tpu_custom_call", output_to_operand_aliasing={{}: (11, {})} | custom-call | tf_op jit(solution)/shard_map/far_last/pallas_call | solution.py:360
  (49 shorter events, 0.2 us)
Async XLA Ops:
  0.0 18.2 %copy-start = (bf16[2,256,2048]{2,1,0:T(8,128)(2,1)S(1)}, bf16[2,256,2048]{2,1,0:T(8,128)(2,1)}, u32[]{:S(2)}) copy-start(bf16[2,256,2048]{2,1,0:T(8,128)(2,1)} %refs_0_.3) | copy-start | bytes 6291460
  0.0 54.1 %copy-start.11 = (f32[16,4,18]{2,1,0:T(4,128)S(1)}, f32[16,4,18]{2,1,0:T(4,128)}, u32[]{:S(2)}) copy-start(f32[16,4,18]{2,1,0:T(4,128)} %param.9) | copy-start | bytes 13828
  0.0 54.1 %copy-start.12 = (s32[2,1024]{1,0:T(2,128)S(1)}, s32[2,1024]{1,0:T(2,128)}, u32[]{:S(2)}) copy-start(s32[2,1024]{1,0:T(2,128)} %param.10) | copy-start | bytes 24580
  0.0 54.1 %copy-start.10 = (f32[2048]{0:T(1024)S(1)}, f32[2048]{0:T(1024)}, u32[]{:S(2)}) copy-start(f32[2048]{0:T(1024)} %param.7) | copy-start | bytes 24580
  1.4 16.3 %collective-permute-start = (bf16[1,128,2048]{2,1,0:T(8,128)(2,1)S(1)}, bf16[1,128,2048]{2,1,0:T(8,128)(2,1)S(1)}, u32[]{:S(2)}, u32[]{:S(2)}) collective-permute-start(bf16[1,128,2048]{2,1,0:T(8,128)(2,1)S(1)} %get-tuple-element.96), channel_id=1, source_target_pairs={{0,1},{1,2},{2,3},{3,0},{4,5},{5,6},{6,7},{7,4},{8,9},{9,10},{10,1... | collective-permute-start | bytes 1572872 | tf_op jit(solution)/shard_map/ppermute | solution.py:446
  4.0 13.8 %collective-permute-start.1 = (bf16[1,128,2048]{2,1,0:T(8,128)(2,1)S(1)}, bf16[1,128,2048]{2,1,0:T(8,128)(2,1)}, u32[]{:S(2)}, u32[]{:S(2)}) collective-permute-start(bf16[1,128,2048]{2,1,0:T(8,128)(2,1)S(1)} %get-tuple-element.95), channel_id=1, source_target_pairs={{0,3},{1,0},{2,1},{3,2},{4,7},{5,4},{6,5},{7,6},{8,11},{9,8},{10,9... | collective-permute-start | bytes 1572872 | tf_op jit(solution)/shard_map/ppermute | solution.py:447
  6.2 22.8 %collective-permute-start.17 = (bf16[1,128,2048]{2,1,0:T(8,128)(2,1)S(1)}, bf16[1,128,2048]{2,1,0:T(8,128)(2,1)S(1)}, u32[]{:S(2)}, u32[]{:S(2)}) collective-permute-start(bf16[1,128,2048]{2,1,0:T(8,128)(2,1)S(1)} %get-tuple-element.95), channel_id=1, source_target_pairs={{0,1},{1,2},{2,3},{3,0},{4,5},{5,6},{6,7},{7,4},{8,9},{9,10},{10,1... | collective-permute-start | bytes 1572872 | tf_op jit(solution)/shard_map/ppermute | solution.py:448
  6.2 24.8 %collective-permute-start.18 = (bf16[1,128,2048]{2,1,0:T(8,128)(2,1)S(1)}, bf16[1,128,2048]{2,1,0:T(8,128)(2,1)S(1)}, u32[]{:S(2)}, u32[]{:S(2)}) collective-permute-start(bf16[1,128,2048]{2,1,0:T(8,128)(2,1)S(1)} %get-tuple-element.96), channel_id=1, source_target_pairs={{0,3},{1,0},{2,1},{3,2},{4,7},{5,4},{6,5},{7,6},{8,11},{9,8},{10,9... | collective-permute-start | bytes 1572872 | tf_op jit(solution)/shard_map/ppermute | solution.py:449
  17.7 33.7 %copy-start.1 = (bf16[1,128,2048]{2,1,0:T(8,128)(2,1)}, bf16[1,128,2048]{2,1,0:T(8,128)(2,1)S(1)}, u32[]{:S(2)}) copy-start(bf16[1,128,2048]{2,1,0:T(8,128)(2,1)S(1)} %collective-permute-done.refs_0_) | copy-start | bytes 1572868
  17.7 22.5 %collective-permute-start.19 = (bf16[1,128,2048]{2,1,0:T(8,128)(2,1)S(1)}, bf16[1,128,2048]{2,1,0:T(8,128)(2,1)S(1)}, u32[]{:S(2)}, u32[]{:S(2)}) collective-permute-start(bf16[1,128,2048]{2,1,0:T(8,128)(2,1)S(1)} %collective-permute-done.refs_0_), channel_id=1, source_target_pairs={{0,1},{1,2},{2,3},{3,0},{4,5},{5,6},{6,7},{7,4},{8,9},{9,10},{10,1... | collective-permute-start | bytes 1572872 | tf_op jit(solution)/shard_map/ppermute | solution.py:452
  19.3 32.1 %collective-permute-start.2 = (bf16[1,128,2048]{2,1,0:T(8,128)(2,1)}, bf16[1,128,2048]{2,1,0:T(8,128)(2,1)S(1)}, u32[]{:S(2)}, u32[]{:S(2)}) collective-permute-start(bf16[1,128,2048]{2,1,0:T(8,128)(2,1)} %get-tuple-element.94), channel_id=1, source_target_pairs={{0,1},{1,2},{2,3},{3,0},{4,5},{5,6},{6,7},{7,4},{8,9},{9,10},{10,1... | collective-permute-start | bytes 1572872 | tf_op jit(solution)/shard_map/ppermute | solution.py:446
  20.6 30.8 %collective-permute-start.5 = (bf16[1,128,2048]{2,1,0:T(8,128)(2,1)}, bf16[1,128,2048]{2,1,0:T(8,128)(2,1)S(1)}, u32[]{:S(2)}, u32[]{:S(2)}) collective-permute-start(bf16[1,128,2048]{2,1,0:T(8,128)(2,1)} %get-tuple-element.93), channel_id=1, source_target_pairs={{0,3},{1,0},{2,1},{3,2},{4,7},{5,4},{6,5},{7,6},{8,11},{9,8},{10,9... | collective-permute-start | bytes 1572872 | tf_op jit(solution)/shard_map/ppermute | solution.py:447
  28.9 0.8 copy-start.3
  29.7 42.1 %collective-permute-start.20 = (bf16[1,128,2048]{2,1,0:T(8,128)(2,1)}, bf16[1,128,2048]{2,1,0:T(8,128)(2,1)}, u32[]{:S(2)}, u32[]{:S(2)}) collective-permute-start(bf16[1,128,2048]{2,1,0:T(8,128)(2,1)} %collective-permute-done.1.refs_3_), channel_id=1, source_target_pairs={{0,3},{1,0},{2,1},{3,2},{4,7},{5,4},{6,5},{7,6},{8,11},{9,8},{10,9... | collective-permute-start | bytes 1572872 | tf_op jit(solution)/shard_map/ppermute | solution.py:453
  30.9 0.8 copy-start.5
  31.7 51.7 %collective-permute-start.3 = (bf16[1,128,2048]{2,1,0:T(8,128)(2,1)}, bf16[1,128,2048]{2,1,0:T(8,128)(2,1)}, u32[]{:S(2)}, u32[]{:S(2)}) collective-permute-start(bf16[1,128,2048]{2,1,0:T(8,128)(2,1)} %get-tuple-element.93), channel_id=1, source_target_pairs={{0,1},{1,2},{2,3},{3,0},{4,5},{5,6},{6,7},{7,4},{8,9},{9,10},{10,1... | collective-permute-start | bytes 1572872 | tf_op jit(solution)/shard_map/ppermute | solution.py:448
  40.2 0.8 copy-start.7
  41.0 42.5 %collective-permute-start.4 = (bf16[1,128,2048]{2,1,0:T(8,128)(2,1)}, bf16[1,128,2048]{2,1,0:T(8,128)(2,1)}, u32[]{:S(2)}, u32[]{:S(2)}) collective-permute-start(bf16[1,128,2048]{2,1,0:T(8,128)(2,1)} %get-tuple-element.94), channel_id=1, source_target_pairs={{0,3},{1,0},{2,1},{3,2},{4,7},{5,4},{6,5},{7,6},{8,11},{9,8},{10,9... | collective-permute-start | bytes 1572872 | tf_op jit(solution)/shard_map/ppermute | solution.py:449
  51.4 39.6 %collective-permute-start.6 = (bf16[1,128,2048]{2,1,0:T(8,128)(2,1)S(1)}, bf16[1,128,2048]{2,1,0:T(8,128)(2,1)}, u32[]{:S(2)}, u32[]{:S(2)}) collective-permute-start(bf16[1,128,2048]{2,1,0:T(8,128)(2,1)S(1)} %collective-permute-done.2.refs_0_), channel_id=1, source_target_pairs={{0,1},{1,2},{2,3},{3,0},{4,5},{5,6},{6,7},{7,4},{8,9},{9,10},{10,1... | collective-permute-start | bytes 1572872 | tf_op jit(solution)/shard_map/ppermute | solution.py:452
  51.4 39.6 %collective-permute-start.7 = (bf16[1,128,2048]{2,1,0:T(8,128)(2,1)S(1)}, bf16[1,128,2048]{2,1,0:T(8,128)(2,1)}, u32[]{:S(2)}, u32[]{:S(2)}) collective-permute-start(bf16[1,128,2048]{2,1,0:T(8,128)(2,1)S(1)} %collective-permute-done.5.refs_3_), channel_id=1, source_target_pairs={{0,3},{1,0},{2,1},{3,2},{4,7},{5,4},{6,5},{7,6},{8,11},{9,8},{10,9... | collective-permute-start | bytes 1572872 | tf_op jit(solution)/shard_map/ppermute | solution.py:453
  60.5 3.8 %copy-start.2 = (bf16[1,128,2048]{2,1,0:T(8,128)(2,1)S(1)}, bf16[1,128,2048]{2,1,0:T(8,128)(2,1)}, u32[]{:S(2)}) copy-start(bf16[1,128,2048]{2,1,0:T(8,128)(2,1)} %copy-done.1) | copy-start | bytes 1572868
  60.6 3.8 %copy-start.4 = (bf16[1,128,2048]{2,1,0:T(8,128)(2,1)S(1)}, bf16[1,128,2048]{2,1,0:T(8,128)(2,1)}, u32[]{:S(2)}) copy-start(bf16[1,128,2048]{2,1,0:T(8,128)(2,1)} %copy-done.3) | copy-start | bytes 1572868
  60.6 3.8 %copy-start.6 = (bf16[1,128,2048]{2,1,0:T(8,128)(2,1)S(1)}, bf16[1,128,2048]{2,1,0:T(8,128)(2,1)}, u32[]{:S(2)}) copy-start(bf16[1,128,2048]{2,1,0:T(8,128)(2,1)} %copy-done.5) | copy-start | bytes 1572868
  64.4 7.5 %copy-start.8 = (bf16[1,128,2048]{2,1,0:T(8,128)(2,1)S(1)}, bf16[1,128,2048]{2,1,0:T(8,128)(2,1)}, u32[]{:S(2)}) copy-start(bf16[1,128,2048]{2,1,0:T(8,128)(2,1)} %copy-done.7) | copy-start | bytes 1572868
  76.8 17.4 %collective-permute-start.21 = (bf16[4,128,128]{2,1,0:T(8,128)(2,1)S(1)}, bf16[4,128,128]{2,1,0:T(8,128)(2,1)S(1)}, u32[]{:S(2)}, u32[]{:S(2)}) collective-permute-start(bf16[4,128,128]{2,1,0:T(8,128)(2,1)S(1)} %get-tuple-element.86), channel_id=1, source_target_pairs={{0,4},{4,0},{8,12},{12,8},{16,20},{20,16},{24,28},{28,24},{32,36},... | collective-permute-start | bytes 393224 | tf_op jit(solution)/shard_map/ppermute | solution.py:418
  94.1 4.1 %collective-permute-start.8 = (bf16[4,128,128]{2,1,0:T(8,128)(2,1)S(1)}, bf16[4,128,128]{2,1,0:T(8,128)(2,1)S(1)}, u32[]{:S(2)}, u32[]{:S(2)}) collective-permute-start(bf16[4,128,128]{2,1,0:T(8,128)(2,1)S(1)} %get-tuple-element.65), channel_id=1, source_target_pairs={{0,4},{4,0},{8,12},{12,8},{16,20},{20,16},{24,28},{28,24},{32,36},... | collective-permute-start | bytes 393224 | tf_op jit(solution)/shard_map/ppermute | solution.py:418
  94.2 6.6 %collective-permute-start.22 = (bf16[2,128,128]{2,1,0:T(8,128)(2,1)S(1)}, bf16[2,128,128]{2,1,0:T(8,128)(2,1)S(1)}, u32[]{:S(2)}, u32[]{:S(2)}) collective-permute-start(bf16[2,128,128]{2,1,0:T(8,128)(2,1)S(1)} %get-tuple-element.89), channel_id=1, source_target_pairs={{0,8},{4,12},{8,0},{12,4},{16,24},{20,28},{24,16},{28,20},{32,40},... | collective-permute-start | bytes 196616 | tf_op jit(solution)/shard_map/ppermute | solution.py:418
  95.5 5.8 %collective-permute-start.23 = (bf16[2,128,128]{2,1,0:T(8,128)(2,1)S(1)}, bf16[2,128,128]{2,1,0:T(8,128)(2,1)S(1)}, u32[]{:S(2)}, u32[]{:S(2)}) collective-permute-start(bf16[2,128,128]{2,1,0:T(8,128)(2,1)S(1)} %get-tuple-element.89), channel_id=1, source_target_pairs={{0,16},{4,20},{8,24},{12,28},{16,0},{20,4},{24,8},{28,12},{32,48},... | collective-permute-start | bytes 196616 | tf_op jit(solution)/shard_map/ppermute | solution.py:418
  98.0 5.5 %collective-permute-start.24 = (bf16[2,128,128]{2,1,0:T(8,128)(2,1)S(1)}, bf16[2,128,128]{2,1,0:T(8,128)(2,1)S(1)}, u32[]{:S(2)}, u32[]{:S(2)}) collective-permute-start(bf16[2,128,128]{2,1,0:T(8,128)(2,1)S(1)} %get-tuple-element.89), channel_id=1, source_target_pairs={{0,24},{4,28},{8,16},{12,20},{16,8},{20,12},{24,0},{28,4},{32,56},... | collective-permute-start | bytes 196616 | tf_op jit(solution)/shard_map/ppermute | solution.py:418
  98.2 9.3 %collective-permute-start.10 = (bf16[2,128,128]{2,1,0:T(8,128)(2,1)S(1)}, bf16[2,128,128]{2,1,0:T(8,128)(2,1)S(1)}, u32[]{:S(2)}, u32[]{:S(2)}) collective-permute-start(bf16[2,128,128]{2,1,0:T(8,128)(2,1)S(1)} %get-tuple-element.68), channel_id=1, source_target_pairs={{0,16},{4,20},{8,24},{12,28},{16,0},{20,4},{24,8},{28,12},{32,48},... | collective-permute-start | bytes 196616 | tf_op jit(solution)/shard_map/ppermute | solution.py:418
  99.8 7.7 %collective-permute-start.11 = (bf16[2,128,128]{2,1,0:T(8,128)(2,1)S(1)}, bf16[2,128,128]{2,1,0:T(8,128)(2,1)S(1)}, u32[]{:S(2)}, u32[]{:S(2)}) collective-permute-start(bf16[2,128,128]{2,1,0:T(8,128)(2,1)S(1)} %get-tuple-element.68), channel_id=1, source_target_pairs={{0,24},{4,28},{8,16},{12,20},{16,8},{20,12},{24,0},{28,4},{32,56},... | collective-permute-start | bytes 196616 | tf_op jit(solution)/shard_map/ppermute | solution.py:418
  100.9 6.7 %collective-permute-start.9 = (bf16[2,128,128]{2,1,0:T(8,128)(2,1)S(1)}, bf16[2,128,128]{2,1,0:T(8,128)(2,1)S(1)}, u32[]{:S(2)}, u32[]{:S(2)}) collective-permute-start(bf16[2,128,128]{2,1,0:T(8,128)(2,1)S(1)} %get-tuple-element.68), channel_id=1, source_target_pairs={{0,8},{4,12},{8,0},{12,4},{16,24},{20,28},{24,16},{28,20},{32,40},... | collective-permute-start | bytes 196616 | tf_op jit(solution)/shard_map/ppermute | solution.py:418
  103.6 8.0 %collective-permute-start.26 = (bf16[2,128,128]{2,1,0:T(8,128)(2,1)S(1)}, bf16[2,128,128]{2,1,0:T(8,128)(2,1)S(1)}, u32[]{:S(2)}, u32[]{:S(2)}) collective-permute-start(bf16[2,128,128]{2,1,0:T(8,128)(2,1)S(1)} %get-tuple-element.92), channel_id=1, source_target_pairs={{0,32},{4,36},{8,40},{12,44},{16,48},{20,52},{24,56},{28,60},{32,0... | collective-permute-start | bytes 196616 | tf_op jit(solution)/shard_map/ppermute | solution.py:418
  104.9 6.7 %collective-permute-start.27 = (bf16[2,128,128]{2,1,0:T(8,128)(2,1)S(1)}, bf16[2,128,128]{2,1,0:T(8,128)(2,1)S(1)}, u32[]{:S(2)}, u32[]{:S(2)}) collective-permute-start(bf16[2,128,128]{2,1,0:T(8,128)(2,1)S(1)} %get-tuple-element.92), channel_id=1, source_target_pairs={{0,64},{4,68},{8,72},{12,76},{16,80},{20,84},{24,88},{28,92},{32,9... | collective-permute-start | bytes 196616 | tf_op jit(solution)/shard_map/ppermute | solution.py:418
  107.6 7.8 %collective-permute-start.28 = (bf16[2,128,128]{2,1,0:T(8,128)(2,1)S(1)}, bf16[2,128,128]{2,1,0:T(8,128)(2,1)S(1)}, u32[]{:S(2)}, u32[]{:S(2)}) collective-permute-start(bf16[2,128,128]{2,1,0:T(8,128)(2,1)S(1)} %get-tuple-element.92), channel_id=1, source_target_pairs={{0,96},{4,100},{8,104},{12,108},{16,112},{20,116},{24,120},{28,124... | collective-permute-start | bytes 196616 | tf_op jit(solution)/shard_map/ppermute | solution.py:418
  107.6 8.2 %collective-permute-start.13 = (bf16[2,128,128]{2,1,0:T(8,128)(2,1)S(1)}, bf16[2,128,128]{2,1,0:T(8,128)(2,1)S(1)}, u32[]{:S(2)}, u32[]{:S(2)}) collective-permute-start(bf16[2,128,128]{2,1,0:T(8,128)(2,1)S(1)} %get-tuple-element.71), channel_id=1, source_target_pairs={{0,32},{4,36},{8,40},{12,44},{16,48},{20,52},{24,56},{28,60},{32,0... | collective-permute-start | bytes 196616 | tf_op jit(solution)/shard_map/ppermute | solution.py:418
  107.7 8.3 %collective-permute-start.14 = (bf16[2,128,128]{2,1,0:T(8,128)(2,1)S(1)}, bf16[2,128,128]{2,1,0:T(8,128)(2,1)S(1)}, u32[]{:S(2)}, u32[]{:S(2)}) collective-permute-start(bf16[2,128,128]{2,1,0:T(8,128)(2,1)S(1)} %get-tuple-element.71), channel_id=1, source_target_pairs={{0,64},{4,68},{8,72},{12,76},{16,80},{20,84},{24,88},{28,92},{32,9... | collective-permute-start | bytes 196616 | tf_op jit(solution)/shard_map/ppermute | solution.py:418
  111.6 4.4 %collective-permute-start.15 = (bf16[2,128,128]{2,1,0:T(8,128)(2,1)S(1)}, bf16[2,128,128]{2,1,0:T(8,128)(2,1)S(1)}, u32[]{:S(2)}, u32[]{:S(2)}) collective-permute-start(bf16[2,128,128]{2,1,0:T(8,128)(2,1)S(1)} %get-tuple-element.71), channel_id=1, source_target_pairs={{0,96},{4,100},{8,104},{12,108},{16,112},{20,116},{24,120},{28,124... | collective-permute-start | bytes 196616 | tf_op jit(solution)/shard_map/ppermute | solution.py:418
  111.6 9.4 %collective-permute-start.25 = (bf16[2,2,128,128]{3,2,1,0:T(8,128)(2,1)S(1)}, bf16[2,2,128,128]{3,2,1,0:T(8,128)(2,1)S(1)}, u32[]{:S(2)}, u32[]{:S(2)}) collective-permute-start(bf16[2,2,128,128]{3,2,1,0:T(8,128)(2,1)S(1)} %get-tuple-element.90.refs_17_), channel_id=1, source_target_pairs={{0,4},{4,0},{8,12},{12,8},{16,20},{20,16},{24,28},{28,24},{32,36},... | collective-permute-start | bytes 393224 | tf_op jit(solution)/shard_map/ppermute | solution.py:418
  115.4 9.0 %collective-permute-start.29 = (bf16[2,2,128,128]{3,2,1,0:T(8,128)(2,1)S(1)}, bf16[2,2,128,128]{3,2,1,0:T(8,128)(2,1)S(1)}, u32[]{:S(2)}, u32[]{:S(2)}) collective-permute-start(bf16[2,2,128,128]{3,2,1,0:T(8,128)(2,1)S(1)} %shard_map.78.refs_9_), channel_id=1, source_target_pairs={{0,4},{4,0},{8,12},{12,8},{16,20},{20,16},{24,28},{28,24},{32,36},... | collective-permute-start | bytes 393224 | tf_op jit(solution)/shard_map/ppermute | solution.py:418
  115.9 12.4 %collective-permute-start.12 = (bf16[2,2,128,128]{3,2,1,0:T(8,128)(2,1)S(1)}, bf16[2,2,128,128]{3,2,1,0:T(8,128)(2,1)S(1)}, u32[]{:S(2)}, u32[]{:S(2)}) collective-permute-start(bf16[2,2,128,128]{3,2,1,0:T(8,128)(2,1)S(1)} %get-tuple-element.69.refs_17_), channel_id=1, source_target_pairs={{0,4},{4,0},{8,12},{12,8},{16,20},{20,16},{24,28},{28,24},{32,36},... | collective-permute-start | bytes 393224 | tf_op jit(solution)/shard_map/ppermute | solution.py:418
  116.0 15.8 %collective-permute-start.16 = (bf16[2,2,128,128]{3,2,1,0:T(8,128)(2,1)S(1)}, bf16[2,2,128,128]{3,2,1,0:T(8,128)(2,1)S(1)}, u32[]{:S(2)}, u32[]{:S(2)}) collective-permute-start(bf16[2,2,128,128]{3,2,1,0:T(8,128)(2,1)S(1)} %shard_map.71.refs_9_), channel_id=1, source_target_pairs={{0,4},{4,0},{8,12},{12,8},{16,20},{20,16},{24,28},{28,24},{32,36},... | collective-permute-start | bytes 393224 | tf_op jit(solution)/shard_map/ppermute | solution.py:418
  120.9 1.7 %copy-start.9 = (s32[2]{0:T(128)S(1)}, s32[2]{0:T(128)}, u32[]{:S(2)}) copy-start(s32[2]{0:T(128)} %lengths_ref.7) | copy-start | bytes 28

commit v3 on v2

--- a/solution.py
+++ b/solution.py
@@ -296,35 +296,67 @@
     return body
 
 
-def last_kernel(picks, half_heads, seq, first_level, mine):
+def finish_half(lengths_ref, refs, picks, half_heads, seq, first_level, half, done):
+    qs, wts = refs[0:4], refs[4:8]
+    part_ref, level_ref = refs[8:10]
+    limit = lengths_ref[seq] - lax.axis_index("seq") * (4 * ROWS)
+    levels = range(first_level, first_level + level_ref.shape[0])
+    lane = lax.broadcasted_iota(jnp.int32, (1, ROWS), 1)
+    for j in range(half_heads):
+        head = half * half_heads + j
+        rows = pl.ds(pl.multiple_of(head * 128, 128), 128)
+        mats = jnp.concatenate([level_ref[i, j] for i in range(len(levels))], axis=1)
+        for r in range(4):
+            place = place_of(r)
+            scaled = scaled_levels(qs[r][picks[r], rows, :], wts[r], picks[r], head, levels)
+            acc = part_ref[r, rows, :] + jnp.dot(mats, scaled, preferred_element_type=F32)
+            scale = lax.rsqrt(jnp.mean(acc * acc, 0, keepdims=True) + 1e-06)
+            valid = place * ROWS + lane < limit
+            acc = acc * jnp.where(valid, scale, 0.0)
+            done(j, r, place, acc.astype(BF16).T)
+
+
+def mine_kernel(picks, half_heads, seq, first_level):
     def body(lengths_ref, *refs):
-        qs, wts = refs[0:4], refs[4:8]
-        part_ref, level_ref = refs[8:10]
-        out_ref, buf, sem = refs[-3:]
+        out_ref = refs[-1]
+
+        def done(j, r, place, rows):
+            out_ref[j, place] = rows
+
         core = lax.axis_index("seq") % 2
-        half = core if mine else 1 - core
-        limit = lengths_ref[seq] - lax.axis_index("seq") * (4 * ROWS)
-        levels = range(first_level, first_level + level_ref.shape[0])
-        lane = lax.broadcasted_iota(jnp.int32, (1, ROWS), 1)
+        finish_half(lengths_ref, refs, picks, half_heads, seq, first_level, core, done)
+
+    return body
+
+
+def last_kernel(picks, half_heads, seq, first_level):
+    def body(lengths_ref, *refs):
+        mine_ref = refs[10]
+        out_ref, buf, sem, mine_sem = refs[-4:]
+        core = lax.axis_index("seq") % 2
         copies = []
+
+        def lanes(half, j):
+            return pl.ds(pl.multiple_of((half * half_heads + j) * 128, 128), 128)
+
         for j in range(half_heads):
-            head = half * half_heads + j
-            rows = pl.ds(pl.multiple_of(head * 128, 128), 128)
-            mats = jnp.concatenate([level_ref[i, j] for i in range(len(levels))], axis=1)
-            for r in range(4):
-                place = place_of(r)
-                scaled = scaled_levels(
-                    qs[r][picks[r], rows, :], wts[r], picks[r], head, levels
+            copies.append(
+                pltpu.make_async_copy(
+                    mine_ref.at[j], out_ref.at[seq, :, :, lanes(core, j)], mine_sem.at[j]
                 )
-                acc = part_ref[r, rows, :] + jnp.dot(mats, scaled, preferred_element_type=F32)
-                scale = lax.rsqrt(jnp.mean(acc * acc, 0, keepdims=True) + 1e-06)
-                valid = place * ROWS + lane < limit
-                acc = acc * jnp.where(valid, scale, 0.0)
-                buf[j, place] = acc.astype(BF16).T
-            copies.append(
-                pltpu.make_async_copy(buf.at[j], out_ref.at[seq, :, :, rows], sem.at[j])
             )
             copies[-1].start()
+
+        def done(j, r, place, rows):
+            buf[j, r] = rows
+            copies.append(
+                pltpu.make_async_copy(
+                    buf.at[j, r], out_ref.at[seq, place, :, lanes(1 - core, j)], sem.at[j, r]
+                )
+            )
+            copies[-1].start()
+
+        finish_half(lengths_ref, refs, picks, half_heads, seq, first_level, 1 - core, done)
         for copy in copies:
             copy.wait()
 
@@ -348,29 +380,39 @@
         compiler_params=pltpu.CompilerParams(vmem_limit_bytes=4 << 20),
         name="far_part",
     )(*args)
-    out = out_prev
-    for mine, levels in ((True, y_levels), (False, y_other)):
-        args = [lengths] + columns[0] + columns[3] + [in_vmem(part), in_vmem(levels)]
-        in_specs = [pl.BlockSpec(memory_space=pltpu.SMEM)] + [vmem] * (len(args) - 1)
-        aliases = {}
-        if out is not None:
-            in_specs.append(pl.BlockSpec(memory_space=pl.ANY))
-            args.append(out)
-            aliases = {len(args) - 1: 0}
-        out = pl.pallas_call(
-            last_kernel(picks, half_heads, seq, 12 + x_levels.shape[0], mine),
-            in_specs=in_specs,
-            out_specs=pl.BlockSpec(memory_space=pl.ANY),
-            out_shape=jax.ShapeDtypeStruct((seqs, 4, ROWS, heads * 128), BF16),
-            scratch_shapes=[
-                pltpu.VMEM((half_heads, 4, ROWS, 128), BF16),
-                pltpu.SemaphoreType.DMA((half_heads,)),
-            ],
-            input_output_aliases=aliases,
-            compiler_params=pltpu.CompilerParams(vmem_limit_bytes=6 << 20),
-            name="far_last",
-        )(*args)
-    return out
+    first_level = 12 + x_levels.shape[0]
+    smem = pl.BlockSpec(memory_space=pltpu.SMEM)
+    half_shape = (half_heads, 4, ROWS, 128)
+    args = [lengths] + columns[0] + columns[3] + [in_vmem(part), in_vmem(y_levels)]
+    mine = pl.pallas_call(
+        mine_kernel(picks, half_heads, seq, first_level),
+        in_specs=[smem] + [vmem] * (len(args) - 1),
+        out_specs=vmem,
+        out_shape=pltpu.VMEM(half_shape, BF16),
+        compiler_params=pltpu.CompilerParams(vmem_limit_bytes=4 << 20),
+        name="far_mine",
+    )(*args)
+    args = args[:-1] + [in_vmem(y_other), in_vmem(mine)]
+    in_specs = [smem] + [vmem] * (len(args) - 1)
+    aliases = {}
+    if out_prev is not None:
+        in_specs.append(pl.BlockSpec(memory_space=pl.ANY))
+        args.append(out_prev)
+        aliases = {len(args) - 1: 0}
+    return pl.pallas_call(
+        last_kernel(picks, half_heads, seq, first_level),
+        in_specs=in_specs,
+        out_specs=pl.BlockSpec(memory_space=pl.ANY),
+        out_shape=jax.ShapeDtypeStruct((seqs, 4, ROWS, heads * 128), BF16),
+        scratch_shapes=[
+            pltpu.VMEM(half_shape, BF16),
+            pltpu.SemaphoreType.DMA((half_heads, 4)),
+            pltpu.SemaphoreType.DMA((half_heads,)),
+        ],
+        input_output_aliases=aliases,
+        compiler_params=pltpu.CompilerParams(vmem_limit_bytes=6 << 20),
+        name="far_last",
+    )(*args)
 
 
 def small_call(body, outs, *args):

time: 134 us -> 133 us (level)
  no operation moved by 1% of the time
where the time goes in v3:
time: 133 us; the launch traced here: 132 us
  Pallas kernels  47.8 us (36%)
  starting transfers between devices  43.2 us (32%)
  waiting for transfers between devices  35.5 us (27%)
  local copies, waits for them, and re-layouts  4.92 us (4%)
    pallas_call x15, Pallas kernels, vmem_call(): pl.pallas_call(body, grid=(steps,), in_specs=[pl.BlockSpec(memory_space=p...  32.7 us
    ppermute x18, starting transfers between devices, swap(): return lax.ppermute(value, 'seq', [(i, i ^ mask) for i in range(size)])  27.3 us
    ppermute x2, waiting for transfers between devices, on_device(): a_low = lax.ppermute(low, 'head', up)  18.1 us
    ppermute x2, waiting for transfers between devices, on_device(): c = lax.ppermute(a_low, 'head', up)  8.17 us
    ppermute x2, waiting for transfers between devices, on_device(): a_high = lax.ppermute(high, 'head', up)  6.99 us
    pallas_call x1, Pallas kernels, fold_gain(): pl.pallas_call(fold_kernel, grid=(width // ROWS,), in_specs=[pl.BlockSpec...  5.89 us
    ppermute x2, starting transfers between devices, on_device(): a_low = lax.ppermute(low, 'head', up)  3.86 us
    ppermute x2, starting transfers between devices, on_device(): b_low = lax.ppermute(low, 'head', down)  3.85 us
  transfers between devices with their start and end apart: 30, of which 5 were waited for; matrix products, arithmetic and copies ran while one was open for 1% of the time, Pallas kernels for 35%

profile of v3, /device:TPU:1, one launch (start us, length us, event | category | flops | bytes accessed | tf_op | source)
XLA Modules:
  0.0 132.5 jit_solution(362173409528035123)
XLA Ops:
  0.0 1.4 %fusion.7 = (bf16[1,128,2048]{2,1,0:T(8,128)(2,1)S(1)}, bf16[1,128,2048]{2,1,0:T(8,128)(2,1)S(1)}) fusion(bf16[2,256,2048]{2,1,0:T(8,128)(2,1)} %refs_0_.3), kind=kLoop, calls=%fused_computation.8 | loop fusion | bytes 2097152 | tf_op jit(solution)/shard_map/slice | solution.py:487
  1.4 2.5 %collective-permute-start = (bf16[1,128,2048]{2,1,0:T(8,128)(2,1)S(1)}, bf16[1,128,2048]{2,1,0:T(8,128)(2,1)S(1)}, u32[]{:S(2)}, u32[]{:S(2)}) collective-permute-start(bf16[1,128,2048]{2,1,0:T(8,128)(2,1)S(1)} %get-tuple-element.96), channel_id=1, source_target_pairs={{0,1},{1,2},{2,3},{3,0},{4,5},{5,6},{6,7},{7,4},{8,9},{9,10},{10,1... | collective-permute-start | bytes 1572872 | tf_op jit(solution)/shard_map/ppermute | solution.py:488
  4.0 2.2 %collective-permute-start.1 = (bf16[1,128,2048]{2,1,0:T(8,128)(2,1)S(1)}, bf16[1,128,2048]{2,1,0:T(8,128)(2,1)}, u32[]{:S(2)}, u32[]{:S(2)}) collective-permute-start(bf16[1,128,2048]{2,1,0:T(8,128)(2,1)S(1)} %get-tuple-element.95), channel_id=1, source_target_pairs={{0,3},{1,0},{2,1},{3,2},{4,7},{5,4},{6,5},{7,6},{8,11},{9,8},{10,9... | collective-permute-start | bytes 1572872 | tf_op jit(solution)/shard_map/ppermute | solution.py:489
  6.2 0.0 collective-permute-start.17
  6.2 2.7 %collective-permute-start.18 = (bf16[1,128,2048]{2,1,0:T(8,128)(2,1)S(1)}, bf16[1,128,2048]{2,1,0:T(8,128)(2,1)S(1)}, u32[]{:S(2)}, u32[]{:S(2)}) collective-permute-start(bf16[1,128,2048]{2,1,0:T(8,128)(2,1)S(1)} %get-tuple-element.96), channel_id=1, source_target_pairs={{0,3},{1,0},{2,1},{3,2},{4,7},{5,4},{6,5},{7,6},{8,11},{9,8},{10,9... | collective-permute-start | bytes 1572872 | tf_op jit(solution)/shard_map/ppermute | solution.py:491
  8.8 8.9 %collective-permute-done.refs_0_ = bf16[1,128,2048]{2,1,0:T(8,128)(2,1)S(1)} collective-permute-done((bf16[1,128,2048]{2,1,0:T(8,128)(2,1)S(1)}, bf16[1,128,2048]{2,1,0:T(8,128)(2,1)S(1)}, u32[]{:S(2)}, u32[]{:S(2)}) %collective-permute-start) | collective-permute-done | bytes 524320 | tf_op jit(solution)/shard_map/ppermute | solution.py:488
  17.7 0.0 collective-permute-done.1.refs_3_
  17.7 0.5 collective-permute-start.19
  18.2 1.0 fusion.6
  19.3 1.3 %collective-permute-start.2 = (bf16[1,128,2048]{2,1,0:T(8,128)(2,1)}, bf16[1,128,2048]{2,1,0:T(8,128)(2,1)S(1)}, u32[]{:S(2)}, u32[]{:S(2)}) collective-permute-start(bf16[1,128,2048]{2,1,0:T(8,128)(2,1)} %get-tuple-element.94), channel_id=1, source_target_pairs={{0,1},{1,2},{2,3},{3,0},{4,5},{5,6},{6,7},{7,4},{8,9},{9,10},{10,1... | collective-permute-start | bytes 1572872 | tf_op jit(solution)/shard_map/ppermute | solution.py:488
  20.6 1.3 %collective-permute-start.5 = (bf16[1,128,2048]{2,1,0:T(8,128)(2,1)}, bf16[1,128,2048]{2,1,0:T(8,128)(2,1)S(1)}, u32[]{:S(2)}, u32[]{:S(2)}) collective-permute-start(bf16[1,128,2048]{2,1,0:T(8,128)(2,1)} %get-tuple-element.93), channel_id=1, source_target_pairs={{0,3},{1,0},{2,1},{3,2},{4,7},{5,4},{6,5},{7,6},{8,11},{9,8},{10,9... | collective-permute-start | bytes 1572872 | tf_op jit(solution)/shard_map/ppermute | solution.py:489
  22.0 7.0 %collective-permute-done.17.refs_1_ = bf16[1,128,2048]{2,1,0:T(8,128)(2,1)S(1)} collective-permute-done((bf16[1,128,2048]{2,1,0:T(8,128)(2,1)S(1)}, bf16[1,128,2048]{2,1,0:T(8,128)(2,1)S(1)}, u32[]{:S(2)}, u32[]{:S(2)}) %collective-permute-start.17) | collective-permute-done | bytes 524320 | tf_op jit(solution)/shard_map/ppermute | solution.py:490
  28.9 0.8 copy-done.3
  29.7 1.2 collective-permute-start.20
  30.9 0.0 collective-permute-done.18.refs_2_
  30.9 0.8 copy-done.5
  31.7 0.3 collective-permute-start.3
  32.0 8.2 %collective-permute-done.19.refs_0_ = bf16[1,128,2048]{2,1,0:T(8,128)(2,1)S(1)} collective-permute-done((bf16[1,128,2048]{2,1,0:T(8,128)(2,1)S(1)}, bf16[1,128,2048]{2,1,0:T(8,128)(2,1)S(1)}, u32[]{:S(2)}, u32[]{:S(2)}) %collective-permute-start.19) | collective-permute-done | bytes 524320 | tf_op jit(solution)/shard_map/ppermute | solution.py:494
  40.2 0.8 copy-done.7
  41.0 1.2 collective-permute-start.4
  42.2 9.2 %collective-permute-done.2.refs_0_ = bf16[1,128,2048]{2,1,0:T(8,128)(2,1)S(1)} collective-permute-done((bf16[1,128,2048]{2,1,0:T(8,128)(2,1)}, bf16[1,128,2048]{2,1,0:T(8,128)(2,1)S(1)}, u32[]{:S(2)}, u32[]{:S(2)}) %collective-permute-start.2) | collective-permute-done | bytes 524320 | tf_op jit(solution)/shard_map/ppermute | solution.py:488
  51.4 0.0 collective-permute-start.6
  51.4 0.0 collective-permute-done.5.refs_3_
  51.4 2.7 %collective-permute-start.7 = (bf16[1,128,2048]{2,1,0:T(8,128)(2,1)S(1)}, bf16[1,128,2048]{2,1,0:T(8,128)(2,1)}, u32[]{:S(2)}, u32[]{:S(2)}) collective-permute-start(bf16[1,128,2048]{2,1,0:T(8,128)(2,1)S(1)} %collective-permute-done.5.refs_3_), channel_id=1, source_target_pairs={{0,3},{1,0},{2,1},{3,2},{4,7},{5,4},{6,5},{7,6},{8,11},{9,8},{10,9... | collective-permute-start | bytes 1572872 | tf_op jit(solution)/shard_map/ppermute | solution.py:495
  54.1 5.9 %fold_gain.1.refs_1_.refs_4_.refs_2_.w_ref = bf16[2048,1536]{1,0:T(8,128)(2,1)S(1)} custom-call(f32[1,2048]{1,0:T(1,128)S(1)} %bitcast.14, bf16[2048,1536]{1,0:T(8,128)(2,1)} %w_ref.1), custom_call_target="tpu_custom_call" | custom-call | tf_op jit(solution)/shard_map/fold_gain/pallas_call | solution.py:33
  60.0 0.5 convolution_bitcast_fusion.refs_2_.refs_5_.refs_3_
  60.6 3.8 %shard_map.72 = (bf16[1,512,256]{2,1,0:T(8,128)(2,1)S(1)}, f32[1,512,256]{2,1,0:T(8,128)S(1)}, f32[1,4,128,128]{3,2,1,0:T(8,128)S(1)}, f32[1,4,24,256]{3,2,1,0:T(8,128)S(1)}) custom-call(bf16[2,256,2048]{2,1,0:T(8,128)(2,1)S(1)} %copy-done, bf16[2048,1536]{1,0:T(8,128)(2,1)S(1)} %fold_gain.1.refs_1_.refs_4_.refs_2_.w_ref, ...), custom_call_target="tpu_custom_call" | custom-call | tf_op jit(solution)/shard_map/pallas_call | solution.py:204
  64.4 7.4 %shard_map.73 = (bf16[2,512,256]{2,1,0:T(8,128)(2,1)S(1)}, f32[2,512,256]{2,1,0:T(8,128)S(1)}, f32[2,4,128,128]{3,2,1,0:T(8,128)S(1)}, f32[2,4,24,256]{3,2,1,0:T(8,128)S(1)}) custom-call(bf16[1,128,2048]{2,1,0:T(8,128)(2,1)S(1)} %copy-done.2, bf16[1,128,2048]{2,1,0:T(8,128)(2,1)S(1)} %copy-done.4, bf16[1,128,2048]{2,1,0:T(8,128)(2,1)S(1)} %copy-done.6, ...), custom_call_target="tpu_custom_call" | custom-call | tf_op jit(solution)/shard_map/pallas_call | solution.py:204
  71.9 0.0 collective-permute-done.20.refs_1_
  71.9 4.8 %shard_map.74 = (bf16[1,512,256]{2,1,0:T(8,128)(2,1)S(1)}, f32[1,512,256]{2,1,0:T(8,128)S(1)}, f32[1,4,128,128]{3,2,1,0:T(8,128)S(1)}, f32[1,4,24,256]{3,2,1,0:T(8,128)S(1)}) custom-call(bf16[1,128,2048]{2,1,0:T(8,128)(2,1)S(1)} %copy-done.8, bf16[1,128,2048]{2,1,0:T(8,128)(2,1)} %collective-permute-done.20.refs_1_, ...), custom_call_target="tpu_custom_call" | custom-call | tf_op jit(solution)/shard_map/pallas_call | solution.py:204
  76.7 0.1 shard_map.75
  76.8 2.9 %collective-permute-start.21 = (bf16[4,128,128]{2,1,0:T(8,128)(2,1)S(1)}, bf16[4,128,128]{2,1,0:T(8,128)(2,1)S(1)}, u32[]{:S(2)}, u32[]{:S(2)}) collective-permute-start(bf16[4,128,128]{2,1,0:T(8,128)(2,1)S(1)} %get-tuple-element.86), channel_id=1, source_target_pairs={{0,4},{4,0},{8,12},{12,8},{16,20},{20,16},{24,28},{28,24},{32,36},... | collective-permute-start | bytes 393224 | tf_op jit(solution)/shard_map/ppermute | solution.py:460
  79.7 3.8 %shard_map.64 = (bf16[1,512,256]{2,1,0:T(8,128)(2,1)S(1)}, f32[1,512,256]{2,1,0:T(8,128)S(1)}, f32[1,4,128,128]{3,2,1,0:T(8,128)S(1)}, f32[1,4,24,256]{3,2,1,0:T(8,128)S(1)}) custom-call(bf16[2,256,2048]{2,1,0:T(8,128)(2,1)S(1)} %copy-done, bf16[2048,1536]{1,0:T(8,128)(2,1)S(1)} %fold_gain.1.refs_1_.refs_4_.refs_2_.w_ref, ...), custom_call_target="tpu_custom_call" | custom-call | tf_op jit(solution)/shard_map/pallas_call | solution.py:204
  83.5 0.0 collective-permute-done.3.refs_1_
  83.5 7.5 %shard_map.65 = (bf16[2,512,256]{2,1,0:T(8,128)(2,1)S(1)}, f32[2,512,256]{2,1,0:T(8,128)S(1)}, f32[2,4,128,128]{3,2,1,0:T(8,128)S(1)}, f32[2,4,24,256]{3,2,1,0:T(8,128)S(1)}) custom-call(bf16[1,128,2048]{2,1,0:T(8,128)(2,1)S(1)} %collective-permute-done.2.refs_0_, bf16[1,128,2048]{2,1,0:T(8,128)(2,1)} %collective-permute-done.3.refs_1_, ...), custom_call_target="tpu_custom_call" | custom-call | tf_op jit(solution)/shard_map/pallas_call | solution.py:204
  91.1 3.0 %shard_map.66 = (f32[1,4,128,128]{3,2,1,0:T(8,128)S(1)}, bf16[4,256,128]{2,1,0:T(8,128)(2,1)S(1)}, bf16[4,128,256]{2,1,0:T(8,128)(2,1)S(1)}, f32[1,4,24,256]{3,2,1,0:T(8,128)S(1)}, bf16[256,2048]{1,0:T(8,128)(2,1)S(1)}) custom-call(bf16[1,128,2048]{2,1,0:T(8,128)(2,1)} %collective-permute-done.6.refs_0_, ...), custom_call_target="tpu_custom_call" | custom-call | tf_op jit(solution)/shard_map/pallas_call | solution.py:204
  94.0 0.1 shard_map.68
  94.1 0.1 collective-permute-start.8
  94.2 0.0 collective-permute-done.21.received_ref.refs_16_
  94.2 1.3 collective-permute-start.22
  95.5 2.5 %collective-permute-start.23 = (bf16[2,128,128]{2,1,0:T(8,128)(2,1)S(1)}, bf16[2,128,128]{2,1,0:T(8,128)(2,1)S(1)}, u32[]{:S(2)}, u32[]{:S(2)}) collective-permute-start(bf16[2,128,128]{2,1,0:T(8,128)(2,1)S(1)} %get-tuple-element.89), channel_id=1, source_target_pairs={{0,16},{4,20},{8,24},{12,28},{16,0},{20,4},{24,8},{28,12},{32,48},... | collective-permute-start | bytes 196616 | tf_op jit(solution)/shard_map/ppermute | solution.py:460
  98.0 0.2 collective-permute-start.24
  98.2 1.6 %collective-permute-start.10 = (bf16[2,128,128]{2,1,0:T(8,128)(2,1)S(1)}, bf16[2,128,128]{2,1,0:T(8,128)(2,1)S(1)}, u32[]{:S(2)}, u32[]{:S(2)}) collective-permute-start(bf16[2,128,128]{2,1,0:T(8,128)(2,1)S(1)} %get-tuple-element.68), channel_id=1, source_target_pairs={{0,16},{4,20},{8,24},{12,28},{16,0},{20,4},{24,8},{28,12},{32,48},... | collective-permute-start | bytes 196616 | tf_op jit(solution)/shard_map/ppermute | solution.py:460
  99.8 1.0 collective-permute-start.11
  100.9 0.5 collective-permute-start.9
  101.4 2.1 %collective-permute-done.24.three_ref = bf16[2,128,128]{2,1,0:T(8,128)(2,1)S(1)} collective-permute-done((bf16[2,128,128]{2,1,0:T(8,128)(2,1)S(1)}, bf16[2,128,128]{2,1,0:T(8,128)(2,1)S(1)}, u32[]{:S(2)}, u32[]{:S(2)}) %collective-permute-start.24) | collective-permute-done | bytes 65568 | tf_op jit(solution)/shard_map/ppermute | solution.py:460
  103.5 0.1 shard_map.77
  103.6 1.4 %collective-permute-start.26 = (bf16[2,128,128]{2,1,0:T(8,128)(2,1)S(1)}, bf16[2,128,128]{2,1,0:T(8,128)(2,1)S(1)}, u32[]{:S(2)}, u32[]{:S(2)}) collective-permute-start(bf16[2,128,128]{2,1,0:T(8,128)(2,1)S(1)} %get-tuple-element.92), channel_id=1, source_target_pairs={{0,32},{4,36},{8,40},{12,44},{16,48},{20,52},{24,56},{28,60},{32,0... | collective-permute-start | bytes 196616 | tf_op jit(solution)/shard_map/ppermute | solution.py:460
  104.9 2.6 %collective-permute-start.27 = (bf16[2,128,128]{2,1,0:T(8,128)(2,1)S(1)}, bf16[2,128,128]{2,1,0:T(8,128)(2,1)S(1)}, u32[]{:S(2)}, u32[]{:S(2)}) collective-permute-start(bf16[2,128,128]{2,1,0:T(8,128)(2,1)S(1)} %get-tuple-element.92), channel_id=1, source_target_pairs={{0,64},{4,68},{8,72},{12,76},{16,80},{20,84},{24,88},{28,92},{32,9... | collective-permute-start | bytes 196616 | tf_op jit(solution)/shard_map/ppermute | solution.py:460
  107.6 0.1 shard_map.70
  107.6 0.1 collective-permute-start.13
  107.7 3.8 %collective-permute-start.14 = (bf16[2,128,128]{2,1,0:T(8,128)(2,1)S(1)}, bf16[2,128,128]{2,1,0:T(8,128)(2,1)S(1)}, u32[]{:S(2)}, u32[]{:S(2)}) collective-permute-start(bf16[2,128,128]{2,1,0:T(8,128)(2,1)S(1)} %get-tuple-element.71), channel_id=1, source_target_pairs={{0,64},{4,68},{8,72},{12,76},{16,80},{20,84},{24,88},{28,92},{32,9... | collective-permute-start | bytes 196616 | tf_op jit(solution)/shard_map/ppermute | solution.py:460
  111.6 0.0 collective-permute-start.15
  111.6 3.8 %collective-permute-start.25 = (bf16[2,2,128,128]{3,2,1,0:T(8,128)(2,1)S(1)}, bf16[2,2,128,128]{3,2,1,0:T(8,128)(2,1)S(1)}, u32[]{:S(2)}, u32[]{:S(2)}) collective-permute-start(bf16[2,2,128,128]{3,2,1,0:T(8,128)(2,1)S(1)} %get-tuple-element.90.refs_17_), channel_id=1, source_target_pairs={{0,4},{4,0},{8,12},{12,8},{16,20},{20,16},{24,28},{28,24},{32,36},... | collective-permute-start | bytes 393224 | tf_op jit(solution)/shard_map/ppermute | solution.py:460
  115.4 0.5 collective-permute-start.29
  115.9 0.1 collective-permute-start.12
  116.0 4.9 %collective-permute-start.16 = (bf16[2,2,128,128]{3,2,1,0:T(8,128)(2,1)S(1)}, bf16[2,2,128,128]{3,2,1,0:T(8,128)(2,1)S(1)}, u32[]{:S(2)}, u32[]{:S(2)}) collective-permute-start(bf16[2,2,128,128]{3,2,1,0:T(8,128)(2,1)S(1)} %shard_map.71.refs_9_), channel_id=1, source_target_pairs={{0,4},{4,0},{8,12},{12,8},{16,20},{20,16},{24,28},{28,24},{32,36},... | collective-permute-start | bytes 393224 | tf_op jit(solution)/shard_map/ppermute | solution.py:460
  120.9 1.7 %far_part.3.refs_8_ = f32[4,512,256]{2,1,0:T(8,128)S(1)} custom-call(bf16[1,512,256]{2,1,0:T(8,128)(2,1)S(1)} %get-tuple-element.72.refs_0_, bf16[2,512,256]{2,1,0:T(8,128)(2,1)S(1)} %get-tuple-element.75.refs_1_.refs_2_, bf16[2,512,256]{2,1,0:T(8,128)(2,1)S(1)} %get-tuple-element.75.refs_1_.refs_2_, bf16[1,512,256]{2,1,0:T(8,128)(2,1)S(1)} %get-tuple-element.76.refs_3_, ...), custom_call_target="tpu_custom_call" | custom-call | tf_op jit(solution)/shard_map/far_part/pallas_call | solution.py:374
  122.7 1.0 far_mine.3.refs_10_
  123.7 1.8 %far_last.2.refs_11_ = bf16[2,4,256,512]{3,2,1,0:T(8,128)(2,1)} custom-call(s32[2]{0:T(128)S(1)} %copy-done.9, bf16[1,512,256]{2,1,0:T(8,128)(2,1)S(1)} %get-tuple-element.72.refs_0_, bf16[2,512,256]{2,1,0:T(8,128)(2,1)S(1)} %get-tuple-element.75.refs_1_.refs_2_, bf16[2,512,256]{2,1,0:T(8,128)(2,1)S(1)} %get-tuple-element.75.refs_1_.refs_2_, ...), custom_call_target="tpu_custom_call" | custom-call | tf_op jit(solution)/shard_map/far_last/pallas_call | solution.py:402
  125.6 2.1 %shard_map.67 = (bf16[1,512,256]{2,1,0:T(8,128)(2,1)S(1)}, f32[1,512,256]{2,1,0:T(8,128)S(1)}) custom-call(bf16[256,2048]{1,0:T(8,128)(2,1)S(1)} %get-tuple-element.52.held, bf16[2048,1536]{1,0:T(8,128)(2,1)S(1)} %fold_gain.1.refs_1_.refs_4_.refs_2_.w_ref, bf16[4,256,128]{2,1,0:T(8,128)(2,1)S(1)} %get-tuple-element.53.k_ref, ...), custom_call_target="tpu_custom_call" | custom-call | tf_op jit(solution)/shard_map/pallas_call | solution.py:204
  127.7 1.7 %far_part.2.refs_8_ = f32[4,512,256]{2,1,0:T(8,128)S(1)} custom-call(bf16[1,512,256]{2,1,0:T(8,128)(2,1)S(1)} %get-tuple-element.49.refs_0_, bf16[2,512,256]{2,1,0:T(8,128)(2,1)S(1)} %get-tuple-element.51.refs_1_.refs_2_, bf16[2,512,256]{2,1,0:T(8,128)(2,1)S(1)} %get-tuple-element.51.refs_1_.refs_2_, bf16[1,512,256]{2,1,0:T(8,128)(2,1)S(1)} %get-tuple-element.56.refs_3_, ...), custom_call_target="tpu_custom_call" | custom-call | tf_op jit(solution)/shard_map/far_part/pallas_call | solution.py:374
  129.4 1.0 far_mine.2.refs_10_
  130.5 1.9 %far_last.3 = bf16[2,4,256,512]{3,2,1,0:T(8,128)(2,1)} custom-call(s32[2]{0:T(128)S(1)} %copy-done.9, bf16[1,512,256]{2,1,0:T(8,128)(2,1)S(1)} %get-tuple-element.49.refs_0_, bf16[2,512,256]{2,1,0:T(8,128)(2,1)S(1)} %get-tuple-element.51.refs_1_.refs_2_, bf16[2,512,256]{2,1,0:T(8,128)(2,1)S(1)} %get-tuple-element.51.refs_1_.refs_2_, ...), custom_call_target="tpu_custom_call", output_to_operand_aliasing={{}: (12, {})} | custom-call | tf_op jit(solution)/shard_map/far_last/pallas_call | solution.py:402
  (49 shorter events, 0.2 us)
Async XLA Ops:
  0.0 18.2 %copy-start = (bf16[2,256,2048]{2,1,0:T(8,128)(2,1)S(1)}, bf16[2,256,2048]{2,1,0:T(8,128)(2,1)}, u32[]{:S(2)}) copy-start(bf16[2,256,2048]{2,1,0:T(8,128)(2,1)} %refs_0_.3) | copy-start | bytes 6291460
  0.0 54.1 %copy-start.11 = (f32[16,4,18]{2,1,0:T(4,128)S(1)}, f32[16,4,18]{2,1,0:T(4,128)}, u32[]{:S(2)}) copy-start(f32[16,4,18]{2,1,0:T(4,128)} %param.9) | copy-start | bytes 13828
  0.0 54.1 %copy-start.12 = (s32[2,1024]{1,0:T(2,128)S(1)}, s32[2,1024]{1,0:T(2,128)}, u32[]{:S(2)}) copy-start(s32[2,1024]{1,0:T(2,128)} %param.10) | copy-start | bytes 24580
  0.0 54.1 %copy-start.10 = (f32[2048]{0:T(1024)S(1)}, f32[2048]{0:T(1024)}, u32[]{:S(2)}) copy-start(f32[2048]{0:T(1024)} %param.7) | copy-start | bytes 24580
  1.4 16.3 %collective-permute-start = (bf16[1,128,2048]{2,1,0:T(8,128)(2,1)S(1)}, bf16[1,128,2048]{2,1,0:T(8,128)(2,1)S(1)}, u32[]{:S(2)}, u32[]{:S(2)}) collective-permute-start(bf16[1,128,2048]{2,1,0:T(8,128)(2,1)S(1)} %get-tuple-element.96), channel_id=1, source_target_pairs={{0,1},{1,2},{2,3},{3,0},{4,5},{5,6},{6,7},{7,4},{8,9},{9,10},{10,1... | collective-permute-start | bytes 1572872 | tf_op jit(solution)/shard_map/ppermute | solution.py:488
  4.0 13.8 %collective-permute-start.1 = (bf16[1,128,2048]{2,1,0:T(8,128)(2,1)S(1)}, bf16[1,128,2048]{2,1,0:T(8,128)(2,1)}, u32[]{:S(2)}, u32[]{:S(2)}) collective-permute-start(bf16[1,128,2048]{2,1,0:T(8,128)(2,1)S(1)} %get-tuple-element.95), channel_id=1, source_target_pairs={{0,3},{1,0},{2,1},{3,2},{4,7},{5,4},{6,5},{7,6},{8,11},{9,8},{10,9... | collective-permute-start | bytes 1572872 | tf_op jit(solution)/shard_map/ppermute | solution.py:489
  6.2 22.8 %collective-permute-start.17 = (bf16[1,128,2048]{2,1,0:T(8,128)(2,1)S(1)}, bf16[1,128,2048]{2,1,0:T(8,128)(2,1)S(1)}, u32[]{:S(2)}, u32[]{:S(2)}) collective-permute-start(bf16[1,128,2048]{2,1,0:T(8,128)(2,1)S(1)} %get-tuple-element.95), channel_id=1, source_target_pairs={{0,1},{1,2},{2,3},{3,0},{4,5},{5,6},{6,7},{7,4},{8,9},{9,10},{10,1... | collective-permute-start | bytes 1572872 | tf_op jit(solution)/shard_map/ppermute | solution.py:490
  6.2 24.8 %collective-permute-start.18 = (bf16[1,128,2048]{2,1,0:T(8,128)(2,1)S(1)}, bf16[1,128,2048]{2,1,0:T(8,128)(2,1)S(1)}, u32[]{:S(2)}, u32[]{:S(2)}) collective-permute-start(bf16[1,128,2048]{2,1,0:T(8,128)(2,1)S(1)} %get-tuple-element.96), channel_id=1, source_target_pairs={{0,3},{1,0},{2,1},{3,2},{4,7},{5,4},{6,5},{7,6},{8,11},{9,8},{10,9... | collective-permute-start | bytes 1572872 | tf_op jit(solution)/shard_map/ppermute | solution.py:491
  17.7 33.7 %copy-start.1 = (bf16[1,128,2048]{2,1,0:T(8,128)(2,1)}, bf16[1,128,2048]{2,1,0:T(8,128)(2,1)S(1)}, u32[]{:S(2)}) copy-start(bf16[1,128,2048]{2,1,0:T(8,128)(2,1)S(1)} %collective-permute-done.refs_0_) | copy-start | bytes 1572868
  17.7 22.5 %collective-permute-start.19 = (bf16[1,128,2048]{2,1,0:T(8,128)(2,1)S(1)}, bf16[1,128,2048]{2,1,0:T(8,128)(2,1)S(1)}, u32[]{:S(2)}, u32[]{:S(2)}) collective-permute-start(bf16[1,128,2048]{2,1,0:T(8,128)(2,1)S(1)} %collective-permute-done.refs_0_), channel_id=1, source_target_pairs={{0,1},{1,2},{2,3},{3,0},{4,5},{5,6},{6,7},{7,4},{8,9},{9,10},{10,1... | collective-permute-start | bytes 1572872 | tf_op jit(solution)/shard_map/ppermute | solution.py:494
  19.3 32.1 %collective-permute-start.2 = (bf16[1,128,2048]{2,1,0:T(8,128)(2,1)}, bf16[1,128,2048]{2,1,0:T(8,128)(2,1)S(1)}, u32[]{:S(2)}, u32[]{:S(2)}) collective-permute-start(bf16[1,128,2048]{2,1,0:T(8,128)(2,1)} %get-tuple-element.94), channel_id=1, source_target_pairs={{0,1},{1,2},{2,3},{3,0},{4,5},{5,6},{6,7},{7,4},{8,9},{9,10},{10,1... | collective-permute-start | bytes 1572872 | tf_op jit(solution)/shard_map/ppermute | solution.py:488
  20.6 30.8 %collective-permute-start.5 = (bf16[1,128,2048]{2,1,0:T(8,128)(2,1)}, bf16[1,128,2048]{2,1,0:T(8,128)(2,1)S(1)}, u32[]{:S(2)}, u32[]{:S(2)}) collective-permute-start(bf16[1,128,2048]{2,1,0:T(8,128)(2,1)} %get-tuple-element.93), channel_id=1, source_target_pairs={{0,3},{1,0},{2,1},{3,2},{4,7},{5,4},{6,5},{7,6},{8,11},{9,8},{10,9... | collective-permute-start | bytes 1572872 | tf_op jit(solution)/shard_map/ppermute | solution.py:489
  28.9 0.8 copy-start.3
  29.7 42.1 %collective-permute-start.20 = (bf16[1,128,2048]{2,1,0:T(8,128)(2,1)}, bf16[1,128,2048]{2,1,0:T(8,128)(2,1)}, u32[]{:S(2)}, u32[]{:S(2)}) collective-permute-start(bf16[1,128,2048]{2,1,0:T(8,128)(2,1)} %collective-permute-done.1.refs_3_), channel_id=1, source_target_pairs={{0,3},{1,0},{2,1},{3,2},{4,7},{5,4},{6,5},{7,6},{8,11},{9,8},{10,9... | collective-permute-start | bytes 1572872 | tf_op jit(solution)/shard_map/ppermute | solution.py:495
  30.9 0.8 copy-start.5
  31.7 51.7 %collective-permute-start.3 = (bf16[1,128,2048]{2,1,0:T(8,128)(2,1)}, bf16[1,128,2048]{2,1,0:T(8,128)(2,1)}, u32[]{:S(2)}, u32[]{:S(2)}) collective-permute-start(bf16[1,128,2048]{2,1,0:T(8,128)(2,1)} %get-tuple-element.93), channel_id=1, source_target_pairs={{0,1},{1,2},{2,3},{3,0},{4,5},{5,6},{6,7},{7,4},{8,9},{9,10},{10,1... | collective-permute-start | bytes 1572872 | tf_op jit(solution)/shard_map/ppermute | solution.py:490
  40.2 0.8 copy-start.7
  41.0 42.5 %collective-permute-start.4 = (bf16[1,128,2048]{2,1,0:T(8,128)(2,1)}, bf16[1,128,2048]{2,1,0:T(8,128)(2,1)}, u32[]{:S(2)}, u32[]{:S(2)}) collective-permute-start(bf16[1,128,2048]{2,1,0:T(8,128)(2,1)} %get-tuple-element.94), channel_id=1, source_target_pairs={{0,3},{1,0},{2,1},{3,2},{4,7},{5,4},{6,5},{7,6},{8,11},{9,8},{10,9... | collective-permute-start | bytes 1572872 | tf_op jit(solution)/shard_map/ppermute | solution.py:491
  51.4 39.6 %collective-permute-start.6 = (bf16[1,128,2048]{2,1,0:T(8,128)(2,1)S(1)}, bf16[1,128,2048]{2,1,0:T(8,128)(2,1)}, u32[]{:S(2)}, u32[]{:S(2)}) collective-permute-start(bf16[1,128,2048]{2,1,0:T(8,128)(2,1)S(1)} %collective-permute-done.2.refs_0_), channel_id=1, source_target_pairs={{0,1},{1,2},{2,3},{3,0},{4,5},{5,6},{6,7},{7,4},{8,9},{9,10},{10,1... | collective-permute-start | bytes 1572872 | tf_op jit(solution)/shard_map/ppermute | solution.py:494
  51.4 39.6 %collective-permute-start.7 = (bf16[1,128,2048]{2,1,0:T(8,128)(2,1)S(1)}, bf16[1,128,2048]{2,1,0:T(8,128)(2,1)}, u32[]{:S(2)}, u32[]{:S(2)}) collective-permute-start(bf16[1,128,2048]{2,1,0:T(8,128)(2,1)S(1)} %collective-permute-done.5.refs_3_), channel_id=1, source_target_pairs={{0,3},{1,0},{2,1},{3,2},{4,7},{5,4},{6,5},{7,6},{8,11},{9,8},{10,9... | collective-permute-start | bytes 1572872 | tf_op jit(solution)/shard_map/ppermute | solution.py:495
  60.5 3.8 %copy-start.2 = (bf16[1,128,2048]{2,1,0:T(8,128)(2,1)S(1)}, bf16[1,128,2048]{2,1,0:T(8,128)(2,1)}, u32[]{:S(2)}) copy-start(bf16[1,128,2048]{2,1,0:T(8,128)(2,1)} %copy-done.1) | copy-start | bytes 1572868
  60.6 3.8 %copy-start.4 = (bf16[1,128,2048]{2,1,0:T(8,128)(2,1)S(1)}, bf16[1,128,2048]{2,1,0:T(8,128)(2,1)}, u32[]{:S(2)}) copy-start(bf16[1,128,2048]{2,1,0:T(8,128)(2,1)} %copy-done.3) | copy-start | bytes 1572868
  60.6 3.8 %copy-start.6 = (bf16[1,128,2048]{2,1,0:T(8,128)(2,1)S(1)}, bf16[1,128,2048]{2,1,0:T(8,128)(2,1)}, u32[]{:S(2)}) copy-start(bf16[1,128,2048]{2,1,0:T(8,128)(2,1)} %copy-done.5) | copy-start | bytes 1572868
  64.4 7.5 %copy-start.8 = (bf16[1,128,2048]{2,1,0:T(8,128)(2,1)S(1)}, bf16[1,128,2048]{2,1,0:T(8,128)(2,1)}, u32[]{:S(2)}) copy-start(bf16[1,128,2048]{2,1,0:T(8,128)(2,1)} %copy-done.7) | copy-start | bytes 1572868
  76.8 17.4 %collective-permute-start.21 = (bf16[4,128,128]{2,1,0:T(8,128)(2,1)S(1)}, bf16[4,128,128]{2,1,0:T(8,128)(2,1)S(1)}, u32[]{:S(2)}, u32[]{:S(2)}) collective-permute-start(bf16[4,128,128]{2,1,0:T(8,128)(2,1)S(1)} %get-tuple-element.86), channel_id=1, source_target_pairs={{0,4},{4,0},{8,12},{12,8},{16,20},{20,16},{24,28},{28,24},{32,36},... | collective-permute-start | bytes 393224 | tf_op jit(solution)/shard_map/ppermute | solution.py:460
  94.1 4.1 %collective-permute-start.8 = (bf16[4,128,128]{2,1,0:T(8,128)(2,1)S(1)}, bf16[4,128,128]{2,1,0:T(8,128)(2,1)S(1)}, u32[]{:S(2)}, u32[]{:S(2)}) collective-permute-start(bf16[4,128,128]{2,1,0:T(8,128)(2,1)S(1)} %get-tuple-element.65), channel_id=1, source_target_pairs={{0,4},{4,0},{8,12},{12,8},{16,20},{20,16},{24,28},{28,24},{32,36},... | collective-permute-start | bytes 393224 | tf_op jit(solution)/shard_map/ppermute | solution.py:460
  94.2 6.6 %collective-permute-start.22 = (bf16[2,128,128]{2,1,0:T(8,128)(2,1)S(1)}, bf16[2,128,128]{2,1,0:T(8,128)(2,1)S(1)}, u32[]{:S(2)}, u32[]{:S(2)}) collective-permute-start(bf16[2,128,128]{2,1,0:T(8,128)(2,1)S(1)} %get-tuple-element.89), channel_id=1, source_target_pairs={{0,8},{4,12},{8,0},{12,4},{16,24},{20,28},{24,16},{28,20},{32,40},... | collective-permute-start | bytes 196616 | tf_op jit(solution)/shard_map/ppermute | solution.py:460
  95.5 5.8 %collective-permute-start.23 = (bf16[2,128,128]{2,1,0:T(8,128)(2,1)S(1)}, bf16[2,128,128]{2,1,0:T(8,128)(2,1)S(1)}, u32[]{:S(2)}, u32[]{:S(2)}) collective-permute-start(bf16[2,128,128]{2,1,0:T(8,128)(2,1)S(1)} %get-tuple-element.89), channel_id=1, source_target_pairs={{0,16},{4,20},{8,24},{12,28},{16,0},{20,4},{24,8},{28,12},{32,48},... | collective-permute-start | bytes 196616 | tf_op jit(solution)/shard_map/ppermute | solution.py:460
  98.0 5.5 %collective-permute-start.24 = (bf16[2,128,128]{2,1,0:T(8,128)(2,1)S(1)}, bf16[2,128,128]{2,1,0:T(8,128)(2,1)S(1)}, u32[]{:S(2)}, u32[]{:S(2)}) collective-permute-start(bf16[2,128,128]{2,1,0:T(8,128)(2,1)S(1)} %get-tuple-element.89), channel_id=1, source_target_pairs={{0,24},{4,28},{8,16},{12,20},{16,8},{20,12},{24,0},{28,4},{32,56},... | collective-permute-start | bytes 196616 | tf_op jit(solution)/shard_map/ppermute | solution.py:460
  98.2 9.3 %collective-permute-start.10 = (bf16[2,128,128]{2,1,0:T(8,128)(2,1)S(1)}, bf16[2,128,128]{2,1,0:T(8,128)(2,1)S(1)}, u32[]{:S(2)}, u32[]{:S(2)}) collective-permute-start(bf16[2,128,128]{2,1,0:T(8,128)(2,1)S(1)} %get-tuple-element.68), channel_id=1, source_target_pairs={{0,16},{4,20},{8,24},{12,28},{16,0},{20,4},{24,8},{28,12},{32,48},... | collective-permute-start | bytes 196616 | tf_op jit(solution)/shard_map/ppermute | solution.py:460
  99.8 7.7 %collective-permute-start.11 = (bf16[2,128,128]{2,1,0:T(8,128)(2,1)S(1)}, bf16[2,128,128]{2,1,0:T(8,128)(2,1)S(1)}, u32[]{:S(2)}, u32[]{:S(2)}) collective-permute-start(bf16[2,128,128]{2,1,0:T(8,128)(2,1)S(1)} %get-tuple-element.68), channel_id=1, source_target_pairs={{0,24},{4,28},{8,16},{12,20},{16,8},{20,12},{24,0},{28,4},{32,56},... | collective-permute-start | bytes 196616 | tf_op jit(solution)/shard_map/ppermute | solution.py:460
  100.9 6.7 %collective-permute-start.9 = (bf16[2,128,128]{2,1,0:T(8,128)(2,1)S(1)}, bf16[2,128,128]{2,1,0:T(8,128)(2,1)S(1)}, u32[]{:S(2)}, u32[]{:S(2)}) collective-permute-start(bf16[2,128,128]{2,1,0:T(8,128)(2,1)S(1)} %get-tuple-element.68), channel_id=1, source_target_pairs={{0,8},{4,12},{8,0},{12,4},{16,24},{20,28},{24,16},{28,20},{32,40},... | collective-permute-start | bytes 196616 | tf_op jit(solution)/shard_map/ppermute | solution.py:460
  103.6 8.0 %collective-permute-start.26 = (bf16[2,128,128]{2,1,0:T(8,128)(2,1)S(1)}, bf16[2,128,128]{2,1,0:T(8,128)(2,1)S(1)}, u32[]{:S(2)}, u32[]{:S(2)}) collective-permute-start(bf16[2,128,128]{2,1,0:T(8,128)(2,1)S(1)} %get-tuple-element.92), channel_id=1, source_target_pairs={{0,32},{4,36},{8,40},{12,44},{16,48},{20,52},{24,56},{28,60},{32,0... | collective-permute-start | bytes 196616 | tf_op jit(solution)/shard_map/ppermute | solution.py:460
  104.9 6.7 %collective-permute-start.27 = (bf16[2,128,128]{2,1,0:T(8,128)(2,1)S(1)}, bf16[2,128,128]{2,1,0:T(8,128)(2,1)S(1)}, u32[]{:S(2)}, u32[]{:S(2)}) collective-permute-start(bf16[2,128,128]{2,1,0:T(8,128)(2,1)S(1)} %get-tuple-element.92), channel_id=1, source_target_pairs={{0,64},{4,68},{8,72},{12,76},{16,80},{20,84},{24,88},{28,92},{32,9... | collective-permute-start | bytes 196616 | tf_op jit(solution)/shard_map/ppermute | solution.py:460
  107.6 7.8 %collective-permute-start.28 = (bf16[2,128,128]{2,1,0:T(8,128)(2,1)S(1)}, bf16[2,128,128]{2,1,0:T(8,128)(2,1)S(1)}, u32[]{:S(2)}, u32[]{:S(2)}) collective-permute-start(bf16[2,128,128]{2,1,0:T(8,128)(2,1)S(1)} %get-tuple-element.92), channel_id=1, source_target_pairs={{0,96},{4,100},{8,104},{12,108},{16,112},{20,116},{24,120},{28,124... | collective-permute-start | bytes 196616 | tf_op jit(solution)/shard_map/ppermute | solution.py:460
  107.6 8.2 %collective-permute-start.13 = (bf16[2,128,128]{2,1,0:T(8,128)(2,1)S(1)}, bf16[2,128,128]{2,1,0:T(8,128)(2,1)S(1)}, u32[]{:S(2)}, u32[]{:S(2)}) collective-permute-start(bf16[2,128,128]{2,1,0:T(8,128)(2,1)S(1)} %get-tuple-element.71), channel_id=1, source_target_pairs={{0,32},{4,36},{8,40},{12,44},{16,48},{20,52},{24,56},{28,60},{32,0... | collective-permute-start | bytes 196616 | tf_op jit(solution)/shard_map/ppermute | solution.py:460
  107.7 8.3 %collective-permute-start.14 = (bf16[2,128,128]{2,1,0:T(8,128)(2,1)S(1)}, bf16[2,128,128]{2,1,0:T(8,128)(2,1)S(1)}, u32[]{:S(2)}, u32[]{:S(2)}) collective-permute-start(bf16[2,128,128]{2,1,0:T(8,128)(2,1)S(1)} %get-tuple-element.71), channel_id=1, source_target_pairs={{0,64},{4,68},{8,72},{12,76},{16,80},{20,84},{24,88},{28,92},{32,9... | collective-permute-start | bytes 196616 | tf_op jit(solution)/shard_map/ppermute | solution.py:460
  111.6 4.4 %collective-permute-start.15 = (bf16[2,128,128]{2,1,0:T(8,128)(2,1)S(1)}, bf16[2,128,128]{2,1,0:T(8,128)(2,1)S(1)}, u32[]{:S(2)}, u32[]{:S(2)}) collective-permute-start(bf16[2,128,128]{2,1,0:T(8,128)(2,1)S(1)} %get-tuple-element.71), channel_id=1, source_target_pairs={{0,96},{4,100},{8,104},{12,108},{16,112},{20,116},{24,120},{28,124... | collective-permute-start | bytes 196616 | tf_op jit(solution)/shard_map/ppermute | solution.py:460
  111.6 9.4 %collective-permute-start.25 = (bf16[2,2,128,128]{3,2,1,0:T(8,128)(2,1)S(1)}, bf16[2,2,128,128]{3,2,1,0:T(8,128)(2,1)S(1)}, u32[]{:S(2)}, u32[]{:S(2)}) collective-permute-start(bf16[2,2,128,128]{3,2,1,0:T(8,128)(2,1)S(1)} %get-tuple-element.90.refs_17_), channel_id=1, source_target_pairs={{0,4},{4,0},{8,12},{12,8},{16,20},{20,16},{24,28},{28,24},{32,36},... | collective-permute-start | bytes 393224 | tf_op jit(solution)/shard_map/ppermute | solution.py:460
  115.4 8.3 %collective-permute-start.29 = (bf16[2,2,128,128]{3,2,1,0:T(8,128)(2,1)S(1)}, bf16[2,2,128,128]{3,2,1,0:T(8,128)(2,1)S(1)}, u32[]{:S(2)}, u32[]{:S(2)}) collective-permute-start(bf16[2,2,128,128]{3,2,1,0:T(8,128)(2,1)S(1)} %shard_map.78.refs_9_), channel_id=1, source_target_pairs={{0,4},{4,0},{8,12},{12,8},{16,20},{20,16},{24,28},{28,24},{32,36},... | collective-permute-start | bytes 393224 | tf_op jit(solution)/shard_map/ppermute | solution.py:460
  115.9 11.8 %collective-permute-start.12 = (bf16[2,2,128,128]{3,2,1,0:T(8,128)(2,1)S(1)}, bf16[2,2,128,128]{3,2,1,0:T(8,128)(2,1)S(1)}, u32[]{:S(2)}, u32[]{:S(2)}) collective-permute-start(bf16[2,2,128,128]{3,2,1,0:T(8,128)(2,1)S(1)} %get-tuple-element.69.refs_17_), channel_id=1, source_target_pairs={{0,4},{4,0},{8,12},{12,8},{16,20},{20,16},{24,28},{28,24},{32,36},... | collective-permute-start | bytes 393224 | tf_op jit(solution)/shard_map/ppermute | solution.py:460
  116.0 14.4 %collective-permute-start.16 = (bf16[2,2,128,128]{3,2,1,0:T(8,128)(2,1)S(1)}, bf16[2,2,128,128]{3,2,1,0:T(8,128)(2,1)S(1)}, u32[]{:S(2)}, u32[]{:S(2)}) collective-permute-start(bf16[2,2,128,128]{3,2,1,0:T(8,128)(2,1)S(1)} %shard_map.71.refs_9_), channel_id=1, source_target_pairs={{0,4},{4,0},{8,12},{12,8},{16,20},{20,16},{24,28},{28,24},{32,36},... | collective-permute-start | bytes 393224 | tf_op jit(solution)/shard_map/ppermute | solution.py:460
  120.9 1.7 %copy-start.9 = (s32[2]{0:T(128)S(1)}, s32[2]{0:T(128)}, u32[]{:S(2)}) copy-start(s32[2]{0:T(128)} %lengths_ref.7) | copy-start | bytes 28

commit v4 on v3

--- a/solution.py
+++ b/solution.py
@@ -48,25 +48,33 @@
     return (lax.axis_index("head") + (0, 3, 1, 2)[relative]) % 4
 
 
-def row_scales(xs, pick, scales):
+def row_scales(xs, blocks, scales):
     sums = []
-    for x_ref in xs:
-        total = jnp.zeros((x_ref.shape[1], TILE), F32)
-        for lane in range(0, x_ref.shape[2], TILE):
-            part = x_ref[pick, :, lane : lane + TILE].astype(F32)
+    for piece, index, first, rows in blocks:
+        total = jnp.zeros((rows, TILE), F32)
+        for lane in range(0, xs[piece].shape[2], TILE):
+            part = xs[piece][index, first : first + rows, lane : lane + TILE].astype(F32)
             total = total + part * part
         sums.append(total)
     sums = jnp.concatenate(sums, axis=0)
     ones = jnp.full((8, TILE), 1.0, F32)
+    width = scales.shape[2]
     for c in range(scales.shape[0]):
         mean = lax.dot_general(
             ones,
-            sums[c * ROWS : (c + 1) * ROWS],
+            sums[c * width : (c + 1) * width],
             NT,
             precision=lax.Precision.HIGHEST,
             preferred_element_type=F32,
         ) * (1.0 / xs[0].shape[2])
         scales[c] = lax.rsqrt(mean + 1e-06)
+
+
+def hold_rows(xs, blocks, held):
+    at = 0
+    for piece, index, first, rows in blocks:
+        held[pl.ds(at, rows), :] = xs[piece][index, first : first + rows]
+        at += rows
 
 
 def columns(w_ref, start, count):
@@ -111,7 +119,7 @@
         near_ref[c, pl.ds(head * 128, 128), :] = near
 
 
-def project_kernel(count, relatives, seq, pick, heads_step, heads):
+def project_kernel(count, relatives, seq, blocks, heads_step, heads):
     chunks = len(relatives)
 
     def body(*refs):
@@ -122,11 +130,8 @@
 
         @pl.when(step == 0)
         def _():
-            at = 0
-            for x_ref in xs:
-                held[pl.ds(at, x_ref.shape[1]), :] = x_ref[pick]
-                at += x_ref.shape[1]
-            row_scales(xs, pick, scales)
+            hold_rows(xs, blocks, held)
+            row_scales(xs, blocks, scales)
 
         x = held[...]
         queries = jnp.dot(
@@ -157,33 +162,42 @@
     return body
 
 
-def keys_kernel(count, relative, seq, heads):
+def keys_kernel(relative, seq, tile, heads):
+    lanes = slice(tile * TILE, (tile + 1) * TILE)
+
     def body(*refs):
-        xs = refs[:count]
-        w_ref, wt_ref = refs[count : count + 2]
-        state_ref, k_ref, v_ref, wt_out, held, scales = refs[count + 2 :]
-        at = 0
-        for x_ref in xs:
-            held[pl.ds(at, x_ref.shape[1]), :] = x_ref[0]
-            at += x_ref.shape[1]
+        xs, (w_ref, wt_ref) = refs[:2], refs[2:4]
+        before_ref = refs[4] if tile else None
+        state_ref, k_ref, v_ref, wt_out, held, scales = refs[-6:]
+        blocks = [(i, 0, 0, x_ref.shape[1]) for i, x_ref in enumerate(xs)]
+        hold_rows(xs, blocks, held)
         kv = jnp.dot(
             held[...], w_ref[:, heads * 128 : heads * 384], preferred_element_type=F32
         )
-        row_scales(xs, 0, scales)
+        row_scales(xs, blocks, scales)
         scale = scales[0, 0:1, :]
-        wt_out[0] = wt_ref[seq, place_of(relative)] * scale
+        wt_out[...] = wt_ref[seq, place_of(relative), :, :, lanes] * scale
         for head in range(heads):
-            k, v = split_keys(kv, scale, slice(0, ROWS), head)
+            k, v = split_keys(kv, scale, slice(0, TILE), head)
             k_ref[head] = k
             v_ref[head] = v
-            state_ref[0, head] = jnp.dot(v, k, preferred_element_type=F32)
+            state = jnp.dot(v, k, preferred_element_type=F32)
+            state_ref[0, head] = state + before_ref[0, head] if tile else state
 
     return body
 
 
 def queries_kernel(heads_step):
-    def body(held, w_ref, k_ref, v_ref, wt_out, q_ref, near_ref):
+    def body(held_a, held_b, w_ref, k_a, k_b, v_a, v_b, wt_a, wt_b, q_ref, near_ref, wt_out, held):
         step = pl.program_id(0)
+
+        @pl.when(step == 0)
+        def _():
+            held[0:TILE, :] = held_a[...]
+            held[TILE:, :] = held_b[...]
+            wt_out[0, :, :, 0:TILE] = wt_a[...]
+            wt_out[0, :, :, TILE:] = wt_b[...]
+
         queries = jnp.dot(
             held[...],
             columns(w_ref, step * (heads_step * 128), heads_step * 128),
@@ -194,7 +208,8 @@
             head = step * heads_step + hh
             q[0, hh] = queries[:, hh * 128 : (hh + 1) * 128].T.astype(BF16)
             q_ref[0, pl.ds(head * 128, 128), :] = q[0, hh]
-            k[0, hh], v[0, hh] = k_ref[head], v_ref[head]
+            k[0, hh] = jnp.concatenate([k_a[head], k_b[head]], axis=0)
+            v[0, hh] = jnp.concatenate([v_a[head], v_b[head]], axis=1)
         near_parts(q, k, v, wt_out, near_ref, step, heads_step)
 
     return body
@@ -212,44 +227,55 @@
     )(*args)
 
 
-def project(xs, seq, relatives, weight, wt, pick=0, states_first=False):
+def project(xs, seq, relatives, weight, wt, blocks):
     chunks = len(relatives)
     width, cols = weight.shape
     heads = cols // 384
     heads_step = 2 if heads % 2 == 0 else 1
-    steps = heads // heads_step
-    weight = in_vmem(weight)
     levels = (chunks, heads, wt.shape[3], ROWS)
     queries, states = (chunks, heads * 128, ROWS), (chunks, heads, 128, 128)
-    held, scales = ((chunks * ROWS, width), BF16), pltpu.VMEM((chunks, 8, ROWS), F32)
-    if states_first:
-        state, k, v, scaled, held = vmem_call(
-            keys_kernel(len(xs), relatives[0], seq, heads),
-            1,
-            [*xs, weight, wt],
-            [
-                (states, F32),
-                ((heads, ROWS, 128), BF16),
-                ((heads, 128, ROWS), BF16),
-                (levels, F32),
-                held,
-            ],
-            [scales],
+    return vmem_call(
+        project_kernel(len(xs), relatives, seq, blocks, heads_step, heads),
+        heads // heads_step,
+        [*xs, in_vmem(weight), wt],
+        [(queries, BF16), (queries, F32), (states, F32), (levels, F32)],
+        [pltpu.VMEM((chunks * ROWS, width), BF16), pltpu.VMEM((chunks, 8, ROWS), F32)],
+    )
+
+
+def project_tiles(tiles, seq, relative, weight, wt):
+    width, cols = weight.shape
+    heads = cols // 384
+    heads_step = 2 if heads % 2 == 0 else 1
+    weight = in_vmem(weight)
+    queries, states = (1, heads * 128, ROWS), (1, heads, 128, 128)
+    made, before = [], []
+    for tile, xs in enumerate(tiles):
+        made.append(
+            vmem_call(
+                keys_kernel(relative, seq, tile, heads),
+                1,
+                [*xs, weight, wt, *before],
+                [
+                    (states, F32),
+                    ((heads, TILE, 128), BF16),
+                    ((heads, 128, TILE), BF16),
+                    ((heads, wt.shape[3], TILE), F32),
+                    ((TILE, width), BF16),
+                ],
+                [pltpu.VMEM((1, 8, TILE), F32)],
+            )
         )
-        q, near = vmem_call(
-            queries_kernel(heads_step),
-            steps,
-            [in_vmem(held), weight, in_vmem(k), in_vmem(v), in_vmem(scaled)],
-            [(queries, BF16), (queries, F32)],
-        )
-        return q, near, state, scaled
-    return vmem_call(
-        project_kernel(len(xs), relatives, seq, pick, heads_step, heads),
-        steps,
-        [*xs, weight, wt],
-        [(queries, BF16), (queries, F32), (states, F32), (levels, F32)],
-        [pltpu.VMEM(*held), scales],
+        before = [in_vmem(made[-1][0])]
+    pairs = [[in_vmem(call[i]) for call in made] for i in (4, 1, 2, 3)]
+    q, near, scaled = vmem_call(
+        queries_kernel(heads_step),
+        heads // heads_step,
+        [*pairs[0], weight, *pairs[1], *pairs[2], *pairs[3]],
+        [(queries, BF16), (queries, F32), ((1, heads, wt.shape[3], ROWS), F32)],
+        [pltpu.VMEM((ROWS, width), BF16)],
     )
+    return q, near, made[-1][0], scaled
 
 
 BEFORE = (1, 3, 0, 2)
@@ -474,7 +500,7 @@
 
 
 def on_device(tokens, norm_gain, projection, level_table, level_index, lengths):
-    seqs, row_count, _ = tokens.shape
+    seqs, row_count, width = tokens.shape
     tables, heads, level_total = level_table.shape
     groups = lax.axis_size("head")
     half = row_count // 2
@@ -484,16 +510,30 @@
     got = []
     held = tokens
     for s in range(seqs):
-        low, high = held[s : s + 1, :half], held[s : s + 1, half:]
+        last = s + 1 == seqs
+        if last:
+            quarters = held[s].reshape(2, 2, half // 2, width)
+            low, high = [quarters[:, i].reshape(1, half, width) for i in range(2)]
+        else:
+            low, high = held[s : s + 1, :half], held[s : s + 1, half:]
         a_low = lax.ppermute(low, "head", up)
         b_high = lax.ppermute(high, "head", down)
         a_high = lax.ppermute(high, "head", up)
         b_low = lax.ppermute(low, "head", down)
-        if s + 1 < seqs:
+        if not last:
             held, a_low, b_high = lax.optimization_barrier((tokens, a_low, b_high))
-        c = lax.ppermute(a_low, "head", up)
-        d = lax.ppermute(b_high, "head", down)
-        got.append(([a_low, a_high, b_low, b_high], [c, d]))
+            far_pieces = [lax.ppermute(a_low, "head", up), lax.ppermute(b_high, "head", down)]
+        else:
+            far_pieces = []
+            for tile in range(2):
+                rows = slice(tile * half // 2, (tile + 1) * half // 2)
+                far_pieces.append(
+                    [
+                        lax.ppermute(a_low[:, rows], "head", up),
+                        lax.ppermute(b_high[:, rows], "head", down),
+                    ]
+                )
+        got.append(([a_low, a_high, b_low, b_high], far_pieces))
 
     level_rows = -(-level_total // 8) * 8
     onehot = (level_index[..., None] == jnp.arange(tables, dtype=jnp.int32)).astype(F32)
@@ -509,11 +549,23 @@
 
     own = []
     for s in range(seqs):
-        own.append(project([tokens], s, [0], weight, wt, s))
+        own.append(project([tokens], s, [0], weight, wt, [(0, s, 0, row_count)]))
     parts = []
     for s in range(seqs):
-        ab = project(got[s][0], s, [1, 2], weight, wt)
-        cd = project(got[s][1], s, [3], weight, wt, states_first=s + 1 == seqs)
+        near_pieces, far_pieces = got[s]
+        if s + 1 < seqs:
+            blocks = [(i, 0, 0, half) for i in range(4)]
+            cd = project(far_pieces, s, [3], weight, wt, blocks[:2])
+        else:
+            quarter = half // 2
+            blocks = [
+                (pair + i, 0, first, quarter)
+                for pair in (0, 2)
+                for first in (0, quarter)
+                for i in range(2)
+            ]
+            cd = project_tiles(far_pieces, s, 3, weight, wt)
+        ab = project(near_pieces, s, [1, 2], weight, wt, blocks)
         parts.append((ab, cd))
 
     out = None

time: 133 us -> 137 us (1.030)
  waiting for transfers between devices: 35.5 us -> 43 us
  Pallas kernels: 47.8 us -> 43.7 us
  starting transfers between devices: 43.2 us -> 45.1 us
  local copies, waits for them, and re-layouts: 4.92 us -> 3.54 us
    ppermute x4 -> x6, waiting for transfers between devices: 8.18 us -> 19.1 us  [the longest x1 19.1 us: on_device(): lax.ppermute(a_low, 'head', up)]
    ppermute x2, waiting for transfers between devices: 6.99 us -> 0.02 us  [on_device(): a_high = lax.ppermute(high, 'head', up)]
    ppermute x2, waiting for transfers between devices: 18.1 us -> 22.9 us  [on_device(): a_low = lax.ppermute(low, 'head', up)]
    pallas_call x15 -> x16, Pallas kernels: 32.7 us -> 28.5 us  [vmem_call(): pl.pallas_call(body, grid=(steps,), in_specs=[pl.BlockSpec(memory_space=p...]
    unnamed x27 -> x11, local copies, waits for them, and re-layouts: 2.44 us -> 0.03 us
    ppermute x2, starting transfers between devices: 3.85 us -> 1.46 us  [on_device(): b_low = lax.ppermute(low, 'head', down)]
    ppermute x4 -> x6, starting transfers between devices: 4.37 us -> 6.68 us  [the longest x2 3.58 us: on_device(): lax.ppermute(b_high[:, rows], 'head', down)]
    ppermute x18, starting transfers between devices: 27.3 us -> 29.4 us  [swap(): return lax.ppermute(value, 'seq', [(i, i ^ mask) for i in range(size)])]
  transfers between devices with their start and end apart: 30 -> 32, of which waited for: 5 -> 6; matrix products, arithmetic and copies ran while one was open for 1% -> 1% of each run, Pallas kernels for 35% -> 31%
where the time goes in v4:
time: 137 us; the launch traced here: 136 us
  starting transfers between devices  45.1 us (33%)
  Pallas kernels  43.7 us (32%)
  waiting for transfers between devices  43 us (31%)
  local copies, waits for them, and re-layouts  3.54 us (3%)
    ppermute x18, starting transfers between devices, swap(): return lax.ppermute(value, 'seq', [(i, i ^ mask) for i in range(size)])  29.4 us
    pallas_call x16, Pallas kernels, vmem_call(): pl.pallas_call(body, grid=(steps,), in_specs=[pl.BlockSpec(memory_space=p...  28.5 us
    ppermute x2, waiting for transfers between devices, on_device(): a_low = lax.ppermute(low, 'head', up)  22.9 us
    ppermute x1, waiting for transfers between devices, on_device(): lax.ppermute(a_low, 'head', up)  19.1 us
    pallas_call x1, Pallas kernels, fold_gain(): pl.pallas_call(fold_kernel, grid=(width // ROWS,), in_specs=[pl.BlockSpec...  5.89 us
    ppermute x2, starting transfers between devices, on_device(): b_high = lax.ppermute(high, 'head', down)  4.46 us
    pallas_call x2, Pallas kernels, far(): pl.pallas_call(last_kernel(picks, half_heads, seq, first_level), in_specs...  3.71 us
    ppermute x2, starting transfers between devices, on_device(): lax.ppermute(b_high[:, rows], 'head', down)  3.58 us
  transfers between devices with their start and end apart: 32, of which 6 were waited for; matrix products, arithmetic and copies ran while one was open for 1% of the time, Pallas kernels for 31%

profile of v4, /device:TPU:1, one launch (start us, length us, event | category | flops | bytes accessed | tf_op | source)
XLA Modules:
  0.0 136.3 jit_solution(17464172014511457524)
XLA Ops:
  0.0 2.4 %fusion.6 = (bf16[1,128,2048]{2,1,0:T(8,128)(2,1)}, bf16[1,128,2048]{2,1,0:T(8,128)(2,1)}) fusion(bf16[2,256,2048]{2,1,0:T(8,128)(2,1)} %refs_0_.3), kind=kLoop, calls=%fused_computation.7 | loop fusion | bytes 2097152 | tf_op jit(solution)/shard_map/slice | solution.py:518
  2.4 2.5 %collective-permute-start = (bf16[1,128,2048]{2,1,0:T(8,128)(2,1)}, bf16[1,128,2048]{2,1,0:T(8,128)(2,1)S(1)}, u32[]{:S(2)}, u32[]{:S(2)}) collective-permute-start(bf16[1,128,2048]{2,1,0:T(8,128)(2,1)} %get-tuple-element.106), channel_id=1, source_target_pairs={{0,1},{1,2},{2,3},{3,0},{4,5},{5,6},{6,7},{7,4},{8,9},{9,10},{10,1... | collective-permute-start | bytes 1572872 | tf_op jit(solution)/shard_map/ppermute | solution.py:519
  4.8 2.2 %collective-permute-start.1 = (bf16[1,128,2048]{2,1,0:T(8,128)(2,1)}, bf16[1,128,2048]{2,1,0:T(8,128)(2,1)S(1)}, u32[]{:S(2)}, u32[]{:S(2)}) collective-permute-start(bf16[1,128,2048]{2,1,0:T(8,128)(2,1)} %get-tuple-element.105), channel_id=1, source_target_pairs={{0,3},{1,0},{2,1},{3,2},{4,7},{5,4},{6,5},{7,6},{8,11},{9,8},{10,9... | collective-permute-start | bytes 1572872 | tf_op jit(solution)/shard_map/ppermute | solution.py:520
  7.0 0.0 collective-permute-start.19
  7.0 11.7 %collective-permute-done.refs_0_ = bf16[1,128,2048]{2,1,0:T(8,128)(2,1)S(1)} collective-permute-done((bf16[1,128,2048]{2,1,0:T(8,128)(2,1)}, bf16[1,128,2048]{2,1,0:T(8,128)(2,1)S(1)}, u32[]{:S(2)}, u32[]{:S(2)}) %collective-permute-start) | collective-permute-done | bytes 524320 | tf_op jit(solution)/shard_map/ppermute | solution.py:519
  18.8 0.0 collective-permute-done.1.refs_3_
  18.8 1.1 fusion.7
  19.8 0.4 collective-permute-start.2
  20.3 2.3 %collective-permute-start.5 = (bf16[1,128,2048]{2,1,0:T(8,128)(2,1)}, bf16[1,128,2048]{2,1,0:T(8,128)(2,1)S(1)}, u32[]{:S(2)}, u32[]{:S(2)}) collective-permute-start(bf16[1,128,2048]{2,1,0:T(8,128)(2,1)} %bitcast.8), channel_id=1, source_target_pairs={{0,3},{1,0},{2,1},{3,2},{4,7},{5,4},{6,5},{7,6},{8,11},{9,8},{10,9... | collective-permute-start | bytes 1572872 | tf_op jit(solution)/shard_map/ppermute | solution.py:520
  22.5 1.3 collective-permute-start.20
  23.8 5.9 %fold_gain.1.refs_1_.refs_4_.refs_2_.w_ref = bf16[2048,1536]{1,0:T(8,128)(2,1)S(1)} custom-call(f32[1,2048]{1,0:T(1,128)S(1)} %bitcast.22, bf16[2048,1536]{1,0:T(8,128)(2,1)} %w_ref.1), custom_call_target="tpu_custom_call" | custom-call | tf_op jit(solution)/shard_map/fold_gain/pallas_call | solution.py:33
  29.7 0.0 copy-start
  29.7 0.3 collective-permute-start.3
  30.0 0.0 collective-permute-done.19.refs_1_
  30.0 0.1 collective-permute-start.21
  30.1 11.2 %collective-permute-done.2.refs_0_ = bf16[1,128,2048]{2,1,0:T(8,128)(2,1)S(1)} collective-permute-done((bf16[1,128,2048]{2,1,0:T(8,128)(2,1)}, bf16[1,128,2048]{2,1,0:T(8,128)(2,1)S(1)}, u32[]{:S(2)}, u32[]{:S(2)}) %collective-permute-start.2) | collective-permute-done | bytes 524320 | tf_op jit(solution)/shard_map/ppermute | solution.py:519
  41.3 1.2 collective-permute-start.22
  42.5 0.0 collective-permute-done.5.refs_3_
  42.5 0.2 collective-permute-start.4
  42.7 0.4 collective-permute-done.20.refs_2_
  43.1 1.6 %collective-permute-start.6 = (bf16[1,64,2048]{2,1,0:T(8,128)(2,1)S(1)}, bf16[1,64,2048]{2,1,0:T(8,128)(2,1)S(1)}, u32[]{:S(2)}, u32[]{:S(2)}) collective-permute-start(bf16[1,64,2048]{2,1,0:T(8,128)(2,1)S(1)} %get-tuple-element.112), channel_id=1, source_target_pairs={{0,1},{1,2},{2,3},{3,0},{4,5},{5,6},{6,7},{7,4},{8,9},{9,10},{10,1... | collective-permute-start | bytes 786440 | tf_op jit(solution)/shard_map/ppermute | solution.py:532
  44.7 19.1 %collective-permute-done.21.refs_0_ = bf16[1,128,2048]{2,1,0:T(8,128)(2,1)S(1)} collective-permute-done((bf16[1,128,2048]{2,1,0:T(8,128)(2,1)S(1)}, bf16[1,128,2048]{2,1,0:T(8,128)(2,1)S(1)}, u32[]{:S(2)}, u32[]{:S(2)}) %collective-permute-start.21) | collective-permute-done | bytes 524320 | tf_op jit(solution)/shard_map/ppermute | solution.py:525
  63.7 1.2 collective-permute-start.7
  64.9 0.0 collective-permute-done.22.refs_1_
  64.9 0.3 collective-permute-start.8
  65.2 2.4 %collective-permute-start.9 = (bf16[1,64,2048]{2,1,0:T(8,128)(2,1)S(1)}, bf16[1,64,2048]{2,1,0:T(8,128)(2,1)S(1)}, u32[]{:S(2)}, u32[]{:S(2)}) collective-permute-start(bf16[1,64,2048]{2,1,0:T(8,128)(2,1)S(1)} %get-tuple-element.109), channel_id=1, source_target_pairs={{0,3},{1,0},{2,1},{3,2},{4,7},{5,4},{6,5},{7,6},{8,11},{9,8},{10,9... | collective-permute-start | bytes 786440 | tf_op jit(solution)/shard_map/ppermute | solution.py:533
  67.6 0.5 convolution_bitcast_fusion.refs_2_.refs_5_.refs_3_
  68.1 3.8 %shard_map.73 = (bf16[1,512,256]{2,1,0:T(8,128)(2,1)S(1)}, f32[1,512,256]{2,1,0:T(8,128)S(1)}, f32[1,4,128,128]{3,2,1,0:T(8,128)S(1)}, f32[1,4,24,256]{3,2,1,0:T(8,128)S(1)}) custom-call(bf16[2,256,2048]{2,1,0:T(8,128)(2,1)S(1)} %copy-done, bf16[2048,1536]{1,0:T(8,128)(2,1)S(1)} %fold_gain.1.refs_1_.refs_4_.refs_2_.w_ref, ...), custom_call_target="tpu_custom_call" | custom-call | tf_op jit(solution)/shard_map/pallas_call | solution.py:219
  71.9 6.3 %shard_map.74 = (bf16[2,512,256]{2,1,0:T(8,128)(2,1)S(1)}, f32[2,512,256]{2,1,0:T(8,128)S(1)}, f32[2,4,128,128]{3,2,1,0:T(8,128)S(1)}, f32[2,4,24,256]{3,2,1,0:T(8,128)S(1)}) custom-call(bf16[1,128,2048]{2,1,0:T(8,128)(2,1)S(1)} %collective-permute-done.refs_0_, bf16[1,128,2048]{2,1,0:T(8,128)(2,1)S(1)} %collective-permute-done.19.refs_1_, ...), custom_call_target="tpu_custom_call" | custom-call | tf_op jit(solution)/shard_map/pallas_call | solution.py:219
  78.3 3.8 %shard_map.75 = (bf16[1,512,256]{2,1,0:T(8,128)(2,1)S(1)}, f32[1,512,256]{2,1,0:T(8,128)S(1)}, f32[1,4,128,128]{3,2,1,0:T(8,128)S(1)}, f32[1,4,24,256]{3,2,1,0:T(8,128)S(1)}) custom-call(bf16[1,128,2048]{2,1,0:T(8,128)(2,1)S(1)} %collective-permute-done.21.refs_0_, bf16[1,128,2048]{2,1,0:T(8,128)(2,1)S(1)} %collective-permute-done.22.refs_1_, ...), custom_call_target="tpu_custom_call" | custom-call | tf_op jit(solution)/shard_map/pallas_call | solution.py:219
  82.0 0.1 shard_map.76
  82.1 3.8 %collective-permute-start.23 = (bf16[4,128,128]{2,1,0:T(8,128)(2,1)S(1)}, bf16[4,128,128]{2,1,0:T(8,128)(2,1)S(1)}, u32[]{:S(2)}, u32[]{:S(2)}) collective-permute-start(bf16[4,128,128]{2,1,0:T(8,128)(2,1)S(1)} %get-tuple-element.98), channel_id=1, source_target_pairs={{0,4},{4,0},{8,12},{12,8},{16,20},{20,16},{24,28},{28,24},{32,36},... | collective-permute-start | bytes 393224 | tf_op jit(solution)/shard_map/ppermute | solution.py:486
  85.9 3.8 %shard_map.64 = (bf16[1,512,256]{2,1,0:T(8,128)(2,1)S(1)}, f32[1,512,256]{2,1,0:T(8,128)S(1)}, f32[1,4,128,128]{3,2,1,0:T(8,128)S(1)}, f32[1,4,24,256]{3,2,1,0:T(8,128)S(1)}) custom-call(bf16[2,256,2048]{2,1,0:T(8,128)(2,1)S(1)} %copy-done, bf16[2048,1536]{1,0:T(8,128)(2,1)S(1)} %fold_gain.1.refs_1_.refs_4_.refs_2_.w_ref, ...), custom_call_target="tpu_custom_call" | custom-call | tf_op jit(solution)/shard_map/pallas_call | solution.py:219
  89.7 6.3 %shard_map.65 = (bf16[2,512,256]{2,1,0:T(8,128)(2,1)S(1)}, f32[2,512,256]{2,1,0:T(8,128)S(1)}, f32[2,4,128,128]{3,2,1,0:T(8,128)S(1)}, f32[2,4,24,256]{3,2,1,0:T(8,128)S(1)}) custom-call(bf16[1,128,2048]{2,1,0:T(8,128)(2,1)S(1)} %collective-permute-done.2.refs_0_, bf16[1,128,2048]{2,1,0:T(8,128)(2,1)S(1)} %collective-permute-done.3.refs_1_, ...), custom_call_target="tpu_custom_call" | custom-call | tf_op jit(solution)/shard_map/pallas_call | solution.py:219
  96.1 1.0 shard_map.66
  97.1 1.0 shard_map.67
  98.2 0.1 shard_map.69
  98.2 0.1 collective-permute-start.10
  98.4 1.3 collective-permute-start.24
  99.7 2.5 %collective-permute-start.25 = (bf16[2,128,128]{2,1,0:T(8,128)(2,1)S(1)}, bf16[2,128,128]{2,1,0:T(8,128)(2,1)S(1)}, u32[]{:S(2)}, u32[]{:S(2)}) collective-permute-start(bf16[2,128,128]{2,1,0:T(8,128)(2,1)S(1)} %get-tuple-element.101), channel_id=1, source_target_pairs={{0,16},{4,20},{8,24},{12,28},{16,0},{20,4},{24,8},{28,12},{32,48},... | collective-permute-start | bytes 196616 | tf_op jit(solution)/shard_map/ppermute | solution.py:486
  102.1 0.2 collective-permute-start.26
  102.3 0.1 collective-permute-start.11
  102.4 3.6 %collective-permute-start.12 = (bf16[2,128,128]{2,1,0:T(8,128)(2,1)S(1)}, bf16[2,128,128]{2,1,0:T(8,128)(2,1)S(1)}, u32[]{:S(2)}, u32[]{:S(2)}) collective-permute-start(bf16[2,128,128]{2,1,0:T(8,128)(2,1)S(1)} %get-tuple-element.80), channel_id=1, source_target_pairs={{0,16},{4,20},{8,24},{12,28},{16,0},{20,4},{24,8},{28,12},{32,48},... | collective-permute-start | bytes 196616 | tf_op jit(solution)/shard_map/ppermute | solution.py:486
  106.1 0.2 collective-permute-start.13
  106.3 0.3 collective-permute-done.26.three_ref
  106.6 0.1 shard_map.78
  106.6 1.4 %collective-permute-start.28 = (bf16[2,128,128]{2,1,0:T(8,128)(2,1)S(1)}, bf16[2,128,128]{2,1,0:T(8,128)(2,1)S(1)}, u32[]{:S(2)}, u32[]{:S(2)}) collective-permute-start(bf16[2,128,128]{2,1,0:T(8,128)(2,1)S(1)} %get-tuple-element.104), channel_id=1, source_target_pairs={{0,32},{4,36},{8,40},{12,44},{16,48},{20,52},{24,56},{28,60},{32,0... | collective-permute-start | bytes 196616 | tf_op jit(solution)/shard_map/ppermute | solution.py:486
  108.0 2.6 %collective-permute-start.29 = (bf16[2,128,128]{2,1,0:T(8,128)(2,1)S(1)}, bf16[2,128,128]{2,1,0:T(8,128)(2,1)S(1)}, u32[]{:S(2)}, u32[]{:S(2)}) collective-permute-start(bf16[2,128,128]{2,1,0:T(8,128)(2,1)S(1)} %get-tuple-element.104), channel_id=1, source_target_pairs={{0,64},{4,68},{8,72},{12,76},{16,80},{20,84},{24,88},{28,92},{32,9... | collective-permute-start | bytes 196616 | tf_op jit(solution)/shard_map/ppermute | solution.py:486
  110.6 0.2 collective-permute-done.13.three_ref
  110.9 0.1 shard_map.71
  111.0 1.4 %collective-permute-start.15 = (bf16[2,128,128]{2,1,0:T(8,128)(2,1)S(1)}, bf16[2,128,128]{2,1,0:T(8,128)(2,1)S(1)}, u32[]{:S(2)}, u32[]{:S(2)}) collective-permute-start(bf16[2,128,128]{2,1,0:T(8,128)(2,1)S(1)} %get-tuple-element.83), channel_id=1, source_target_pairs={{0,32},{4,36},{8,40},{12,44},{16,48},{20,52},{24,56},{28,60},{32,0... | collective-permute-start | bytes 196616 | tf_op jit(solution)/shard_map/ppermute | solution.py:486
  112.3 2.6 %collective-permute-start.16 = (bf16[2,128,128]{2,1,0:T(8,128)(2,1)S(1)}, bf16[2,128,128]{2,1,0:T(8,128)(2,1)S(1)}, u32[]{:S(2)}, u32[]{:S(2)}) collective-permute-start(bf16[2,128,128]{2,1,0:T(8,128)(2,1)S(1)} %get-tuple-element.83), channel_id=1, source_target_pairs={{0,64},{4,68},{8,72},{12,76},{16,80},{20,84},{24,88},{28,92},{32,9... | collective-permute-start | bytes 196616 | tf_op jit(solution)/shard_map/ppermute | solution.py:486
  115.0 4.0 %collective-permute-start.27 = (bf16[2,2,128,128]{3,2,1,0:T(8,128)(2,1)S(1)}, bf16[2,2,128,128]{3,2,1,0:T(8,128)(2,1)S(1)}, u32[]{:S(2)}, u32[]{:S(2)}) collective-permute-start(bf16[2,2,128,128]{3,2,1,0:T(8,128)(2,1)S(1)} %get-tuple-element.102.refs_17_), channel_id=1, source_target_pairs={{0,4},{4,0},{8,12},{12,8},{16,20},{20,16},{24,28},{28,24},{32,36},... | collective-permute-start | bytes 393224 | tf_op jit(solution)/shard_map/ppermute | solution.py:486
  119.1 0.6 collective-permute-start.31
  119.7 0.1 collective-permute-start.14
  119.8 4.8 %collective-permute-start.18 = (bf16[2,2,128,128]{3,2,1,0:T(8,128)(2,1)S(1)}, bf16[2,2,128,128]{3,2,1,0:T(8,128)(2,1)S(1)}, u32[]{:S(2)}, u32[]{:S(2)}) collective-permute-start(bf16[2,2,128,128]{3,2,1,0:T(8,128)(2,1)S(1)} %shard_map.72.refs_9_), channel_id=1, source_target_pairs={{0,4},{4,0},{8,12},{12,8},{16,20},{20,16},{24,28},{28,24},{32,36},... | collective-permute-start | bytes 393224 | tf_op jit(solution)/shard_map/ppermute | solution.py:486
  124.7 2.1 %shard_map.68 = (bf16[1,512,256]{2,1,0:T(8,128)(2,1)S(1)}, f32[1,512,256]{2,1,0:T(8,128)S(1)}, f32[1,4,24,256]{3,2,1,0:T(8,128)S(1)}) custom-call(bf16[128,2048]{1,0:T(8,128)(2,1)S(1)} %get-tuple-element.58.held_a, bf16[128,2048]{1,0:T(8,128)(2,1)S(1)} %get-tuple-element.60.held_b, bf16[2048,1536]{1,0:T(8,128)(2,1)S(1)} %fold_gain.1.refs_1_.refs_4_.refs_2_.w_ref, ...), custom_call_target="tpu_custom_call" | custom-call | tf_op jit(solution)/shard_map/pallas_call | solution.py:219
  126.8 0.0 copy-start.1
  126.8 1.7 %far_part.3.refs_8_ = f32[4,512,256]{2,1,0:T(8,128)S(1)} custom-call(bf16[1,512,256]{2,1,0:T(8,128)(2,1)S(1)} %get-tuple-element.84.refs_0_, bf16[2,512,256]{2,1,0:T(8,128)(2,1)S(1)} %get-tuple-element.87.refs_1_.refs_2_, bf16[2,512,256]{2,1,0:T(8,128)(2,1)S(1)} %get-tuple-element.87.refs_1_.refs_2_, bf16[1,512,256]{2,1,0:T(8,128)(2,1)S(1)} %get-tuple-element.88.refs_3_, ...), custom_call_target="tpu_custom_call" | custom-call | tf_op jit(solution)/shard_map/far_part/pallas_call | solution.py:400
  128.6 1.0 far_mine.3.refs_10_
  129.6 1.9 %far_last.2.refs_11_ = bf16[2,4,256,512]{3,2,1,0:T(8,128)(2,1)} custom-call(s32[2]{0:T(128)S(1)} %copy-done.1, bf16[1,512,256]{2,1,0:T(8,128)(2,1)S(1)} %get-tuple-element.84.refs_0_, bf16[2,512,256]{2,1,0:T(8,128)(2,1)S(1)} %get-tuple-element.87.refs_1_.refs_2_, bf16[2,512,256]{2,1,0:T(8,128)(2,1)S(1)} %get-tuple-element.87.refs_1_.refs_2_, ...), custom_call_target="tpu_custom_call" | custom-call | tf_op jit(solution)/shard_map/far_last/pallas_call | solution.py:428
  131.5 1.7 %far_part.2.refs_8_ = f32[4,512,256]{2,1,0:T(8,128)S(1)} custom-call(bf16[1,512,256]{2,1,0:T(8,128)(2,1)S(1)} %get-tuple-element.55.refs_0_, bf16[2,512,256]{2,1,0:T(8,128)(2,1)S(1)} %get-tuple-element.57.refs_1_.refs_2_, bf16[2,512,256]{2,1,0:T(8,128)(2,1)S(1)} %get-tuple-element.57.refs_1_.refs_2_, bf16[1,512,256]{2,1,0:T(8,128)(2,1)S(1)} %get-tuple-element.67.refs_3_, ...), custom_call_target="tpu_custom_call" | custom-call | tf_op jit(solution)/shard_map/far_part/pallas_call | solution.py:400
  133.2 1.0 far_mine.2.refs_10_
  134.3 1.9 %far_last.3 = bf16[2,4,256,512]{3,2,1,0:T(8,128)(2,1)} custom-call(s32[2]{0:T(128)S(1)} %copy-done.1, bf16[1,512,256]{2,1,0:T(8,128)(2,1)S(1)} %get-tuple-element.55.refs_0_, bf16[2,512,256]{2,1,0:T(8,128)(2,1)S(1)} %get-tuple-element.57.refs_1_.refs_2_, bf16[2,512,256]{2,1,0:T(8,128)(2,1)S(1)} %get-tuple-element.57.refs_1_.refs_2_, ...), custom_call_target="tpu_custom_call", output_to_operand_aliasing={{}: (12, {})} | custom-call | tf_op jit(solution)/shard_map/far_last/pallas_call | solution.py:428
  (42 shorter events, 0.3 us)
Async XLA Ops:
  0.0 18.8 %slice-start = ((bf16[2,256,2048]{2,1,0:T(8,128)(2,1)}), bf16[1,256,2048]{2,1,0:T(8,128)(2,1)S(1)}, s32[]{:S(2)}) async-start(bf16[2,256,2048]{2,1,0:T(8,128)(2,1)} %refs_0_.3), calls=%async_computation | async-start | bytes 2097152 | tf_op jit(solution)/shard_map/slice | solution.py:515
  2.4 16.4 %collective-permute-start = (bf16[1,128,2048]{2,1,0:T(8,128)(2,1)}, bf16[1,128,2048]{2,1,0:T(8,128)(2,1)S(1)}, u32[]{:S(2)}, u32[]{:S(2)}) collective-permute-start(bf16[1,128,2048]{2,1,0:T(8,128)(2,1)} %get-tuple-element.106), channel_id=1, source_target_pairs={{0,1},{1,2},{2,3},{3,0},{4,5},{5,6},{6,7},{7,4},{8,9},{9,10},{10,1... | collective-permute-start | bytes 1572872 | tf_op jit(solution)/shard_map/ppermute | solution.py:519
  4.8 19.0 %copy-start.3 = (f32[16,4,18]{2,1,0:T(4,128)S(1)}, f32[16,4,18]{2,1,0:T(4,128)}, u32[]{:S(2)}) copy-start(f32[16,4,18]{2,1,0:T(4,128)} %param.9) | copy-start | bytes 13828
  4.8 19.0 %copy-start.4 = (s32[2,1024]{1,0:T(2,128)S(1)}, s32[2,1024]{1,0:T(2,128)}, u32[]{:S(2)}) copy-start(s32[2,1024]{1,0:T(2,128)} %param.10) | copy-start | bytes 24580
  4.8 19.0 %copy-start.2 = (f32[2048]{0:T(1024)S(1)}, f32[2048]{0:T(1024)}, u32[]{:S(2)}) copy-start(f32[2048]{0:T(1024)} %param.7) | copy-start | bytes 24580
  4.8 14.0 %collective-permute-start.1 = (bf16[1,128,2048]{2,1,0:T(8,128)(2,1)}, bf16[1,128,2048]{2,1,0:T(8,128)(2,1)S(1)}, u32[]{:S(2)}, u32[]{:S(2)}) collective-permute-start(bf16[1,128,2048]{2,1,0:T(8,128)(2,1)} %get-tuple-element.105), channel_id=1, source_target_pairs={{0,3},{1,0},{2,1},{3,2},{4,7},{5,4},{6,5},{7,6},{8,11},{9,8},{10,9... | collective-permute-start | bytes 1572872 | tf_op jit(solution)/shard_map/ppermute | solution.py:520
  7.0 23.0 %collective-permute-start.19 = (bf16[1,128,2048]{2,1,0:T(8,128)(2,1)}, bf16[1,128,2048]{2,1,0:T(8,128)(2,1)S(1)}, u32[]{:S(2)}, u32[]{:S(2)}) collective-permute-start(bf16[1,128,2048]{2,1,0:T(8,128)(2,1)} %get-tuple-element.105), channel_id=1, source_target_pairs={{0,1},{1,2},{2,3},{3,0},{4,5},{5,6},{6,7},{7,4},{8,9},{9,10},{10,1... | collective-permute-start | bytes 1572872 | tf_op jit(solution)/shard_map/ppermute | solution.py:521
  19.8 21.4 %collective-permute-start.2 = (bf16[1,128,2048]{2,1,0:T(8,128)(2,1)}, bf16[1,128,2048]{2,1,0:T(8,128)(2,1)S(1)}, u32[]{:S(2)}, u32[]{:S(2)}) collective-permute-start(bf16[1,128,2048]{2,1,0:T(8,128)(2,1)} %bitcast.7), channel_id=1, source_target_pairs={{0,1},{1,2},{2,3},{3,0},{4,5},{5,6},{6,7},{7,4},{8,9},{9,10},{10,1... | collective-permute-start | bytes 1572872 | tf_op jit(solution)/shard_map/ppermute | solution.py:519
  20.3 22.2 %collective-permute-start.5 = (bf16[1,128,2048]{2,1,0:T(8,128)(2,1)}, bf16[1,128,2048]{2,1,0:T(8,128)(2,1)S(1)}, u32[]{:S(2)}, u32[]{:S(2)}) collective-permute-start(bf16[1,128,2048]{2,1,0:T(8,128)(2,1)} %bitcast.8), channel_id=1, source_target_pairs={{0,3},{1,0},{2,1},{3,2},{4,7},{5,4},{6,5},{7,6},{8,11},{9,8},{10,9... | collective-permute-start | bytes 1572872 | tf_op jit(solution)/shard_map/ppermute | solution.py:520
  22.5 20.6 %collective-permute-start.20 = (bf16[1,128,2048]{2,1,0:T(8,128)(2,1)}, bf16[1,128,2048]{2,1,0:T(8,128)(2,1)S(1)}, u32[]{:S(2)}, u32[]{:S(2)}) collective-permute-start(bf16[1,128,2048]{2,1,0:T(8,128)(2,1)} %get-tuple-element.106), channel_id=1, source_target_pairs={{0,3},{1,0},{2,1},{3,2},{4,7},{5,4},{6,5},{7,6},{8,11},{9,8},{10,9... | collective-permute-start | bytes 1572872 | tf_op jit(solution)/shard_map/ppermute | solution.py:522
  29.7 38.4 %copy-start = (bf16[2,256,2048]{2,1,0:T(8,128)(2,1)S(1)}, bf16[2,256,2048]{2,1,0:T(8,128)(2,1)}, u32[]{:S(2)}) copy-start(bf16[2,256,2048]{2,1,0:T(8,128)(2,1)} %refs_0_.3) | copy-start | bytes 6291460
  29.7 35.5 %collective-permute-start.3 = (bf16[1,128,2048]{2,1,0:T(8,128)(2,1)}, bf16[1,128,2048]{2,1,0:T(8,128)(2,1)S(1)}, u32[]{:S(2)}, u32[]{:S(2)}) collective-permute-start(bf16[1,128,2048]{2,1,0:T(8,128)(2,1)} %bitcast.8), channel_id=1, source_target_pairs={{0,1},{1,2},{2,3},{3,0},{4,5},{5,6},{6,7},{7,4},{8,9},{9,10},{10,1... | collective-permute-start | bytes 1572872 | tf_op jit(solution)/shard_map/ppermute | solution.py:521
  30.0 33.7 %collective-permute-start.21 = (bf16[1,128,2048]{2,1,0:T(8,128)(2,1)S(1)}, bf16[1,128,2048]{2,1,0:T(8,128)(2,1)S(1)}, u32[]{:S(2)}, u32[]{:S(2)}) collective-permute-start(bf16[1,128,2048]{2,1,0:T(8,128)(2,1)S(1)} %collective-permute-done.refs_0_), channel_id=1, source_target_pairs={{0,1},{1,2},{2,3},{3,0},{4,5},{5,6},{6,7},{7,4},{8,9},{9,10},{10,1... | collective-permute-start | bytes 1572872 | tf_op jit(solution)/shard_map/ppermute | solution.py:525
  41.3 23.7 %collective-permute-start.22 = (bf16[1,128,2048]{2,1,0:T(8,128)(2,1)S(1)}, bf16[1,128,2048]{2,1,0:T(8,128)(2,1)S(1)}, u32[]{:S(2)}, u32[]{:S(2)}) collective-permute-start(bf16[1,128,2048]{2,1,0:T(8,128)(2,1)S(1)} %collective-permute-done.1.refs_3_), channel_id=1, source_target_pairs={{0,3},{1,0},{2,1},{3,2},{4,7},{5,4},{6,5},{7,6},{8,11},{9,8},{10,9... | collective-permute-start | bytes 1572872 | tf_op jit(solution)/shard_map/ppermute | solution.py:525
  42.5 39.6 %collective-permute-start.4 = (bf16[1,128,2048]{2,1,0:T(8,128)(2,1)}, bf16[1,128,2048]{2,1,0:T(8,128)(2,1)S(1)}, u32[]{:S(2)}, u32[]{:S(2)}) collective-permute-start(bf16[1,128,2048]{2,1,0:T(8,128)(2,1)} %bitcast.7), channel_id=1, source_target_pairs={{0,3},{1,0},{2,1},{3,2},{4,7},{5,4},{6,5},{7,6},{8,11},{9,8},{10,9... | collective-permute-start | bytes 1572872 | tf_op jit(solution)/shard_map/ppermute | solution.py:522
  43.1 52.9 %collective-permute-start.6 = (bf16[1,64,2048]{2,1,0:T(8,128)(2,1)S(1)}, bf16[1,64,2048]{2,1,0:T(8,128)(2,1)S(1)}, u32[]{:S(2)}, u32[]{:S(2)}) collective-permute-start(bf16[1,64,2048]{2,1,0:T(8,128)(2,1)S(1)} %get-tuple-element.112), channel_id=1, source_target_pairs={{0,1},{1,2},{2,3},{3,0},{4,5},{5,6},{6,7},{7,4},{8,9},{9,10},{10,1... | collective-permute-start | bytes 786440 | tf_op jit(solution)/shard_map/ppermute | solution.py:532
  63.7 32.3 %collective-permute-start.7 = (bf16[1,64,2048]{2,1,0:T(8,128)(2,1)S(1)}, bf16[1,64,2048]{2,1,0:T(8,128)(2,1)S(1)}, u32[]{:S(2)}, u32[]{:S(2)}) collective-permute-start(bf16[1,64,2048]{2,1,0:T(8,128)(2,1)S(1)} %get-tuple-element.110), channel_id=1, source_target_pairs={{0,3},{1,0},{2,1},{3,2},{4,7},{5,4},{6,5},{7,6},{8,11},{9,8},{10,9... | collective-permute-start | bytes 786440 | tf_op jit(solution)/shard_map/ppermute | solution.py:533
  64.9 32.2 %collective-permute-start.8 = (bf16[1,64,2048]{2,1,0:T(8,128)(2,1)S(1)}, bf16[1,64,2048]{2,1,0:T(8,128)(2,1)S(1)}, u32[]{:S(2)}, u32[]{:S(2)}) collective-permute-start(bf16[1,64,2048]{2,1,0:T(8,128)(2,1)S(1)} %get-tuple-element.111), channel_id=1, source_target_pairs={{0,1},{1,2},{2,3},{3,0},{4,5},{5,6},{6,7},{7,4},{8,9},{9,10},{10,1... | collective-permute-start | bytes 786440 | tf_op jit(solution)/shard_map/ppermute | solution.py:532
  65.2 31.9 %collective-permute-start.9 = (bf16[1,64,2048]{2,1,0:T(8,128)(2,1)S(1)}, bf16[1,64,2048]{2,1,0:T(8,128)(2,1)S(1)}, u32[]{:S(2)}, u32[]{:S(2)}) collective-permute-start(bf16[1,64,2048]{2,1,0:T(8,128)(2,1)S(1)} %get-tuple-element.109), channel_id=1, source_target_pairs={{0,3},{1,0},{2,1},{3,2},{4,7},{5,4},{6,5},{7,6},{8,11},{9,8},{10,9... | collective-permute-start | bytes 786440 | tf_op jit(solution)/shard_map/ppermute | solution.py:533
  82.1 16.2 %collective-permute-start.23 = (bf16[4,128,128]{2,1,0:T(8,128)(2,1)S(1)}, bf16[4,128,128]{2,1,0:T(8,128)(2,1)S(1)}, u32[]{:S(2)}, u32[]{:S(2)}) collective-permute-start(bf16[4,128,128]{2,1,0:T(8,128)(2,1)S(1)} %get-tuple-element.98), channel_id=1, source_target_pairs={{0,4},{4,0},{8,12},{12,8},{16,20},{20,16},{24,28},{28,24},{32,36},... | collective-permute-start | bytes 393224 | tf_op jit(solution)/shard_map/ppermute | solution.py:486
  98.2 4.1 %collective-permute-start.10 = (bf16[4,128,128]{2,1,0:T(8,128)(2,1)S(1)}, bf16[4,128,128]{2,1,0:T(8,128)(2,1)S(1)}, u32[]{:S(2)}, u32[]{:S(2)}) collective-permute-start(bf16[4,128,128]{2,1,0:T(8,128)(2,1)S(1)} %get-tuple-element.77), channel_id=1, source_target_pairs={{0,4},{4,0},{8,12},{12,8},{16,20},{20,16},{24,28},{28,24},{32,36},... | collective-permute-start | bytes 393224 | tf_op jit(solution)/shard_map/ppermute | solution.py:486
  98.4 7.7 %collective-permute-start.24 = (bf16[2,128,128]{2,1,0:T(8,128)(2,1)S(1)}, bf16[2,128,128]{2,1,0:T(8,128)(2,1)S(1)}, u32[]{:S(2)}, u32[]{:S(2)}) collective-permute-start(bf16[2,128,128]{2,1,0:T(8,128)(2,1)S(1)} %get-tuple-element.101), channel_id=1, source_target_pairs={{0,8},{4,12},{8,0},{12,4},{16,24},{20,28},{24,16},{28,20},{32,40},... | collective-permute-start | bytes 196616 | tf_op jit(solution)/shard_map/ppermute | solution.py:486
  99.7 6.6 %collective-permute-start.25 = (bf16[2,128,128]{2,1,0:T(8,128)(2,1)S(1)}, bf16[2,128,128]{2,1,0:T(8,128)(2,1)S(1)}, u32[]{:S(2)}, u32[]{:S(2)}) collective-permute-start(bf16[2,128,128]{2,1,0:T(8,128)(2,1)S(1)} %get-tuple-element.101), channel_id=1, source_target_pairs={{0,16},{4,20},{8,24},{12,28},{16,0},{20,4},{24,8},{28,12},{32,48},... | collective-permute-start | bytes 196616 | tf_op jit(solution)/shard_map/ppermute | solution.py:486
  102.1 4.5 %collective-permute-start.26 = (bf16[2,128,128]{2,1,0:T(8,128)(2,1)S(1)}, bf16[2,128,128]{2,1,0:T(8,128)(2,1)S(1)}, u32[]{:S(2)}, u32[]{:S(2)}) collective-permute-start(bf16[2,128,128]{2,1,0:T(8,128)(2,1)S(1)} %get-tuple-element.101), channel_id=1, source_target_pairs={{0,24},{4,28},{8,16},{12,20},{16,8},{20,12},{24,0},{28,4},{32,56},... | collective-permute-start | bytes 196616 | tf_op jit(solution)/shard_map/ppermute | solution.py:486
  102.3 8.3 %collective-permute-start.11 = (bf16[2,128,128]{2,1,0:T(8,128)(2,1)S(1)}, bf16[2,128,128]{2,1,0:T(8,128)(2,1)S(1)}, u32[]{:S(2)}, u32[]{:S(2)}) collective-permute-start(bf16[2,128,128]{2,1,0:T(8,128)(2,1)S(1)} %get-tuple-element.80), channel_id=1, source_target_pairs={{0,8},{4,12},{8,0},{12,4},{16,24},{20,28},{24,16},{28,20},{32,40},... | collective-permute-start | bytes 196616 | tf_op jit(solution)/shard_map/ppermute | solution.py:486
  102.4 8.2 %collective-permute-start.12 = (bf16[2,128,128]{2,1,0:T(8,128)(2,1)S(1)}, bf16[2,128,128]{2,1,0:T(8,128)(2,1)S(1)}, u32[]{:S(2)}, u32[]{:S(2)}) collective-permute-start(bf16[2,128,128]{2,1,0:T(8,128)(2,1)S(1)} %get-tuple-element.80), channel_id=1, source_target_pairs={{0,16},{4,20},{8,24},{12,28},{16,0},{20,4},{24,8},{28,12},{32,48},... | collective-permute-start | bytes 196616 | tf_op jit(solution)/shard_map/ppermute | solution.py:486
  106.1 4.8 %collective-permute-start.13 = (bf16[2,128,128]{2,1,0:T(8,128)(2,1)S(1)}, bf16[2,128,128]{2,1,0:T(8,128)(2,1)S(1)}, u32[]{:S(2)}, u32[]{:S(2)}) collective-permute-start(bf16[2,128,128]{2,1,0:T(8,128)(2,1)S(1)} %get-tuple-element.80), channel_id=1, source_target_pairs={{0,24},{4,28},{8,16},{12,20},{16,8},{20,12},{24,0},{28,4},{32,56},... | collective-permute-start | bytes 196616 | tf_op jit(solution)/shard_map/ppermute | solution.py:486
  106.6 8.3 %collective-permute-start.28 = (bf16[2,128,128]{2,1,0:T(8,128)(2,1)S(1)}, bf16[2,128,128]{2,1,0:T(8,128)(2,1)S(1)}, u32[]{:S(2)}, u32[]{:S(2)}) collective-permute-start(bf16[2,128,128]{2,1,0:T(8,128)(2,1)S(1)} %get-tuple-element.104), channel_id=1, source_target_pairs={{0,32},{4,36},{8,40},{12,44},{16,48},{20,52},{24,56},{28,60},{32,0... | collective-permute-start | bytes 196616 | tf_op jit(solution)/shard_map/ppermute | solution.py:486
  108.0 7.0 %collective-permute-start.29 = (bf16[2,128,128]{2,1,0:T(8,128)(2,1)S(1)}, bf16[2,128,128]{2,1,0:T(8,128)(2,1)S(1)}, u32[]{:S(2)}, u32[]{:S(2)}) collective-permute-start(bf16[2,128,128]{2,1,0:T(8,128)(2,1)S(1)} %get-tuple-element.104), channel_id=1, source_target_pairs={{0,64},{4,68},{8,72},{12,76},{16,80},{20,84},{24,88},{28,92},{32,9... | collective-permute-start | bytes 196616 | tf_op jit(solution)/shard_map/ppermute | solution.py:486
  110.6 8.4 %collective-permute-start.30 = (bf16[2,128,128]{2,1,0:T(8,128)(2,1)S(1)}, bf16[2,128,128]{2,1,0:T(8,128)(2,1)S(1)}, u32[]{:S(2)}, u32[]{:S(2)}) collective-permute-start(bf16[2,128,128]{2,1,0:T(8,128)(2,1)S(1)} %get-tuple-element.104), channel_id=1, source_target_pairs={{0,96},{4,100},{8,104},{12,108},{16,112},{20,116},{24,120},{28,124... | collective-permute-start | bytes 196616 | tf_op jit(solution)/shard_map/ppermute | solution.py:486
  111.0 8.7 %collective-permute-start.15 = (bf16[2,128,128]{2,1,0:T(8,128)(2,1)S(1)}, bf16[2,128,128]{2,1,0:T(8,128)(2,1)S(1)}, u32[]{:S(2)}, u32[]{:S(2)}) collective-permute-start(bf16[2,128,128]{2,1,0:T(8,128)(2,1)S(1)} %get-tuple-element.83), channel_id=1, source_target_pairs={{0,32},{4,36},{8,40},{12,44},{16,48},{20,52},{24,56},{28,60},{32,0... | collective-permute-start | bytes 196616 | tf_op jit(solution)/shard_map/ppermute | solution.py:486
  112.3 7.4 %collective-permute-start.16 = (bf16[2,128,128]{2,1,0:T(8,128)(2,1)S(1)}, bf16[2,128,128]{2,1,0:T(8,128)(2,1)S(1)}, u32[]{:S(2)}, u32[]{:S(2)}) collective-permute-start(bf16[2,128,128]{2,1,0:T(8,128)(2,1)S(1)} %get-tuple-element.83), channel_id=1, source_target_pairs={{0,64},{4,68},{8,72},{12,76},{16,80},{20,84},{24,88},{28,92},{32,9... | collective-permute-start | bytes 196616 | tf_op jit(solution)/shard_map/ppermute | solution.py:486
  115.0 4.8 %collective-permute-start.17 = (bf16[2,128,128]{2,1,0:T(8,128)(2,1)S(1)}, bf16[2,128,128]{2,1,0:T(8,128)(2,1)S(1)}, u32[]{:S(2)}, u32[]{:S(2)}) collective-permute-start(bf16[2,128,128]{2,1,0:T(8,128)(2,1)S(1)} %get-tuple-element.83), channel_id=1, source_target_pairs={{0,96},{4,100},{8,104},{12,108},{16,112},{20,116},{24,120},{28,124... | collective-permute-start | bytes 196616 | tf_op jit(solution)/shard_map/ppermute | solution.py:486
  115.0 11.8 %collective-permute-start.27 = (bf16[2,2,128,128]{3,2,1,0:T(8,128)(2,1)S(1)}, bf16[2,2,128,128]{3,2,1,0:T(8,128)(2,1)S(1)}, u32[]{:S(2)}, u32[]{:S(2)}) collective-permute-start(bf16[2,2,128,128]{3,2,1,0:T(8,128)(2,1)S(1)} %get-tuple-element.102.refs_17_), channel_id=1, source_target_pairs={{0,4},{4,0},{8,12},{12,8},{16,20},{20,16},{24,28},{28,24},{32,36},... | collective-permute-start | bytes 393224 | tf_op jit(solution)/shard_map/ppermute | solution.py:486
  119.1 10.6 %collective-permute-start.31 = (bf16[2,2,128,128]{3,2,1,0:T(8,128)(2,1)S(1)}, bf16[2,2,128,128]{3,2,1,0:T(8,128)(2,1)S(1)}, u32[]{:S(2)}, u32[]{:S(2)}) collective-permute-start(bf16[2,2,128,128]{3,2,1,0:T(8,128)(2,1)S(1)} %shard_map.79.refs_9_), channel_id=1, source_target_pairs={{0,4},{4,0},{8,12},{12,8},{16,20},{20,16},{24,28},{28,24},{32,36},... | collective-permute-start | bytes 393224 | tf_op jit(solution)/shard_map/ppermute | solution.py:486
  119.7 11.8 %collective-permute-start.14 = (bf16[2,2,128,128]{3,2,1,0:T(8,128)(2,1)S(1)}, bf16[2,2,128,128]{3,2,1,0:T(8,128)(2,1)S(1)}, u32[]{:S(2)}, u32[]{:S(2)}) collective-permute-start(bf16[2,2,128,128]{3,2,1,0:T(8,128)(2,1)S(1)} %get-tuple-element.81.refs_17_), channel_id=1, source_target_pairs={{0,4},{4,0},{8,12},{12,8},{16,20},{20,16},{24,28},{28,24},{32,36},... | collective-permute-start | bytes 393224 | tf_op jit(solution)/shard_map/ppermute | solution.py:486
  119.8 14.4 %collective-permute-start.18 = (bf16[2,2,128,128]{3,2,1,0:T(8,128)(2,1)S(1)}, bf16[2,2,128,128]{3,2,1,0:T(8,128)(2,1)S(1)}, u32[]{:S(2)}, u32[]{:S(2)}) collective-permute-start(bf16[2,2,128,128]{3,2,1,0:T(8,128)(2,1)S(1)} %shard_map.72.refs_9_), channel_id=1, source_target_pairs={{0,4},{4,0},{8,12},{12,8},{16,20},{20,16},{24,28},{28,24},{32,36},... | collective-permute-start | bytes 393224 | tf_op jit(solution)/shard_map/ppermute | solution.py:486
  126.8 1.8 %copy-start.1 = (s32[2]{0:T(128)S(1)}, s32[2]{0:T(128)}, u32[]{:S(2)}) copy-start(s32[2]{0:T(128)} %lengths_ref.7) | copy-start | bytes 28
